TPU v7x, 32 devices: a whole 2x2x4 slice. The times are simulated.
32 devices in a mesh: depth: 4 (over y, x), probe: 8 (over z, core).
Axes of the slice: x: 2, y: 2, z: 4, core: 2. Of those that a mesh axis runs over, the one named last changes fastest.
Arguments:
- probe: float32 [2, 256, 256], replicated, may hold values from -6 to 6
- phase: float32 [8, 2048, 768], P('depth', 'probe'), may hold values from -6 to 6
- row_offsets: int32 [16], P('probe'), may hold values from 0 to 2047, as said below
- col_offsets: int32 [16], P('probe'), may hold values from 0 to 512
Outputs:
- exit_waves: bfloat16 [4, 16, 2, 256, 256], P('depth', 'probe')
Inputs may be any that keep to these rules, and one draw needn't show every extreme that they name: `row_offsets`: offsets 2 * i to 2 * i + 1 lie within i * 256 to (i + 1) * 256 - 1.
All inputs are finite; a program needn't handle non-finite values.
Results may differ from a plain program's by a relative error of at most 0.014.
Values may be sent and summed in bfloat16 or wider, within the bound.
No kernel may reach another device: no remote copies, remote signals or barrier semaphores. Data moves between devices by JAX's collectives and lax.ppermute only.
A program may use at most 64 MiB of HBM per device.

v0:
```python
import math

import jax
import jax.numpy as jnp
from jax import lax
from jax.sharding import PartitionSpec as P

CHIRP = 40.0
HIGH = lax.Precision.HIGHEST


def passed_along(block, axis, distance):
    devices = range(lax.axis_size(axis))
    route = [(i - distance, i) for i in devices if i - distance in devices]
    return lax.ppermute(block, axis, route)


def chirp_parts(size):
    k = jnp.arange(size)
    freq = jnp.where(k < size // 2, k, k - size).astype(jnp.float32) / size
    angle = -CHIRP * freq * freq
    return (jnp.cos(angle), jnp.sin(angle))


def fourier_tables(size):
    k = jnp.arange(size)
    product = k[:, None] * k[None, :] % size
    angle = 2.0 * math.pi / size * product.astype(jnp.float32)
    return (jnp.cos(angle), jnp.sin(angle))


def both_sides(wave, m_real, m_imag):
    first = jnp.einsum("nqab,bc->nqac", wave, m_real, precision=HIGH)
    second = jnp.einsum("nqab,bc->nqac", wave, m_imag, precision=HIGH)
    wave = jnp.stack([first[:, 0] - second[:, 1], second[:, 0] + first[:, 1]], axis=1)
    first = jnp.einsum("ab,nqbc->nqac", m_real, wave, precision=HIGH)
    second = jnp.einsum("ab,nqbc->nqac", m_imag, wave, precision=HIGH)
    return jnp.stack([first[:, 0] - second[:, 1], second[:, 0] + first[:, 1]], axis=1)


def build_operators(size):
    cos_table, sin_table = fourier_tables(size)
    h_real, h_imag = chirp_parts(size)
    grid_real = h_real[:, None] * h_real[None, :] - h_imag[:, None] * h_imag[None, :]
    grid_imag = h_real[:, None] * h_imag[None, :] + h_imag[:, None] * h_real[None, :]
    return (cos_table, sin_table, grid_real, grid_imag)


def propagate(wave, operators):
    size = wave.shape[-1]
    cos_table, sin_table, grid_real, grid_imag = operators
    spectrum = both_sides(wave, cos_table, -sin_table)
    real_part = grid_real * spectrum[:, 0] - grid_imag * spectrum[:, 1]
    imag_part = grid_real * spectrum[:, 1] + grid_imag * spectrum[:, 0]
    spectrum = jnp.stack([real_part, imag_part], axis=1)
    return both_sides(spectrum, cos_table / size, sin_table / size)


def traverse(wave, rows, cols, extended, operators):
    size = wave.shape[-1]
    for inner in range(extended.shape[0]):
        layer = extended[inner]
        windows = jax.vmap(lambda r, c: lax.dynamic_slice(layer, (r, c), (size, size)))(rows, cols)
        trans_real = jnp.cos(windows)
        trans_imag = jnp.sin(windows)
        wave = jnp.stack(
            [
                trans_real * wave[:, 0] - trans_imag * wave[:, 1],
                trans_real * wave[:, 1] + trans_imag * wave[:, 0],
            ],
            axis=1,
        )
        wave = propagate(wave, operators)
    return wave


def body(probe, phase, row_offsets, col_offsets):
    size = probe.shape[-1]
    strip = phase.shape[1]
    count = row_offsets.shape[0]
    groups = lax.axis_size("depth")
    group = lax.axis_index("depth")
    following = passed_along(phase.astype(jnp.bfloat16), "probe", -1).astype(phase.dtype)
    extended = jnp.concatenate([phase, following], axis=1)
    rows = row_offsets - lax.axis_index("probe") * strip
    operators = build_operators(size)
    incident = probe[None]
    empty = jnp.zeros((count, 2, size, size), jnp.bfloat16)
    start_waves = jnp.broadcast_to(incident, (count, 2, size, size))

    def section(step, carry):
        received, result = carry
        active = group == step
        incoming = jnp.where(group == 0, start_waves, received.astype(jnp.float32))
        leaving = lax.cond(
            active,
            lambda v: traverse(v, rows, col_offsets, extended, operators).astype(jnp.bfloat16),
            lambda v: jnp.zeros(v.shape, jnp.bfloat16),
            incoming,
        )
        result = jnp.where(active, leaving, result)
        received = passed_along(leaving, "depth", 1)
        return (received, result)

    received, result = lax.fori_loop(0, groups, section, (empty, empty))
    return result[None]


def solution(mesh):
    return jax.shard_map(
        body,
        mesh=mesh,
        in_specs=(P(), P("depth", "probe", None), P("probe"), P("probe")),
        out_specs=P("depth", "probe", None, None, None),
        check_vma=False,
    )
```

profile of v0, /device:TPU:21, one launch (start us, length us, event | category | flops | bytes accessed | tf_op | source)
XLA Modules:
  0.0 299.4 jit_solution(12826881452727965266)
XLA Ops:
  0.0 2.4 convert_element_type.89
  2.4 2.7 collective-permute-start.1
  5.2 11.0 %collective-permute-done.1 = bf16[2,256,768]{2,1,0:T(8,128)(2,1)S(1)} collective-permute-done((bf16[2,256,768]{2,1,0:T(8,128)(2,1)}, bf16[2,256,768]{2,1,0:T(8,128)(2,1)S(1)}, u32[]{:S(2)}, u32[]{:S(2)}) %collective-permute-start.1) | collective-permute-done | bytes 786464 | tf_op jit(solution)/shard_map/ppermute | solution.py:15
  18.2 279.1 %while.26 = (s32[]{:T(128)}, bf16[2,2,256,256]{2,3,1,0:T(8,128)(2,1)S(1)}, bf16[2,2,256,256]{2,3,1,0:T(8,128)(2,1)}, s32[]{:T(128)}, f32[2,512,768]{2,1,0:T(8,12...) while((s32[]{:T(128)}, ...), condition=%wide.region_3.4_spmd.clone.clone.clone.clone, body=%wide.region_0.3_spmd.clone.clone.clone.clone.sunk | while | flops 12898009088 | bytes 93067000 | solution.py:105
  18.6 3.1 %collective-permute-start = (bf16[2,2,256,256]{2,3,1,0:T(8,128)(2,1)S(1)}, bf16[2,2,256,256]{2,3,1,0:T(8,128)(2,1)S(1)}, u32[]{:S(2)}, u32[]{:S(2)}) collective-permute-start(bf16[2,2,256,256]{2,3,1,0:T(8,128)(2,1)S(1)} %get-tuple-element.939), channel_id=1, source_target_pairs={{0,8},{8,16},{16,24},{1,9},{9,17},{17,25},{2,10},{10,18},{18,26},{... | collective-permute-start | bytes 1572872 | tf_op jit(solution)/shard_map/while/body/eval_jaxpr/ppermute | solution.py:15
  22.5 11.7 %collective-permute-done = bf16[2,2,256,256]{2,3,1,0:T(8,128)(2,1)S(1)} collective-permute-done((bf16[2,2,256,256]{2,3,1,0:T(8,128)(2,1)S(1)}, bf16[2,2,256,256]{2,3,1,0:T(8,128)(2,1)S(1)}, u32[]{:S(2)}, u32[]{:S(2)}) %collective-permute-start) | collective-permute-done | bytes 524320 | tf_op jit(solution)/shard_map/while/body/eval_jaxpr/ppermute | solution.py:15
  34.6 2.2 collective-permute-start
  36.8 1.9 select_select_fusion.2
  38.7 119.2 %collective-permute-done = bf16[2,2,256,256]{2,3,1,0:T(8,128)(2,1)S(1)} collective-permute-done((bf16[2,2,256,256]{2,3,1,0:T(8,128)(2,1)S(1)}, bf16[2,2,256,256]{2,3,1,0:T(8,128)(2,1)S(1)}, u32[]{:S(2)}, u32[]{:S(2)}) %collective-permute-start) | collective-permute-done | bytes 524320 | tf_op jit(solution)/shard_map/while/body/eval_jaxpr/ppermute | solution.py:15
  158.2 55.7 %conditional.6 = (bf16[2,2,256,256]{2,3,1,0:T(8,128)(2,1)S(1)}) conditional(s32[]{:T(128)} %convert_element_type.123, () %tuple.125, (f32[256,256]{0,1:T(8,128)S(1)}, f32[256,256]{0,1:T(8,128)S(1)}, f32[2,512,768]{2,1,0:T(8,128)}, s32[2]{0:T(128)S(1)}, s32[2]{0:T(128)S(1)}, /*index=5*/pred[]{:T(512)}, bf16[2,2,256,256]{2,3,1,0:T(8,128)(2,1)S(1)}, ...), branch_computations={%region_1.1_spmd, %region_2.2_spmd.clone} | conditional | flops 12896567296 | bytes 88345032 | solution.py:95
  158.4 3.3 %slice_bitcast_fusion = (f32[512,768]{1,0:T(8,128)S(1)}, f32[512,768]{1,0:T(8,128)}) fusion(f32[2,512,768]{2,1,0:T(8,128)} %get-tuple-element.644), kind=kLoop, calls=%fused_computation.10 | loop fusion | bytes 6291456 | tf_op jit(solution)/shard_map/while/body/eval_jaxpr/cond/branch_1_fun/squeeze | solution.py:62
  161.7 7.9 %while.24 = (s32[]{:T(128)}, f32[512,768]{1,0:T(8,128)}, s32[2,2]{1,0:T(2,128)S(1)}, f32[2,256,256]{1,2,0:T(8,128)}, s32[]{:T(128)}) while((s32[]{:T(128)}, f32[512,768]{1,0:T(8,128)}, s32[2,2]{1,0:T(2,128)S(1)}, f32[2,256,256]{1,2,0:T(8,128)}, s32[]{:T(128)}) %tuple.131), condition=%wide.while_cond, body=%wide.while_body.sunk | while | flops 2 | bytes 1572981 | solution.py:63
  162.4 2.4 dynamic-slice_bitcast_fusion.2
  166.4 2.4 dynamic-slice_bitcast_fusion.2
  169.7 3.5 %fusion.98 = (f32[2,256,256]{1,2,0:T(8,128)S(1)}, f32[2,256,256]{1,2,0:T(8,128)}) fusion(f32[2,256,256]{1,2,0:T(8,128)} %get-tuple-element.642), kind=kLoop, calls=%fused_computation.159 | loop fusion | bytes 1572864 | tf_op jit(solution)/shard_map/while/body/eval_jaxpr/cond/branch_1_fun/cos | solution.py:64
  173.2 5.6 %while.25 = (s32[]{:T(128)}, f32[512,768]{1,0:T(8,128)S(1)}, s32[2,2]{1,0:T(2,128)S(1)}, f32[2,256,256]{2,1,0:T(8,128)}, s32[]{:T(128)}) while((s32[]{:T(128)}, f32[512,768]{1,0:T(8,128)S(1)}, s32[2,2]{1,0:T(2,128)S(1)}, f32[2,256,256]{2,1,0:T(8,128)}, s32[]{:T(128)}) %tuple.142), condition=%wide.while_cond.1, body=%wide.while_body.1.sunk | while | flops 2 | bytes 525421 | solution.py:63
  173.8 2.2 bitcast_dynamic-update-slice_fusion.2
  176.6 2.2 bitcast_dynamic-update-slice_fusion.2
  178.8 2.8 fusion.97
  190.8 1.8 fusion.14
  192.6 1.8 fusion.15
  198.5 1.8 fusion.12
  200.3 1.9 fusion.13
  206.2 1.8 fusion.10
  208.0 1.8 fusion.11
  213.9 1.9 collective-permute-start
  215.8 1.9 select_select_fusion.2
  217.7 12.0 %collective-permute-done = bf16[2,2,256,256]{2,3,1,0:T(8,128)(2,1)S(1)} collective-permute-done((bf16[2,2,256,256]{2,3,1,0:T(8,128)(2,1)S(1)}, bf16[2,2,256,256]{2,3,1,0:T(8,128)(2,1)S(1)}, u32[]{:S(2)}, u32[]{:S(2)}) %collective-permute-start) | collective-permute-done | bytes 524320 | tf_op jit(solution)/shard_map/while/body/eval_jaxpr/ppermute | solution.py:15
  230.1 56.9 %collective-permute-start = (bf16[2,2,256,256]{2,3,1,0:T(8,128)(2,1)S(1)}, bf16[2,2,256,256]{2,3,1,0:T(8,128)(2,1)S(1)}, u32[]{:S(2)}, u32[]{:S(2)}) collective-permute-start(bf16[2,2,256,256]{2,3,1,0:T(8,128)(2,1)S(1)} %get-tuple-element.939), channel_id=1, source_target_pairs={{0,8},{8,16},{16,24},{1,9},{9,17},{17,25},{2,10},{10,18},{18,26},{... | collective-permute-start | bytes 1572872 | tf_op jit(solution)/shard_map/while/body/eval_jaxpr/ppermute | solution.py:15
  287.0 1.9 select_select_fusion.2
  288.9 8.4 %collective-permute-done = bf16[2,2,256,256]{2,3,1,0:T(8,128)(2,1)S(1)} collective-permute-done((bf16[2,2,256,256]{2,3,1,0:T(8,128)(2,1)S(1)}, bf16[2,2,256,256]{2,3,1,0:T(8,128)(2,1)S(1)}, u32[]{:S(2)}, u32[]{:S(2)}) %collective-permute-start) | collective-permute-done | bytes 524320 | tf_op jit(solution)/shard_map/while/body/eval_jaxpr/ppermute | solution.py:15
  297.3 2.0 copy.24
  (79 shorter events, 29.8 us)
Async XLA Ops:
  0.0 5.2 %copy-start.3 = (s32[2]{0:T(128)S(1)}, s32[2]{0:T(128)}, u32[]{:S(2)}) copy-start(s32[2]{0:T(128)} %param.10) | copy-start | bytes 28
  2.4 13.9 %copy-start.1 = (f32[2,256,768]{2,1,0:T(8,128)S(1)}, f32[2,256,768]{2,1,0:T(8,128)}, u32[]{:S(2)}) copy-start(f32[2,256,768]{2,1,0:T(8,128)} %param.9) | copy-start | bytes 4718596
  2.4 13.8 %collective-permute-start.1 = (bf16[2,256,768]{2,1,0:T(8,128)(2,1)}, bf16[2,256,768]{2,1,0:T(8,128)(2,1)S(1)}, u32[]{:S(2)}, u32[]{:S(2)}) collective-permute-start(bf16[2,256,768]{2,1,0:T(8,128)(2,1)} %convert_element_type.89), channel_id=1, source_target_pairs={{1,0},{2,1},{3,2},{4,3},{5,4},{6,5},{7,6},{9,8},{10,9},{11,10},{12... | collective-permute-start | bytes 2359304 | tf_op jit(solution)/shard_map/ppermute | solution.py:15
  16.3 1.9 copy-start.2
  18.6 15.7 %collective-permute-start = (bf16[2,2,256,256]{2,3,1,0:T(8,128)(2,1)S(1)}, bf16[2,2,256,256]{2,3,1,0:T(8,128)(2,1)S(1)}, u32[]{:S(2)}, u32[]{:S(2)}) collective-permute-start(bf16[2,2,256,256]{2,3,1,0:T(8,128)(2,1)S(1)} %get-tuple-element.939), channel_id=1, source_target_pairs={{0,8},{8,16},{16,24},{1,9},{9,17},{17,25},{2,10},{10,18},{18,26},{... | collective-permute-start | bytes 1572872 | tf_op jit(solution)/shard_map/while/body/eval_jaxpr/ppermute | solution.py:15
  34.6 123.3 %collective-permute-start = (bf16[2,2,256,256]{2,3,1,0:T(8,128)(2,1)S(1)}, bf16[2,2,256,256]{2,3,1,0:T(8,128)(2,1)S(1)}, u32[]{:S(2)}, u32[]{:S(2)}) collective-permute-start(bf16[2,2,256,256]{2,3,1,0:T(8,128)(2,1)S(1)} %get-tuple-element.939), channel_id=1, source_target_pairs={{0,8},{8,16},{16,24},{1,9},{9,17},{17,25},{2,10},{10,18},{18,26},{... | collective-permute-start | bytes 1572872 | tf_op jit(solution)/shard_map/while/body/eval_jaxpr/ppermute | solution.py:15
  196.4 1.8 copy-start
  213.9 15.9 %collective-permute-start = (bf16[2,2,256,256]{2,3,1,0:T(8,128)(2,1)S(1)}, bf16[2,2,256,256]{2,3,1,0:T(8,128)(2,1)S(1)}, u32[]{:S(2)}, u32[]{:S(2)}) collective-permute-start(bf16[2,2,256,256]{2,3,1,0:T(8,128)(2,1)S(1)} %get-tuple-element.939), channel_id=1, source_target_pairs={{0,8},{8,16},{16,24},{1,9},{9,17},{17,25},{2,10},{10,18},{18,26},{... | collective-permute-start | bytes 1572872 | tf_op jit(solution)/shard_map/while/body/eval_jaxpr/ppermute | solution.py:15
  230.1 67.2 %collective-permute-start = (bf16[2,2,256,256]{2,3,1,0:T(8,128)(2,1)S(1)}, bf16[2,2,256,256]{2,3,1,0:T(8,128)(2,1)S(1)}, u32[]{:S(2)}, u32[]{:S(2)}) collective-permute-start(bf16[2,2,256,256]{2,3,1,0:T(8,128)(2,1)S(1)} %get-tuple-element.939), channel_id=1, source_target_pairs={{0,8},{8,16},{16,24},{1,9},{9,17},{17,25},{2,10},{10,18},{18,26},{... | collective-permute-start | bytes 1572872 | tf_op jit(solution)/shard_map/while/body/eval_jaxpr/ppermute | solution.py:15
where the time goes:
time: 302 us; the launch traced here: 299 us
  waiting for transfers between devices  162 us (54%)
  starting transfers between devices  66.9 us (22%)
  local copies, waits for them, and re-layouts  27.8 us (9%)
  matrix products  27.5 us (9%)
  other arithmetic  14.2 us (5%)
    ppermute x5, waiting for transfers between devices, passed_along(): return lax.ppermute(block, axis, route)  162 us
    ppermute x5, starting transfers between devices, passed_along(): return lax.ppermute(block, axis, route)  66.9 us
    gather x16, local copies, waits for them, and re-layouts  13.5 us
    dot_general x4, matrix products, both_sides(): first = jnp.einsum('ab,nqbc->nqac', m_real, wave, precision=HIGH)  7.25 us
    dot_general x4, matrix products, both_sides(): second = jnp.einsum('ab,nqbc->nqac', m_imag, wave, precision=HIGH)  7.25 us
    select_n x4, other arithmetic, section(): result = jnp.where(active, leaving, result)  6.57 us
    dot_general x4, matrix products, both_sides(): first = jnp.einsum('nqab,bc->nqac', wave, m_real, precision=HIGH)  6.52 us
    dot_general x4, matrix products, both_sides(): second = jnp.einsum('nqab,bc->nqac', wave, m_imag, precision=HIGH)  6.52 us
  transfers between devices with their start and end apart: 5, of which 5 were waited for; matrix products, arithmetic and copies ran while one was open for 2% of the time, Pallas kernels for 0%

commit v1 on v0

v1 whole, which is shorter than its diff:
```python
import functools
import math

import numpy as np
import jax
import jax.numpy as jnp
from jax import lax
from jax.experimental import pallas as pl
from jax.experimental.pallas import tpu as pltpu
from jax.sharding import PartitionSpec as P

CHIRP = 40.0
F32 = jnp.float32
BF16 = jnp.bfloat16
OCTAVES = 120.0
ROOM = 8 * 2**20


def passed_along(block, axis, distance):
    devices = range(lax.axis_size(axis))
    route = [(i - distance, i) for i in devices if i - distance in devices]
    return lax.ppermute(block, axis, route)


def operator_tables(size):
    k = np.arange(size)
    freq = np.where(k < size // 2, k, k - size) / size
    taps = np.fft.ifft(np.exp(-1j * CHIRP * freq * freq))
    half = size // 2
    lag = (np.arange(half)[:, None] - np.arange(half)[None, :]) % size
    right, left = [], []
    for sign in (1.0, -1.0):
        part = 0.5 * (taps[lag] + sign * taps[(lag + half) % size])
        full = np.block([[part.real, part.imag], [-part.imag, part.real]]).astype(np.float32)
        high = full.astype(BF16)
        low = (full - high.astype(np.float32)).astype(BF16)
        right.append(np.concatenate([high, low], axis=0))
        left.append(np.concatenate([high.T, low.T], axis=1))
    return [jnp.asarray(np.stack(right)), jnp.asarray(np.stack(left))]


def fit(function, powers, reach):
    x = np.cos(np.pi * (np.arange(400) + 0.5) / 400) * reach
    basis = np.stack([(x / reach) ** p for p in powers], axis=1)
    found = np.linalg.lstsq(basis, function(x), rcond=None)[0]
    return [float(c / reach**p) for c, p in zip(found, powers)]


def half_angle(position):
    return position * (math.pi / OCTAVES)


SIN_FIT = fit(lambda y: math.sqrt(2.0) * np.sin(half_angle(y)), (1, 3, 5, 7), OCTAVES / 2)
COS_FIT = fit(lambda y: math.sqrt(2.0) * np.cos(half_angle(y)), (0, 2, 4, 6, 8), OCTAVES / 2)


def horner(square, coefficients):
    value = coefficients[-1]
    for c in coefficients[-2::-1]:
        value = value * square + c
    return value


def phase_factor(code):
    position = jnp.log2(code)
    square = position * position
    sine = position * horner(square, SIN_FIT)
    cosine = horner(square, COS_FIT)
    return 1.0 - sine * sine, sine * cosine


def coded(phase):
    turns = phase * (0.5 / math.pi)
    return jnp.exp2(OCTAVES * (turns - jnp.round(turns))).astype(BF16)


def window_kernel(rows_ref, cols_ref, edge_ref, own_ref, next_ref, *refs):
    outs, scratch = refs[:-1], refs[-1]
    layers, strip, width = own_ref.shape
    size = outs[0].shape[-1]
    span = size + 128
    edge = edge_ref[0].astype(F32)
    line = lax.broadcasted_iota(jnp.int32, (strip, span), 0)
    for j, out in enumerate(outs):
        r = rows_ref[j]
        c = cols_ref[j]
        base = jnp.minimum(c // 128, (width - span) // 128)
        shift = c - base * 128
        lanes = pl.ds(pl.multiple_of(base * 128, 128), span)
        for s in range(layers):
            own = own_ref[s, :, lanes].astype(F32)
            following = next_ref[s, :, lanes].astype(F32) + edge
            merged = jnp.where(line >= r, own, following)
            turned = pltpu.roll(merged, span - shift, 1)[:, :size]
            for part in range(size // 128):
                columns = turned[:, part * 128 : (part + 1) * 128]
                scratch[part, pl.ds(0, strip), :] = columns
                scratch[part, pl.ds(strip, strip), :] = columns
                out[s, :, part * 128 : (part + 1) * 128] = scratch[part, pl.ds(r, size), :].astype(BF16)


SMEM = pl.BlockSpec(memory_space=pltpu.SMEM)
VMEM = pl.BlockSpec(memory_space=pltpu.VMEM)


def windows(own, following, rows, cols, edge, size):
    layers, strip, _ = own.shape
    count = rows.shape[0]
    return pl.pallas_call(
        window_kernel,
        out_shape=[jax.ShapeDtypeStruct((layers, size, size), BF16)] * count,
        in_specs=[SMEM, SMEM, SMEM, VMEM, VMEM],
        out_specs=[VMEM] * count,
        scratch_shapes=[pltpu.VMEM((size // 128, 2 * strip, 128), F32)],
        compiler_params=pltpu.CompilerParams(vmem_limit_bytes=ROOM),
    )(rows, cols, edge, own, following)


def product(a, b):
    return jnp.dot(a, b, preferred_element_type=F32)


def propagated(real, imag, right_ref, left_ref):
    size = real.shape[-1]
    half = size // 2

    def right(k, sign):
        data = jnp.concatenate([real[:, :half] + sign * real[:, half:], imag[:, :half] + sign * imag[:, half:]], axis=1).astype(BF16)
        return product(data, right_ref[k, :size]) + product(data, right_ref[k, size:])

    plus, minus = right(0, 1.0), right(1, -1.0)
    re = jnp.concatenate([plus[:, :half], minus[:, :half]], axis=1)
    im = jnp.concatenate([plus[:, half:], minus[:, half:]], axis=1)

    def left(k, sign):
        data = jnp.concatenate([re[:half] + sign * re[half:], im[:half] + sign * im[half:]], axis=0).astype(BF16)
        return product(left_ref[k, :, :size], data) + product(left_ref[k, :, size:], data)

    top, low = left(0, 1.0), left(1, -1.0)
    re = jnp.concatenate([top[:half] + low[:half], top[:half] - low[:half]], axis=0)
    im = jnp.concatenate([top[half:] + low[half:], top[half:] - low[half:]], axis=0)
    real = jnp.concatenate([re[:, :half] + re[:, half:], re[:, :half] - re[:, half:]], axis=1)
    imag = jnp.concatenate([im[:, :half] + im[:, half:], im[:, :half] - im[:, half:]], axis=1)
    return real, imag


def group_kernel(distance, place, group_ref, probe_ref, wave_ref, layers_ref, right_ref, left_ref, *refs):
    out_ref = refs[-1]
    out = out_ref if place is None else out_ref.at[0]
    group = group_ref[0]

    @pl.when(group >= distance)
    def _():
        first = group == distance
        real = jnp.where(first, probe_ref[0], wave_ref[0].astype(F32))
        imag = jnp.where(first, probe_ref[1], wave_ref[1].astype(F32))
        for s in range(layers_ref.shape[0]):
            cosine, sine = phase_factor(layers_ref[s].astype(F32))
            real, imag = cosine * real - sine * imag, cosine * imag + sine * real
            real, imag = propagated(real, imag, right_ref, left_ref)
        out[0] = real.astype(BF16)
        out[1] = imag.astype(BF16)


def through_group(distance, group, probe, wave, layers, tables, place=None, count=None, partial=None):
    arguments = [group, probe, wave, layers, *tables]
    specs = [SMEM] + [VMEM] * 5
    aliases = {}
    if place is None:
        out_shape, out_spec = jax.ShapeDtypeStruct(wave.shape, BF16), VMEM
    else:
        out_shape = jax.ShapeDtypeStruct((count, *wave.shape), BF16)
        out_spec = pl.BlockSpec((1, *wave.shape), lambda i: (place, 0, 0, 0))
        specs = [SMEM] + [pl.BlockSpec(a.shape, lambda i, n=a.ndim: (0,) * n) for a in arguments[1:]]
        if partial is not None:
            arguments.append(partial)
            specs.append(pl.BlockSpec(memory_space=pl.ANY))
            aliases = {len(arguments) - 1: 0}
    return pl.pallas_call(
        functools.partial(group_kernel, distance, place),
        out_shape=out_shape,
        grid=() if place is None else (1,),
        in_specs=specs,
        out_specs=out_spec,
        input_output_aliases=aliases,
        compiler_params=pltpu.CompilerParams(vmem_limit_bytes=ROOM),
    )(*arguments)


def gathered(layers, groups):
    arrived = {0: layers}
    for distance in range(1, groups):
        arrived[distance] = [None] * len(layers)
    for j, block in enumerate(layers):
        for distance in range(groups - 1, 0, -1):
            arrived[distance][j] = passed_along(block, "depth", distance)
    return arrived


def body(probe, phase, row_offsets, col_offsets):
    size = probe.shape[-1]
    strip = phase.shape[1]
    count = row_offsets.shape[0]
    groups = lax.axis_size("depth")
    strips = lax.axis_size("probe")
    group = lax.axis_index("depth").astype(jnp.int32).reshape(1)
    place = lax.axis_index("probe")
    own = coded(phase)
    following = passed_along(own, "probe", -1)
    rows = row_offsets - place * strip
    edge = (place == strips - 1).astype(jnp.int32).reshape(1)
    layers = windows(own, following, rows, col_offsets, edge, size)
    tables = operator_tables(size)
    arrived = gathered(layers, groups)
    result = None
    for j in range(count):
        wave = jnp.zeros((2, size, size), BF16)
        for distance in range(groups - 1, 0, -1):
            wave = through_group(distance, group, probe, wave, arrived[distance][j], tables)
        result = through_group(0, group, probe, wave, arrived[0][j], tables, j, count, result)
    return result[None]


def solution(mesh):
    return jax.shard_map(
        body,
        mesh=mesh,
        in_specs=(P(), P("depth", "probe", None), P("probe"), P("probe")),
        out_specs=P("depth", "probe", None, None, None),
        check_vma=False,
    )
```

time: 302 us -> 52.8 us (0.17)
  waiting for transfers between devices: 162 us -> 20.5 us
  starting transfers between devices: 66.9 us -> 16.7 us
  local copies, waits for them, and re-layouts: 27.8 us -> 0.04 us
  matrix products: 27.5 us -> 0 us
  Pallas kernels: 0 us -> 13.3 us
  other arithmetic: 14.2 us -> 1.87 us
    ppermute x5 -> x7, waiting for transfers between devices: 162 us -> 20.5 us  [passed_along(): return lax.ppermute(block, axis, route)]
    ppermute x5 -> x7, starting transfers between devices: 66.9 us -> 16.7 us  [passed_along(): return lax.ppermute(block, axis, route)]
    dot_general x16 -> x0, matrix products: 27.5 us -> none  [the longest x4 7.25 us: both_sides(): first = jnp.einsum('ab,nqbc->nqac', m_real, wave, precision=HIGH)]
    gather x16 -> x0, local copies, waits for them, and re-layouts: 13.5 us -> none
    pallas_call x0 -> x9, Pallas kernels: none -> 13.3 us  [the longest x8 11.4 us: through_group(): pl.pallas_call(functools.partial(group_kernel, distance, place), out_shap...]
    select_n x5 -> x0, other arithmetic: 7.72 us -> none  [the longest x4 6.57 us: section(): result = jnp.where(active, leaving, result)]
    cos x3 -> x0, local copies, waits for them, and re-layouts: 7.11 us -> none  [the longest x2 6.27 us: traverse(): trans_real = jnp.cos(windows)]
    squeeze x1 -> x0, local copies, waits for them, and re-layouts: 3.26 us -> none  [traverse(): layer = extended[inner]]
  transfers between devices with their start and end apart: 5 -> 7, of which waited for: 5 -> 2; matrix products, arithmetic and copies ran while one was open for 2% -> 0% of each run, Pallas kernels for 0% -> 15%
where the time goes in v1:
time: 52.8 us; the launch traced here: 52.6 us
  waiting for transfers between devices  20.5 us (39%)
  starting transfers between devices  16.7 us (32%)
  Pallas kernels  13.3 us (25%)
  other arithmetic  1.87 us (4%)
    ppermute x7, waiting for transfers between devices, passed_along(): return lax.ppermute(block, axis, route)  20.5 us
    ppermute x7, starting transfers between devices, passed_along(): return lax.ppermute(block, axis, route)  16.7 us
    pallas_call x8, Pallas kernels, through_group(): pl.pallas_call(functools.partial(group_kernel, distance, place), out_shap...  11.4 us
    convert_element_type x1, other arithmetic, coded(): return jnp.exp2(OCTAVES * (turns - jnp.round(turns))).astype(BF16)  1.87 us
    pallas_call x1, Pallas kernels, windows(): pl.pallas_call(window_kernel, out_shape=[jax.ShapeDtypeStruct((layers, si...  1.85 us
  transfers between devices with their start and end apart: 7, of which 2 were waited for; matrix products, arithmetic and copies ran while one was open for 0% of the time, Pallas kernels for 15%

profile of v1, /device:TPU:21, one launch (start us, length us, event | category | flops | bytes accessed | tf_op | source)
XLA Modules:
  0.0 52.6 jit_solution(2326054910377602658)
XLA Ops:
  0.0 0.0 copy-start.1
  0.0 0.0 copy-start.2
  0.0 0.0 copy-start.4
  0.0 0.0 copy-start.3
  0.0 0.0 copy-start
  0.0 1.9 %fusion.2.own_ref = bf16[2,256,768]{2,1,0:T(8,128)(2,1)S(1)} fusion(f32[2,256,768]{2,1,0:T(8,128)} %param.7), kind=kLoop, calls=%fused_computation.3 | loop fusion | flops 1966080 | bytes 2359296 | tf_op jit(solution)/shard_map/convert_element_type | solution.py:74
  1.9 2.6 %collective-permute-start = (bf16[2,256,768]{2,1,0:T(8,128)(2,1)S(1)}, bf16[2,256,768]{2,1,0:T(8,128)(2,1)S(1)}, u32[]{:S(2)}, u32[]{:S(2)}) collective-permute-start(bf16[2,256,768]{2,1,0:T(8,128)(2,1)S(1)} %fusion.2.own_ref), channel_id=1, source_target_pairs={{1,0},{2,1},{3,2},{4,3},{5,4},{6,5},{7,6},{9,8},{10,9},{11,10},{12... | collective-permute-start | bytes 2359304 | tf_op jit(solution)/shard_map/ppermute | solution.py:22
  4.5 0.0 copy-done.4
  4.5 10.8 %collective-permute-done.next_ref = bf16[2,256,768]{2,1,0:T(8,128)(2,1)S(1)} collective-permute-done((bf16[2,256,768]{2,1,0:T(8,128)(2,1)S(1)}, bf16[2,256,768]{2,1,0:T(8,128)(2,1)S(1)}, u32[]{:S(2)}, u32[]{:S(2)}) %collective-permute-start) | collective-permute-done | bytes 786464 | tf_op jit(solution)/shard_map/ppermute | solution.py:22
  15.3 0.0 copy-done.3
  15.3 1.8 %shard_map.64 = (bf16[2,256,256]{2,1,0:T(8,128)(2,1)}, bf16[2,256,256]{2,1,0:T(8,128)(2,1)S(1)}) custom-call(s32[2]{0:T(128)S(1)} %broadcast_subtract_fusion.rows_ref, s32[2]{0:T(128)S(1)} %copy-done.3, s32[1]{0:T(128)} %bitcast.1.edge_ref, bf16[2,256,768]{2,1,0:T(8,128)(2,1)S(1)} %fusion.2.own_ref, bf16[2,256,768]{2,1,0:T(8,128)(2,1)S(1)} %collective-permute-done.next_ref), custom_call_target="tpu_custom_call" | custom-call | tf_op jit(solution)/shard_map/pallas_call | solution.py:109
  17.2 0.7 %collective-permute-start.4 = (bf16[2,256,256]{2,1,0:T(8,128)(2,1)}, bf16[2,256,256]{2,1,0:T(8,128)(2,1)S(1)}, u32[]{:S(2)}, u32[]{:S(2)}) collective-permute-start(bf16[2,256,256]{2,1,0:T(8,128)(2,1)} %get-tuple-element.8.layers_ref), channel_id=1, source_target_pairs={{0,24},{1,25},{2,26},{3,27},{4,28},{5,29},{6,30},{7,31}} | collective-permute-start | bytes 786440 | tf_op jit(solution)/shard_map/ppermute | solution.py:22
  17.9 1.3 %collective-permute-start.5 = (bf16[2,256,256]{2,1,0:T(8,128)(2,1)}, bf16[2,256,256]{2,1,0:T(8,128)(2,1)S(1)}, u32[]{:S(2)}, u32[]{:S(2)}) collective-permute-start(bf16[2,256,256]{2,1,0:T(8,128)(2,1)} %get-tuple-element.8.layers_ref), channel_id=1, source_target_pairs={{0,16},{8,24},{1,17},{9,25},{2,18},{10,26},{3,19},{11,27},{4,20},{... | collective-permute-start | bytes 786440 | tf_op jit(solution)/shard_map/ppermute | solution.py:22
  19.2 3.7 %collective-permute-start.6 = (bf16[2,256,256]{2,1,0:T(8,128)(2,1)}, bf16[2,256,256]{2,1,0:T(8,128)(2,1)S(1)}, u32[]{:S(2)}, u32[]{:S(2)}) collective-permute-start(bf16[2,256,256]{2,1,0:T(8,128)(2,1)} %get-tuple-element.8.layers_ref), channel_id=1, source_target_pairs={{0,8},{8,16},{16,24},{1,9},{9,17},{17,25},{2,10},{10,18},{18,26},{... | collective-permute-start | bytes 786440 | tf_op jit(solution)/shard_map/ppermute | solution.py:22
  22.9 0.7 %collective-permute-start.1 = (bf16[2,256,256]{2,1,0:T(8,128)(2,1)S(1)}, bf16[2,256,256]{2,1,0:T(8,128)(2,1)S(1)}, u32[]{:S(2)}, u32[]{:S(2)}) collective-permute-start(bf16[2,256,256]{2,1,0:T(8,128)(2,1)S(1)} %get-tuple-element.7.layers_ref), channel_id=1, source_target_pairs={{0,24},{1,25},{2,26},{3,27},{4,28},{5,29},{6,30},{7,31}} | collective-permute-start | bytes 786440 | tf_op jit(solution)/shard_map/ppermute | solution.py:22
  23.6 1.3 %collective-permute-start.2 = (bf16[2,256,256]{2,1,0:T(8,128)(2,1)S(1)}, bf16[2,256,256]{2,1,0:T(8,128)(2,1)S(1)}, u32[]{:S(2)}, u32[]{:S(2)}) collective-permute-start(bf16[2,256,256]{2,1,0:T(8,128)(2,1)S(1)} %get-tuple-element.7.layers_ref), channel_id=1, source_target_pairs={{0,16},{8,24},{1,17},{9,25},{2,18},{10,26},{3,19},{11,27},{4,20},{... | collective-permute-start | bytes 786440 | tf_op jit(solution)/shard_map/ppermute | solution.py:22
  24.9 0.0 collective-permute-done.4.layers_ref
  24.9 6.5 %collective-permute-start.3 = (bf16[2,256,256]{2,1,0:T(8,128)(2,1)S(1)}, bf16[2,256,256]{2,1,0:T(8,128)(2,1)S(1)}, u32[]{:S(2)}, u32[]{:S(2)}) collective-permute-start(bf16[2,256,256]{2,1,0:T(8,128)(2,1)S(1)} %get-tuple-element.7.layers_ref), channel_id=1, source_target_pairs={{0,8},{8,16},{16,24},{1,9},{9,17},{17,25},{2,10},{10,18},{18,26},{... | collective-permute-start | bytes 786440 | tf_op jit(solution)/shard_map/ppermute | solution.py:22
  31.4 0.0 copy-done.1
  31.4 0.0 copy-done.2
  31.4 0.0 copy-done
  31.4 9.6 %collective-permute-done.5.layers_ref = bf16[2,256,256]{2,1,0:T(8,128)(2,1)S(1)} collective-permute-done((bf16[2,256,256]{2,1,0:T(8,128)(2,1)}, bf16[2,256,256]{2,1,0:T(8,128)(2,1)S(1)}, u32[]{:S(2)}, u32[]{:S(2)}) %collective-permute-start.5) | collective-permute-done | bytes 262176 | tf_op jit(solution)/shard_map/ppermute | solution.py:22
  41.1 1.5 %shard_map.69.wave_ref = bf16[2,256,256]{2,1,0:T(8,128)(2,1)S(1)} custom-call(s32[1]{0:T(128)} %bitcast.group_ref, f32[2,256,256]{2,1,0:T(8,128)S(1)} %copy-done, bf16[2,256,256]{2,1,0:T(8,128)(2,1)S(1)} %shard_map.68.wave_ref, bf16[2,256,256]{2,1,0:T(8,128)(2,1)S(1)} %collective-permute-done.5.layers_ref, bf16[2,512,256]{2,1,0:T(8,128)(2,1)S(1)} %copy-done.1, ...), custom_call_target="tpu_custom_call" | custom-call | tf_op jit(solution)/shard_map/pallas_call | solution.py:179
  42.6 0.0 collective-permute-done.6.layers_ref
  42.6 1.5 %shard_map.70.wave_ref = bf16[2,256,256]{2,1,0:T(8,128)(2,1)S(1)} custom-call(s32[1]{0:T(128)} %bitcast.group_ref, f32[2,256,256]{2,1,0:T(8,128)S(1)} %copy-done, bf16[2,256,256]{2,1,0:T(8,128)(2,1)S(1)} %shard_map.69.wave_ref, bf16[2,256,256]{2,1,0:T(8,128)(2,1)S(1)} %collective-permute-done.6.layers_ref, bf16[2,512,256]{2,1,0:T(8,128)(2,1)S(1)} %copy-done.1, ...), custom_call_target="tpu_custom_call" | custom-call | tf_op jit(solution)/shard_map/pallas_call | solution.py:179
  44.1 3.2 %shard_map.71.refs_0_ = bf16[2,2,256,256]{3,2,1,0:T(8,128)(2,1)} custom-call(s32[1]{0:T(128)} %bitcast.group_ref, f32[2,256,256]{2,1,0:T(8,128)S(1)} %copy-done, bf16[2,256,256]{2,1,0:T(8,128)(2,1)S(1)} %shard_map.70.wave_ref, bf16[2,256,256]{2,1,0:T(8,128)(2,1)} %get-tuple-element.8.layers_ref, bf16[2,512,256]{2,1,0:T(8,128)(2,1)S(1)} %copy-done.1, ...), custom_call_target="tpu_custom_call" | custom-call | tf_op jit(solution)/shard_map/pallas_call | solution.py:179
  47.3 0.0 collective-permute-done.1.layers_ref
  47.3 0.0 collective-permute-done.2.layers_ref
  47.3 1.5 %shard_map.66.wave_ref = bf16[2,256,256]{2,1,0:T(8,128)(2,1)S(1)} custom-call(s32[1]{0:T(128)} %bitcast.group_ref, f32[2,256,256]{2,1,0:T(8,128)S(1)} %copy-done, bf16[2,256,256]{2,1,0:T(8,128)(2,1)S(1)} %shard_map.65.wave_ref, bf16[2,256,256]{2,1,0:T(8,128)(2,1)S(1)} %collective-permute-done.2.layers_ref, bf16[2,512,256]{2,1,0:T(8,128)(2,1)S(1)} %copy-done.1, ...), custom_call_target="tpu_custom_call" | custom-call | tf_op jit(solution)/shard_map/pallas_call | solution.py:179
  48.8 0.0 collective-permute-done.3.layers_ref
  48.8 1.5 %shard_map.67.wave_ref = bf16[2,256,256]{2,1,0:T(8,128)(2,1)S(1)} custom-call(s32[1]{0:T(128)} %bitcast.group_ref, f32[2,256,256]{2,1,0:T(8,128)S(1)} %copy-done, bf16[2,256,256]{2,1,0:T(8,128)(2,1)S(1)} %shard_map.66.wave_ref, bf16[2,256,256]{2,1,0:T(8,128)(2,1)S(1)} %collective-permute-done.3.layers_ref, bf16[2,512,256]{2,1,0:T(8,128)(2,1)S(1)} %copy-done.1, ...), custom_call_target="tpu_custom_call" | custom-call | tf_op jit(solution)/shard_map/pallas_call | solution.py:179
  50.3 2.2 %shard_map.72 = bf16[2,2,256,256]{3,2,1,0:T(8,128)(2,1)} custom-call(s32[1]{0:T(128)} %bitcast.group_ref, f32[2,256,256]{2,1,0:T(8,128)S(1)} %copy-done, bf16[2,256,256]{2,1,0:T(8,128)(2,1)S(1)} %shard_map.67.wave_ref, bf16[2,256,256]{2,1,0:T(8,128)(2,1)S(1)} %get-tuple-element.7.layers_ref, ...), custom_call_target="tpu_custom_call", output_to_operand_aliasing={{}: (6, {})} | custom-call | tf_op jit(solution)/shard_map/pallas_call | solution.py:179
  (4 shorter events, 0.0 us)
Async XLA Ops:
  0.0 31.4 %copy-start.1 = (bf16[2,512,256]{2,1,0:T(8,128)(2,1)S(1)}, bf16[2,512,256]{2,1,0:T(8,128)(2,1)}, u32[]{:S(2)}) copy-start(bf16[2,512,256]{2,1,0:T(8,128)(2,1)} %constant.24.clone.right_ref) | copy-start | bytes 1572868
  0.0 31.4 %copy-start.2 = (bf16[2,256,512]{2,1,0:T(8,128)(2,1)S(1)}, bf16[2,256,512]{2,1,0:T(8,128)(2,1)}, u32[]{:S(2)}) copy-start(bf16[2,256,512]{2,1,0:T(8,128)(2,1)} %constant.25.clone.left_ref) | copy-start | bytes 1572868
  0.0 4.5 %copy-start.4 = (s32[2]{0:T(128)S(1)}, s32[2]{0:T(128)}, u32[]{:S(2)}) copy-start(s32[2]{0:T(128)} %param.8) | copy-start | bytes 28
  0.0 15.3 %copy-start.3 = (s32[2]{0:T(128)S(1)}, s32[2]{0:T(128)}, u32[]{:S(2)}) copy-start(s32[2]{0:T(128)} %cols_ref.1) | copy-start | bytes 28
  0.0 31.4 %copy-start = (f32[2,256,256]{2,1,0:T(8,128)S(1)}, f32[2,256,256]{2,1,0:T(8,128)}, u32[]{:S(2)}) copy-start(f32[2,256,256]{2,1,0:T(8,128)} %probe_ref.15) | copy-start | bytes 1572868
  1.9 13.4 %collective-permute-start = (bf16[2,256,768]{2,1,0:T(8,128)(2,1)S(1)}, bf16[2,256,768]{2,1,0:T(8,128)(2,1)S(1)}, u32[]{:S(2)}, u32[]{:S(2)}) collective-permute-start(bf16[2,256,768]{2,1,0:T(8,128)(2,1)S(1)} %fusion.2.own_ref), channel_id=1, source_target_pairs={{1,0},{2,1},{3,2},{4,3},{5,4},{6,5},{7,6},{9,8},{10,9},{11,10},{12... | collective-permute-start | bytes 2359304 | tf_op jit(solution)/shard_map/ppermute | solution.py:22
  17.2 7.7 %collective-permute-start.4 = (bf16[2,256,256]{2,1,0:T(8,128)(2,1)}, bf16[2,256,256]{2,1,0:T(8,128)(2,1)S(1)}, u32[]{:S(2)}, u32[]{:S(2)}) collective-permute-start(bf16[2,256,256]{2,1,0:T(8,128)(2,1)} %get-tuple-element.8.layers_ref), channel_id=1, source_target_pairs={{0,24},{1,25},{2,26},{3,27},{4,28},{5,29},{6,30},{7,31}} | collective-permute-start | bytes 786440 | tf_op jit(solution)/shard_map/ppermute | solution.py:22
  17.9 23.2 %collective-permute-start.5 = (bf16[2,256,256]{2,1,0:T(8,128)(2,1)}, bf16[2,256,256]{2,1,0:T(8,128)(2,1)S(1)}, u32[]{:S(2)}, u32[]{:S(2)}) collective-permute-start(bf16[2,256,256]{2,1,0:T(8,128)(2,1)} %get-tuple-element.8.layers_ref), channel_id=1, source_target_pairs={{0,16},{8,24},{1,17},{9,25},{2,18},{10,26},{3,19},{11,27},{4,20},{... | collective-permute-start | bytes 786440 | tf_op jit(solution)/shard_map/ppermute | solution.py:22
  19.2 23.4 %collective-permute-start.6 = (bf16[2,256,256]{2,1,0:T(8,128)(2,1)}, bf16[2,256,256]{2,1,0:T(8,128)(2,1)S(1)}, u32[]{:S(2)}, u32[]{:S(2)}) collective-permute-start(bf16[2,256,256]{2,1,0:T(8,128)(2,1)} %get-tuple-element.8.layers_ref), channel_id=1, source_target_pairs={{0,8},{8,16},{16,24},{1,9},{9,17},{17,25},{2,10},{10,18},{18,26},{... | collective-permute-start | bytes 786440 | tf_op jit(solution)/shard_map/ppermute | solution.py:22
  22.9 24.4 %collective-permute-start.1 = (bf16[2,256,256]{2,1,0:T(8,128)(2,1)S(1)}, bf16[2,256,256]{2,1,0:T(8,128)(2,1)S(1)}, u32[]{:S(2)}, u32[]{:S(2)}) collective-permute-start(bf16[2,256,256]{2,1,0:T(8,128)(2,1)S(1)} %get-tuple-element.7.layers_ref), channel_id=1, source_target_pairs={{0,24},{1,25},{2,26},{3,27},{4,28},{5,29},{6,30},{7,31}} | collective-permute-start | bytes 786440 | tf_op jit(solution)/shard_map/ppermute | solution.py:22
  23.6 23.7 %collective-permute-start.2 = (bf16[2,256,256]{2,1,0:T(8,128)(2,1)S(1)}, bf16[2,256,256]{2,1,0:T(8,128)(2,1)S(1)}, u32[]{:S(2)}, u32[]{:S(2)}) collective-permute-start(bf16[2,256,256]{2,1,0:T(8,128)(2,1)S(1)} %get-tuple-element.7.layers_ref), channel_id=1, source_target_pairs={{0,16},{8,24},{1,17},{9,25},{2,18},{10,26},{3,19},{11,27},{4,20},{... | collective-permute-start | bytes 786440 | tf_op jit(solution)/shard_map/ppermute | solution.py:22
  24.9 23.9 %collective-permute-start.3 = (bf16[2,256,256]{2,1,0:T(8,128)(2,1)S(1)}, bf16[2,256,256]{2,1,0:T(8,128)(2,1)S(1)}, u32[]{:S(2)}, u32[]{:S(2)}) collective-permute-start(bf16[2,256,256]{2,1,0:T(8,128)(2,1)S(1)} %get-tuple-element.7.layers_ref), channel_id=1, source_target_pairs={{0,8},{8,16},{16,24},{1,9},{9,17},{17,25},{2,10},{10,18},{18,26},{... | collective-permute-start | bytes 786440 | tf_op jit(solution)/shard_map/ppermute | solution.py:22

commit v2 on v1

v2 whole, which is shorter than its diff:
```python
import functools
import math

import numpy as np
import jax
import jax.numpy as jnp
from jax import lax
from jax.experimental import pallas as pl
from jax.experimental.pallas import tpu as pltpu
from jax.sharding import PartitionSpec as P


CHIRP = 40.0
F32 = jnp.float32
BF16 = jnp.bfloat16
OCTAVES = 120.0
ROOM = 8 * 2**20


def handed_down(block, parity):
    strips = lax.axis_size("probe")
    return lax.ppermute(block, "probe", [(i + 1, i) for i in range(parity, strips - 1, 2)])


def sent_on(block, parity, pairs):
    strips = lax.axis_size("probe")
    route = [(a * strips + p, b * strips + p) for a, b in pairs for p in range(parity, strips, 2)]
    return lax.ppermute(block, ("depth", "probe"), route)


def operator_tables(size):
    k = np.arange(size)
    freq = np.where(k < size // 2, k, k - size) / size
    taps = np.fft.ifft(np.exp(-1j * CHIRP * freq * freq))
    half = size // 2
    lag = (np.arange(half)[:, None] - np.arange(half)[None, :]) % size
    right, left = [], []
    for sign in (1.0, -1.0):
        part = 0.5 * (taps[lag] + sign * taps[(lag + half) % size])
        full = np.block([[part.real, part.imag], [-part.imag, part.real]]).astype(np.float32)
        high = full.astype(BF16)
        low = (full - high.astype(np.float32)).astype(BF16)
        right.append(np.concatenate([high, low], axis=0))
        left.append(np.concatenate([high.T, low.T], axis=1))
    return [jnp.asarray(np.stack(right)), jnp.asarray(np.stack(left))]


def fit(function, powers, reach):
    x = np.cos(np.pi * (np.arange(400) + 0.5) / 400) * reach
    basis = np.stack([(x / reach) ** p for p in powers], axis=1)
    found = np.linalg.lstsq(basis, function(x), rcond=None)[0]
    return [float(c / reach**p) for c, p in zip(found, powers)]


def half_angle(position):
    return position * (math.pi / OCTAVES)


SIN_FIT = fit(lambda y: math.sqrt(2.0) * np.sin(half_angle(y)), (1, 3, 5, 7), OCTAVES / 2)
COS_FIT = fit(lambda y: math.sqrt(2.0) * np.cos(half_angle(y)), (0, 2, 4, 6, 8), OCTAVES / 2)


def horner(square, coefficients):
    value = coefficients[-1]
    for c in coefficients[-2::-1]:
        value = value * square + c
    return value


def phase_factor(code):
    position = jnp.log2(code)
    square = position * position
    sine = position * horner(square, SIN_FIT)
    cosine = horner(square, COS_FIT)
    return 1.0 - sine * sine, sine * cosine


def coded(phase):
    turns = phase * (0.5 / math.pi)
    return jnp.exp2(OCTAVES * (turns - jnp.round(turns))).astype(BF16)


SMEM = pl.BlockSpec(memory_space=pltpu.SMEM)
VMEM = pl.BlockSpec(memory_space=pltpu.VMEM)


def product(a, b):
    return jnp.dot(a, b, preferred_element_type=F32)


def propagated(real, imag, right_ref, left_ref):
    size = real.shape[-1]
    half = size // 2

    def right(k, sign):
        data = jnp.concatenate([real[:, :half] + sign * real[:, half:], imag[:, :half] + sign * imag[:, half:]], axis=1).astype(BF16)
        return product(data, right_ref[k, :size]) + product(data, right_ref[k, size:])

    plus, minus = right(0, 1.0), right(1, -1.0)
    re = jnp.concatenate([plus[:, :half], minus[:, :half]], axis=1)
    im = jnp.concatenate([plus[:, half:], minus[:, half:]], axis=1)

    def left(k, sign):
        data = jnp.concatenate([re[:half] + sign * re[half:], im[:half] + sign * im[half:]], axis=0).astype(BF16)
        return product(left_ref[k, :, :size], data) + product(left_ref[k, :, size:], data)

    top, low = left(0, 1.0), left(1, -1.0)
    re = jnp.concatenate([top[:half] + low[:half], top[:half] - low[:half]], axis=0)
    im = jnp.concatenate([top[half:] + low[half:], top[half:] - low[half:]], axis=0)
    real = jnp.concatenate([re[:, :half] + re[:, half:], re[:, :half] - re[:, half:]], axis=1)
    imag = jnp.concatenate([im[:, :half] + im[:, half:], im[:, :half] - im[:, half:]], axis=1)
    return real, imag


def sliced(real, imag, code, right_ref, left_ref):
    cosine, sine = phase_factor(code.astype(F32))
    real, imag = cosine * real - sine * imag, cosine * imag + sine * real
    return propagated(real, imag, right_ref, left_ref)


def first_kernel(j, parity, where_ref, rows_ref, cols_ref, own_ref, next_ref, probe_ref, right_ref, left_ref, *refs):
    out_ref, scratch = refs[-2:]
    layers, strip, width = own_ref.shape
    size = out_ref.shape[-1]
    span = size + 128

    @pl.when(where_ref[1] % 2 == parity)
    def _():
        edge = where_ref[2].astype(F32)
        line = lax.broadcasted_iota(jnp.int32, (strip, span), 0)
        r = rows_ref[j]
        c = cols_ref[j]
        base = jnp.minimum(c // 128, (width - span) // 128)
        shift = c - base * 128
        lanes = pl.ds(pl.multiple_of(base * 128, 128), span)
        for s in range(layers):
            own = own_ref[s, :, lanes].astype(F32)
            following = next_ref[s, :, lanes].astype(F32) + edge
            merged = jnp.where(line >= r, own, following)
            turned = pltpu.roll(merged, span - shift, 1)[:, :size]
            for part in range(size // 128):
                columns = turned[:, part * 128 : (part + 1) * 128]
                scratch[part, pl.ds(0, strip), :] = columns
                scratch[part, pl.ds(strip, strip), :] = columns
                out_ref[s, :, part * 128 : (part + 1) * 128] = scratch[part, pl.ds(r, size), :].astype(BF16)

        @pl.when(where_ref[0] == 0)
        def _():
            real, imag = probe_ref[0], probe_ref[1]
            for s in range(layers):
                real, imag = sliced(real, imag, out_ref[s], right_ref, left_ref)
            out_ref[0] = real.astype(BF16)
            out_ref[1] = imag.astype(BF16)


def first_group(j, parity, where, rows, cols, own, following, probe, tables, after):
    layers, strip, _ = own.shape
    size = probe.shape[-1]
    return pl.pallas_call(
        functools.partial(first_kernel, j, parity),
        out_shape=jax.ShapeDtypeStruct((layers, size, size), BF16),
        in_specs=[SMEM, SMEM, SMEM] + [VMEM] * (5 + len(after)),
        out_specs=VMEM,
        scratch_shapes=[pltpu.VMEM((size // 128, 2 * strip, 128), F32)],
        compiler_params=pltpu.CompilerParams(vmem_limit_bytes=ROOM),
    )(where, rows, cols, own, following, probe, *tables, *after)


def chain_kernel(groups, before, where_ref, right_ref, left_ref, *refs):
    arrived = (refs[:groups], refs[groups : 2 * groups])
    out_ref, wave_ref = refs[-2], refs[-1]
    group = where_ref[0]
    parity = where_ref[1] % 2

    def block(offset, s):
        value = jnp.where(parity == 0, arrived[0][0][s], arrived[1][0][s])
        for m in range(1, groups):
            value = jnp.where(offset == m, jnp.where(parity == 0, arrived[0][m][s], arrived[1][m][s]), value)
        return value

    for s in range(2):
        wave_ref[s] = block(group, s)

    def step(g, _):
        real, imag = wave_ref[0].astype(F32), wave_ref[1].astype(F32)
        for s in range(arrived[0][0].shape[0]):
            real, imag = sliced(real, imag, block(g ^ group, s), right_ref, left_ref)
        wave_ref[0] = real.astype(BF16)
        wave_ref[1] = imag.astype(BF16)
        return 0

    lax.fori_loop(1, group + 1, step, 0)
    out_ref[before] = wave_ref[...]
    for j in range(before):
        out_ref[j] = refs[2 * groups + j][0]


def chain(where, tables, even, odd, finished):
    groups = len(even)
    shape = (2, *even[0].shape[1:])
    arguments = [where, *tables, *even, *odd, *finished]
    return pl.pallas_call(
        functools.partial(chain_kernel, groups, len(finished)),
        out_shape=jax.ShapeDtypeStruct((len(finished) + 1, *shape), BF16),
        in_specs=[SMEM] + [VMEM] * (len(arguments) - 1),
        out_specs=VMEM,
        scratch_shapes=[pltpu.VMEM(shape, BF16)],
        compiler_params=pltpu.CompilerParams(vmem_limit_bytes=ROOM),
    )(*arguments)


def mark_kernel(block_ref, out_ref):
    out_ref[...] = block_ref[0, :16, :128]


def mark(block):
    return pl.pallas_call(
        mark_kernel,
        out_shape=jax.ShapeDtypeStruct((16, 128), BF16),
        in_specs=[VMEM],
        out_specs=VMEM,
        compiler_params=pltpu.CompilerParams(vmem_limit_bytes=ROOM),
    )(block)


def body(probe, phase, row_offsets, col_offsets):
    size = probe.shape[-1]
    strip = phase.shape[1]
    count = row_offsets.shape[0]
    groups = lax.axis_size("depth")
    strips = lax.axis_size("probe")
    group = lax.axis_index("depth")
    place = lax.axis_index("probe")
    where = jnp.stack([group, place, (place == strips - 1).astype(jnp.int32)]).astype(jnp.int32)
    rows = row_offsets - place * strip
    tables = operator_tables(size)
    own = coded(phase)
    following = {}
    for parity in (1, 0):
        following[parity] = handed_down(own, parity)
    arrived = {0: [], 1: []}
    after = []
    for parity in (0, 1):
        for j in range(count):
            first = first_group(j, parity, where, rows, col_offsets, own, following[parity], probe, tables, after)
            after = [first]
            blocks = {0: first}
            for m in ORDER if groups == 4 else range(1, groups):
                blocks[m] = sent_on(first, parity, [(i, i ^ m) for i in range(groups) if i < i ^ m < groups])
            arrived[parity].append([blocks[m] for m in range(groups)])
        if parity == 0:
            after = after + [mark(first)]
    finished = []
    for j in range(count):
        wave = chain(where, tables, arrived[0][j], arrived[1][j], finished if j == count - 1 else [])
        finished.append(wave)
    return wave[None]


ORDER = (2, 3, 1)


def solution(mesh):
    return jax.shard_map(
        body,
        mesh=mesh,
        in_specs=(P(), P("depth", "probe", None), P("probe"), P("probe")),
        out_specs=P("depth", "probe", None, None, None),
        check_vma=False,
    )
```

time: 52.8 us -> 58.6 us (1.11)
  waiting for transfers between devices: 20.5 us -> 24.1 us
  starting transfers between devices: 16.7 us -> 19.2 us
  Pallas kernels: 13.3 us -> 12.6 us
    ppermute x7 -> x14, waiting for transfers between devices: 20.5 us -> 24.1 us  [the longest x12 14.6 us: sent_on(): return lax.ppermute(block, ('depth', 'probe'), route)]
    ppermute x7 -> x14, starting transfers between devices: 16.7 us -> 19.2 us  [the longest x12 14.5 us: sent_on(): return lax.ppermute(block, ('depth', 'probe'), route)]
    pallas_call x9 -> x7, Pallas kernels: 13.3 us -> 12.6 us  [the longest x2 8.42 us: chain(): pl.pallas_call(functools.partial(chain_kernel, groups, len(finished)), ou...]
  transfers between devices with their start and end apart: 7 -> 14, of which waited for: 2 -> 3; matrix products, arithmetic and copies ran while one was open for 0% -> 0% of each run, Pallas kernels for 15% -> 12%
where the time goes in v2:
time: 58.6 us; the launch traced here: 58.2 us
  waiting for transfers between devices  24.1 us (41%)
  starting transfers between devices  19.2 us (33%)
  Pallas kernels  12.6 us (22%)
  other arithmetic  1.95 us (3%)
    ppermute x12, waiting for transfers between devices, sent_on(): return lax.ppermute(block, ('depth', 'probe'), route)  14.6 us
    ppermute x12, starting transfers between devices, sent_on(): return lax.ppermute(block, ('depth', 'probe'), route)  14.5 us
    ppermute x2, waiting for transfers between devices, handed_down(): lax.ppermute(block, 'probe', [(i + 1, i) for i in range(parity, strips -...  9.53 us
    pallas_call x2, Pallas kernels, chain(): pl.pallas_call(functools.partial(chain_kernel, groups, len(finished)), ou...  8.42 us
    ppermute x2, starting transfers between devices, handed_down(): lax.ppermute(block, 'probe', [(i + 1, i) for i in range(parity, strips -...  4.76 us
    pallas_call x4, Pallas kernels, first_group(): pl.pallas_call(functools.partial(first_kernel, j, parity), out_shape=jax....  4.19 us
    convert_element_type x1, other arithmetic, coded(): return jnp.exp2(OCTAVES * (turns - jnp.round(turns))).astype(BF16)  1.87 us
  transfers between devices with their start and end apart: 14, of which 3 were waited for; matrix products, arithmetic and copies ran while one was open for 0% of the time, Pallas kernels for 12%

profile of v2, /device:TPU:21, one launch (start us, length us, event | category | flops | bytes accessed | tf_op | source)
XLA Modules:
  0.0 58.2 jit_solution(3491567327527407159)
XLA Ops:
  0.0 1.9 %fusion.2.own_ref = bf16[2,256,768]{2,1,0:T(8,128)(2,1)S(1)} fusion(f32[2,256,768]{2,1,0:T(8,128)} %param.7), kind=kLoop, calls=%fused_computation.3 | loop fusion | flops 1966080 | bytes 2359296 | tf_op jit(solution)/shard_map/convert_element_type | solution.py:80
  1.9 3.5 %collective-permute-start = (bf16[2,256,768]{2,1,0:T(8,128)(2,1)S(1)}, bf16[2,256,768]{2,1,0:T(8,128)(2,1)}, u32[]{:S(2)}, u32[]{:S(2)}) collective-permute-start(bf16[2,256,768]{2,1,0:T(8,128)(2,1)S(1)} %fusion.2.own_ref), channel_id=1, source_target_pairs={{1,0},{3,2},{5,4},{7,6},{9,8},{11,10},{13,12},{15,14},{17,16},{19,... | collective-permute-start | bytes 2359304 | tf_op jit(solution)/shard_map/ppermute | solution.py:22
  5.4 1.3 %collective-permute-start.4 = (bf16[2,256,768]{2,1,0:T(8,128)(2,1)S(1)}, bf16[2,256,768]{2,1,0:T(8,128)(2,1)S(1)}, u32[]{:S(2)}, u32[]{:S(2)}) collective-permute-start(bf16[2,256,768]{2,1,0:T(8,128)(2,1)S(1)} %fusion.2.own_ref), channel_id=1, source_target_pairs={{2,1},{4,3},{6,5},{10,9},{12,11},{14,13},{18,17},{20,19},{22,21},{... | collective-permute-start | bytes 2359304 | tf_op jit(solution)/shard_map/ppermute | solution.py:22
  6.7 0.1 pad_add_fusion.where_ref
  6.8 0.0 collective-permute-done.next_ref
  6.8 1.2 %shard_map.64.refs_0_ = bf16[2,256,256]{2,1,0:T(8,128)(2,1)S(1)} custom-call(s32[3]{0:T(128)S(1)} %pad_add_fusion.where_ref, s32[2]{0:T(128)S(1)} %broadcast_subtract_fusion.rows_ref, s32[2]{0:T(128)S(1)} %copy-done.3, bf16[2,256,768]{2,1,0:T(8,128)(2,1)S(1)} %fusion.2.own_ref, bf16[2,256,768]{2,1,0:T(8,128)(2,1)} %collective-permute-done.next_ref, ...), custom_call_target="tpu_custom_call" | custom-call | tf_op jit(solution)/shard_map/pallas_call | solution.py:159
  8.0 1.2 %shard_map.65.block_ref.refs_0_ = bf16[2,256,256]{2,1,0:T(8,128)(2,1)S(1)} custom-call(s32[3]{0:T(128)S(1)} %pad_add_fusion.where_ref, s32[2]{0:T(128)S(1)} %broadcast_subtract_fusion.rows_ref, s32[2]{0:T(128)S(1)} %copy-done.3, bf16[2,256,768]{2,1,0:T(8,128)(2,1)S(1)} %fusion.2.own_ref, bf16[2,256,768]{2,1,0:T(8,128)(2,1)} %collective-permute-done.next_ref, ...), custom_call_target="tpu_custom_call" | custom-call | tf_op jit(solution)/shard_map/pallas_call | solution.py:159
  9.2 9.5 %collective-permute-done.4.next_ref = bf16[2,256,768]{2,1,0:T(8,128)(2,1)S(1)} collective-permute-done((bf16[2,256,768]{2,1,0:T(8,128)(2,1)S(1)}, bf16[2,256,768]{2,1,0:T(8,128)(2,1)S(1)}, u32[]{:S(2)}, u32[]{:S(2)}) %collective-permute-start.4) | collective-permute-done | bytes 786464 | tf_op jit(solution)/shard_map/ppermute | solution.py:22
  18.7 0.9 %shard_map.67.refs_0_.refs_4_ = bf16[2,256,256]{2,1,0:T(8,128)(2,1)S(1)} custom-call(s32[3]{0:T(128)S(1)} %pad_add_fusion.where_ref, s32[2]{0:T(128)S(1)} %broadcast_subtract_fusion.rows_ref, s32[2]{0:T(128)S(1)} %copy-done.3, bf16[2,256,768]{2,1,0:T(8,128)(2,1)S(1)} %fusion.2.own_ref, bf16[2,256,768]{2,1,0:T(8,128)(2,1)S(1)} %collective-permute-done.4.next_ref, ...), custom_call_target="tpu_custom_call" | custom-call | tf_op jit(solution)/shard_map/pallas_call | solution.py:159
  19.6 3.1 %collective-permute-start.11 = (bf16[2,256,256]{2,1,0:T(8,128)(2,1)S(1)}, bf16[2,256,256]{2,1,0:T(8,128)(2,1)S(1)}, u32[]{:S(2)}, u32[]{:S(2)}) collective-permute-start(bf16[2,256,256]{2,1,0:T(8,128)(2,1)S(1)} %shard_map.67.refs_0_.refs_4_), channel_id=1, source_target_pairs={{1,9},{3,11},{5,13},{7,15},{17,25},{19,27},{21,29},{23,31}} | collective-permute-start | bytes 786440 | tf_op jit(solution)/shard_map/ppermute | solution.py:28
  22.8 1.3 %collective-permute-start.12 = (bf16[2,256,256]{2,1,0:T(8,128)(2,1)S(1)}, bf16[2,256,256]{2,1,0:T(8,128)(2,1)S(1)}, u32[]{:S(2)}, u32[]{:S(2)}) collective-permute-start(bf16[2,256,256]{2,1,0:T(8,128)(2,1)S(1)} %shard_map.67.refs_0_.refs_4_), channel_id=1, source_target_pairs={{1,17},{3,19},{5,21},{7,23},{9,25},{11,27},{13,29},{15,31}} | collective-permute-start | bytes 786440 | tf_op jit(solution)/shard_map/ppermute | solution.py:28
  24.1 1.3 %collective-permute-start.13 = (bf16[2,256,256]{2,1,0:T(8,128)(2,1)S(1)}, bf16[2,256,256]{2,1,0:T(8,128)(2,1)S(1)}, u32[]{:S(2)}, u32[]{:S(2)}) collective-permute-start(bf16[2,256,256]{2,1,0:T(8,128)(2,1)S(1)} %shard_map.67.refs_0_.refs_4_), channel_id=1, source_target_pairs={{1,25},{3,27},{5,29},{7,31},{9,17},{11,19},{13,21},{15,23}} | collective-permute-start | bytes 786440 | tf_op jit(solution)/shard_map/ppermute | solution.py:28
  25.4 0.7 %collective-permute-start.10 = (bf16[2,256,256]{2,1,0:T(8,128)(2,1)S(1)}, bf16[2,256,256]{2,1,0:T(8,128)(2,1)S(1)}, u32[]{:S(2)}, u32[]{:S(2)}) collective-permute-start(bf16[2,256,256]{2,1,0:T(8,128)(2,1)S(1)} %shard_map.64.refs_0_), channel_id=1, source_target_pairs={{0,24},{2,26},{4,28},{6,30},{8,16},{10,18},{12,20},{14,22}} | collective-permute-start | bytes 786440 | tf_op jit(solution)/shard_map/ppermute | solution.py:28
  26.1 0.7 %collective-permute-start.8 = (bf16[2,256,256]{2,1,0:T(8,128)(2,1)S(1)}, bf16[2,256,256]{2,1,0:T(8,128)(2,1)S(1)}, u32[]{:S(2)}, u32[]{:S(2)}) collective-permute-start(bf16[2,256,256]{2,1,0:T(8,128)(2,1)S(1)} %shard_map.64.refs_0_), channel_id=1, source_target_pairs={{0,8},{2,10},{4,12},{6,14},{16,24},{18,26},{20,28},{22,30}} | collective-permute-start | bytes 786440 | tf_op jit(solution)/shard_map/ppermute | solution.py:28
  26.7 0.9 %shard_map.68.refs_4_ = bf16[2,256,256]{2,1,0:T(8,128)(2,1)S(1)} custom-call(s32[3]{0:T(128)S(1)} %pad_add_fusion.where_ref, s32[2]{0:T(128)S(1)} %broadcast_subtract_fusion.rows_ref, s32[2]{0:T(128)S(1)} %copy-done.3, bf16[2,256,768]{2,1,0:T(8,128)(2,1)S(1)} %fusion.2.own_ref, bf16[2,256,768]{2,1,0:T(8,128)(2,1)S(1)} %collective-permute-done.4.next_ref, ...), custom_call_target="tpu_custom_call" | custom-call | tf_op jit(solution)/shard_map/pallas_call | solution.py:159
  27.7 0.0 collective-permute-done.11.refs_5_
  27.7 0.7 %collective-permute-start.9 = (bf16[2,256,256]{2,1,0:T(8,128)(2,1)S(1)}, bf16[2,256,256]{2,1,0:T(8,128)(2,1)S(1)}, u32[]{:S(2)}, u32[]{:S(2)}) collective-permute-start(bf16[2,256,256]{2,1,0:T(8,128)(2,1)S(1)} %shard_map.64.refs_0_), channel_id=1, source_target_pairs={{0,16},{2,18},{4,20},{6,22},{8,24},{10,26},{12,28},{14,30}} | collective-permute-start | bytes 786440 | tf_op jit(solution)/shard_map/ppermute | solution.py:28
  28.4 7.9 %collective-permute-done.12.refs_6_ = bf16[2,256,256]{2,1,0:T(8,128)(2,1)S(1)} collective-permute-done((bf16[2,256,256]{2,1,0:T(8,128)(2,1)S(1)}, bf16[2,256,256]{2,1,0:T(8,128)(2,1)S(1)}, u32[]{:S(2)}, u32[]{:S(2)}) %collective-permute-start.12) | collective-permute-done | bytes 262176 | tf_op jit(solution)/shard_map/ppermute | solution.py:28
  36.2 2.1 %collective-permute-start.5 = (bf16[2,256,256]{2,1,0:T(8,128)(2,1)S(1)}, bf16[2,256,256]{2,1,0:T(8,128)(2,1)S(1)}, u32[]{:S(2)}, u32[]{:S(2)}) collective-permute-start(bf16[2,256,256]{2,1,0:T(8,128)(2,1)S(1)} %shard_map.68.refs_4_), channel_id=1, source_target_pairs={{1,9},{3,11},{5,13},{7,15},{17,25},{19,27},{21,29},{23,31}} | collective-permute-start | bytes 786440 | tf_op jit(solution)/shard_map/ppermute | solution.py:28
  38.3 0.0 collective-permute-done.13.refs_7_
  38.4 1.3 %collective-permute-start.6 = (bf16[2,256,256]{2,1,0:T(8,128)(2,1)S(1)}, bf16[2,256,256]{2,1,0:T(8,128)(2,1)S(1)}, u32[]{:S(2)}, u32[]{:S(2)}) collective-permute-start(bf16[2,256,256]{2,1,0:T(8,128)(2,1)S(1)} %shard_map.68.refs_4_), channel_id=1, source_target_pairs={{1,17},{3,19},{5,21},{7,23},{9,25},{11,27},{13,29},{15,31}} | collective-permute-start | bytes 786440 | tf_op jit(solution)/shard_map/ppermute | solution.py:28
  39.7 1.3 %collective-permute-start.7 = (bf16[2,256,256]{2,1,0:T(8,128)(2,1)S(1)}, bf16[2,256,256]{2,1,0:T(8,128)(2,1)S(1)}, u32[]{:S(2)}, u32[]{:S(2)}) collective-permute-start(bf16[2,256,256]{2,1,0:T(8,128)(2,1)S(1)} %shard_map.68.refs_4_), channel_id=1, source_target_pairs={{1,25},{3,27},{5,29},{7,31},{9,17},{11,19},{13,21},{15,23}} | collective-permute-start | bytes 786440 | tf_op jit(solution)/shard_map/ppermute | solution.py:28
  41.0 0.7 %collective-permute-start.1 = (bf16[2,256,256]{2,1,0:T(8,128)(2,1)S(1)}, bf16[2,256,256]{2,1,0:T(8,128)(2,1)S(1)}, u32[]{:S(2)}, u32[]{:S(2)}) collective-permute-start(bf16[2,256,256]{2,1,0:T(8,128)(2,1)S(1)} %shard_map.65.block_ref.refs_0_), channel_id=1, source_target_pairs={{0,8},{2,10},{4,12},{6,14},{16,24},{18,26},{20,28},{22,30}} | collective-permute-start | bytes 786440 | tf_op jit(solution)/shard_map/ppermute | solution.py:28
  41.7 0.0 collective-permute-done.9.refs_2_
  41.7 0.7 %collective-permute-start.2 = (bf16[2,256,256]{2,1,0:T(8,128)(2,1)S(1)}, bf16[2,256,256]{2,1,0:T(8,128)(2,1)S(1)}, u32[]{:S(2)}, u32[]{:S(2)}) collective-permute-start(bf16[2,256,256]{2,1,0:T(8,128)(2,1)S(1)} %shard_map.65.block_ref.refs_0_), channel_id=1, source_target_pairs={{0,16},{2,18},{4,20},{6,22},{8,24},{10,26},{12,28},{14,30}} | collective-permute-start | bytes 786440 | tf_op jit(solution)/shard_map/ppermute | solution.py:28
  42.4 0.7 %collective-permute-start.3 = (bf16[2,256,256]{2,1,0:T(8,128)(2,1)S(1)}, bf16[2,256,256]{2,1,0:T(8,128)(2,1)S(1)}, u32[]{:S(2)}, u32[]{:S(2)}) collective-permute-start(bf16[2,256,256]{2,1,0:T(8,128)(2,1)S(1)} %shard_map.65.block_ref.refs_0_), channel_id=1, source_target_pairs={{0,24},{2,26},{4,28},{6,30},{8,16},{10,18},{12,20},{14,22}} | collective-permute-start | bytes 786440 | tf_op jit(solution)/shard_map/ppermute | solution.py:28
  43.0 3.8 %shard_map.69.refs_8_ = bf16[1,2,256,256]{3,2,1,0:T(8,128)(2,1)S(1)} custom-call(s32[3]{0:T(128)S(1)} %pad_add_fusion.where_ref, bf16[2,512,256]{2,1,0:T(8,128)(2,1)S(1)} %copy-done, bf16[2,256,512]{2,1,0:T(8,128)(2,1)S(1)} %copy-done.1, bf16[2,256,256]{2,1,0:T(8,128)(2,1)S(1)} %shard_map.64.refs_0_, ...), custom_call_target="tpu_custom_call" | custom-call | tf_op jit(solution)/shard_map/pallas_call | solution.py:202
  46.9 6.7 %collective-permute-done.6.refs_6_ = bf16[2,256,256]{2,1,0:T(8,128)(2,1)S(1)} collective-permute-done((bf16[2,256,256]{2,1,0:T(8,128)(2,1)S(1)}, bf16[2,256,256]{2,1,0:T(8,128)(2,1)S(1)}, u32[]{:S(2)}, u32[]{:S(2)}) %collective-permute-start.6) | collective-permute-done | bytes 262176 | tf_op jit(solution)/shard_map/ppermute | solution.py:28
  53.5 0.0 collective-permute-done.7.refs_7_
  53.6 0.0 collective-permute-done.1.refs_1_
  53.6 0.0 collective-permute-done.2.refs_2_
  53.6 4.6 %shard_map.70 = bf16[2,2,256,256]{3,2,1,0:T(8,128)(2,1)} custom-call(s32[3]{0:T(128)S(1)} %pad_add_fusion.where_ref, bf16[2,512,256]{2,1,0:T(8,128)(2,1)S(1)} %copy-done, bf16[2,256,512]{2,1,0:T(8,128)(2,1)S(1)} %copy-done.1, bf16[2,256,256]{2,1,0:T(8,128)(2,1)S(1)} %shard_map.65.block_ref.refs_0_, bf16[2,256,256]{2,1,0:T(8,128)(2,1)S(1)} %collective-permute-done.1.refs_1_, ...), custom_call_target="tpu_custom_call" | custom-call | tf_op jit(solution)/shard_map/pallas_call | solution.py:202
  (16 shorter events, 0.0 us)
Async XLA Ops:
  0.0 6.8 %copy-start = (bf16[2,512,256]{2,1,0:T(8,128)(2,1)S(1)}, bf16[2,512,256]{2,1,0:T(8,128)(2,1)}, u32[]{:S(2)}) copy-start(bf16[2,512,256]{2,1,0:T(8,128)(2,1)} %constant.22.clone.right_ref) | copy-start | bytes 1572868
  0.0 6.8 %copy-start.1 = (bf16[2,256,512]{2,1,0:T(8,128)(2,1)S(1)}, bf16[2,256,512]{2,1,0:T(8,128)(2,1)}, u32[]{:S(2)}) copy-start(bf16[2,256,512]{2,1,0:T(8,128)(2,1)} %constant.23.clone.left_ref) | copy-start | bytes 1572868
  0.0 6.8 %copy-start.4 = (s32[2]{0:T(128)S(1)}, s32[2]{0:T(128)}, u32[]{:S(2)}) copy-start(s32[2]{0:T(128)} %param.8) | copy-start | bytes 28
  0.0 6.8 %copy-start.2 = (f32[2,256,256]{2,1,0:T(8,128)S(1)}, f32[2,256,256]{2,1,0:T(8,128)}, u32[]{:S(2)}) copy-start(f32[2,256,256]{2,1,0:T(8,128)} %probe_ref.7) | copy-start | bytes 1572868
  0.0 6.8 %copy-start.3 = (s32[2]{0:T(128)S(1)}, s32[2]{0:T(128)}, u32[]{:S(2)}) copy-start(s32[2]{0:T(128)} %cols_ref.7) | copy-start | bytes 28
  1.9 4.9 %collective-permute-start = (bf16[2,256,768]{2,1,0:T(8,128)(2,1)S(1)}, bf16[2,256,768]{2,1,0:T(8,128)(2,1)}, u32[]{:S(2)}, u32[]{:S(2)}) collective-permute-start(bf16[2,256,768]{2,1,0:T(8,128)(2,1)S(1)} %fusion.2.own_ref), channel_id=1, source_target_pairs={{1,0},{3,2},{5,4},{7,6},{9,8},{11,10},{13,12},{15,14},{17,16},{19,... | collective-permute-start | bytes 2359304 | tf_op jit(solution)/shard_map/ppermute | solution.py:22
  5.4 13.3 %collective-permute-start.4 = (bf16[2,256,768]{2,1,0:T(8,128)(2,1)S(1)}, bf16[2,256,768]{2,1,0:T(8,128)(2,1)S(1)}, u32[]{:S(2)}, u32[]{:S(2)}) collective-permute-start(bf16[2,256,768]{2,1,0:T(8,128)(2,1)S(1)} %fusion.2.own_ref), channel_id=1, source_target_pairs={{2,1},{4,3},{6,5},{10,9},{12,11},{14,13},{18,17},{20,19},{22,21},{... | collective-permute-start | bytes 2359304 | tf_op jit(solution)/shard_map/ppermute | solution.py:22
  19.6 8.1 %collective-permute-start.11 = (bf16[2,256,256]{2,1,0:T(8,128)(2,1)S(1)}, bf16[2,256,256]{2,1,0:T(8,128)(2,1)S(1)}, u32[]{:S(2)}, u32[]{:S(2)}) collective-permute-start(bf16[2,256,256]{2,1,0:T(8,128)(2,1)S(1)} %shard_map.67.refs_0_.refs_4_), channel_id=1, source_target_pairs={{1,9},{3,11},{5,13},{7,15},{17,25},{19,27},{21,29},{23,31}} | collective-permute-start | bytes 786440 | tf_op jit(solution)/shard_map/ppermute | solution.py:28
  22.8 13.5 %collective-permute-start.12 = (bf16[2,256,256]{2,1,0:T(8,128)(2,1)S(1)}, bf16[2,256,256]{2,1,0:T(8,128)(2,1)S(1)}, u32[]{:S(2)}, u32[]{:S(2)}) collective-permute-start(bf16[2,256,256]{2,1,0:T(8,128)(2,1)S(1)} %shard_map.67.refs_0_.refs_4_), channel_id=1, source_target_pairs={{1,17},{3,19},{5,21},{7,23},{9,25},{11,27},{13,29},{15,31}} | collective-permute-start | bytes 786440 | tf_op jit(solution)/shard_map/ppermute | solution.py:28
  24.1 14.3 %collective-permute-start.13 = (bf16[2,256,256]{2,1,0:T(8,128)(2,1)S(1)}, bf16[2,256,256]{2,1,0:T(8,128)(2,1)S(1)}, u32[]{:S(2)}, u32[]{:S(2)}) collective-permute-start(bf16[2,256,256]{2,1,0:T(8,128)(2,1)S(1)} %shard_map.67.refs_0_.refs_4_), channel_id=1, source_target_pairs={{1,25},{3,27},{5,29},{7,31},{9,17},{11,19},{13,21},{15,23}} | collective-permute-start | bytes 786440 | tf_op jit(solution)/shard_map/ppermute | solution.py:28
  25.4 14.3 %collective-permute-start.10 = (bf16[2,256,256]{2,1,0:T(8,128)(2,1)S(1)}, bf16[2,256,256]{2,1,0:T(8,128)(2,1)S(1)}, u32[]{:S(2)}, u32[]{:S(2)}) collective-permute-start(bf16[2,256,256]{2,1,0:T(8,128)(2,1)S(1)} %shard_map.64.refs_0_), channel_id=1, source_target_pairs={{0,24},{2,26},{4,28},{6,30},{8,16},{10,18},{12,20},{14,22}} | collective-permute-start | bytes 786440 | tf_op jit(solution)/shard_map/ppermute | solution.py:28
  26.1 14.9 %collective-permute-start.8 = (bf16[2,256,256]{2,1,0:T(8,128)(2,1)S(1)}, bf16[2,256,256]{2,1,0:T(8,128)(2,1)S(1)}, u32[]{:S(2)}, u32[]{:S(2)}) collective-permute-start(bf16[2,256,256]{2,1,0:T(8,128)(2,1)S(1)} %shard_map.64.refs_0_), channel_id=1, source_target_pairs={{0,8},{2,10},{4,12},{6,14},{16,24},{18,26},{20,28},{22,30}} | collective-permute-start | bytes 786440 | tf_op jit(solution)/shard_map/ppermute | solution.py:28
  27.7 14.0 %collective-permute-start.9 = (bf16[2,256,256]{2,1,0:T(8,128)(2,1)S(1)}, bf16[2,256,256]{2,1,0:T(8,128)(2,1)S(1)}, u32[]{:S(2)}, u32[]{:S(2)}) collective-permute-start(bf16[2,256,256]{2,1,0:T(8,128)(2,1)S(1)} %shard_map.64.refs_0_), channel_id=1, source_target_pairs={{0,16},{2,18},{4,20},{6,22},{8,24},{10,26},{12,28},{14,30}} | collective-permute-start | bytes 786440 | tf_op jit(solution)/shard_map/ppermute | solution.py:28
  36.2 6.1 %collective-permute-start.5 = (bf16[2,256,256]{2,1,0:T(8,128)(2,1)S(1)}, bf16[2,256,256]{2,1,0:T(8,128)(2,1)S(1)}, u32[]{:S(2)}, u32[]{:S(2)}) collective-permute-start(bf16[2,256,256]{2,1,0:T(8,128)(2,1)S(1)} %shard_map.68.refs_4_), channel_id=1, source_target_pairs={{1,9},{3,11},{5,13},{7,15},{17,25},{19,27},{21,29},{23,31}} | collective-permute-start | bytes 786440 | tf_op jit(solution)/shard_map/ppermute | solution.py:28
  38.4 15.2 %collective-permute-start.6 = (bf16[2,256,256]{2,1,0:T(8,128)(2,1)S(1)}, bf16[2,256,256]{2,1,0:T(8,128)(2,1)S(1)}, u32[]{:S(2)}, u32[]{:S(2)}) collective-permute-start(bf16[2,256,256]{2,1,0:T(8,128)(2,1)S(1)} %shard_map.68.refs_4_), channel_id=1, source_target_pairs={{1,17},{3,19},{5,21},{7,23},{9,25},{11,27},{13,29},{15,31}} | collective-permute-start | bytes 786440 | tf_op jit(solution)/shard_map/ppermute | solution.py:28
  39.7 13.9 %collective-permute-start.7 = (bf16[2,256,256]{2,1,0:T(8,128)(2,1)S(1)}, bf16[2,256,256]{2,1,0:T(8,128)(2,1)S(1)}, u32[]{:S(2)}, u32[]{:S(2)}) collective-permute-start(bf16[2,256,256]{2,1,0:T(8,128)(2,1)S(1)} %shard_map.68.refs_4_), channel_id=1, source_target_pairs={{1,25},{3,27},{5,29},{7,31},{9,17},{11,19},{13,21},{15,23}} | collective-permute-start | bytes 786440 | tf_op jit(solution)/shard_map/ppermute | solution.py:28
  41.0 12.6 %collective-permute-start.1 = (bf16[2,256,256]{2,1,0:T(8,128)(2,1)S(1)}, bf16[2,256,256]{2,1,0:T(8,128)(2,1)S(1)}, u32[]{:S(2)}, u32[]{:S(2)}) collective-permute-start(bf16[2,256,256]{2,1,0:T(8,128)(2,1)S(1)} %shard_map.65.block_ref.refs_0_), channel_id=1, source_target_pairs={{0,8},{2,10},{4,12},{6,14},{16,24},{18,26},{20,28},{22,30}} | collective-permute-start | bytes 786440 | tf_op jit(solution)/shard_map/ppermute | solution.py:28
  41.7 11.9 %collective-permute-start.2 = (bf16[2,256,256]{2,1,0:T(8,128)(2,1)S(1)}, bf16[2,256,256]{2,1,0:T(8,128)(2,1)S(1)}, u32[]{:S(2)}, u32[]{:S(2)}) collective-permute-start(bf16[2,256,256]{2,1,0:T(8,128)(2,1)S(1)} %shard_map.65.block_ref.refs_0_), channel_id=1, source_target_pairs={{0,16},{2,18},{4,20},{6,22},{8,24},{10,26},{12,28},{14,30}} | collective-permute-start | bytes 786440 | tf_op jit(solution)/shard_map/ppermute | solution.py:28
  42.4 11.2 %collective-permute-start.3 = (bf16[2,256,256]{2,1,0:T(8,128)(2,1)S(1)}, bf16[2,256,256]{2,1,0:T(8,128)(2,1)S(1)}, u32[]{:S(2)}, u32[]{:S(2)}) collective-permute-start(bf16[2,256,256]{2,1,0:T(8,128)(2,1)S(1)} %shard_map.65.block_ref.refs_0_), channel_id=1, source_target_pairs={{0,24},{2,26},{4,28},{6,30},{8,16},{10,18},{12,20},{14,22}} | collective-permute-start | bytes 786440 | tf_op jit(solution)/shard_map/ppermute | solution.py:28

commit v3 on v2

v3 whole, which is shorter than its diff:
```python
import functools
import math

import numpy as np
import jax
import jax.numpy as jnp
from jax import lax
from jax.experimental import pallas as pl
from jax.experimental.pallas import tpu as pltpu
from jax.sharding import PartitionSpec as P


CHIRP = 40.0
F32 = jnp.float32
BF16 = jnp.bfloat16
OCTAVES = 120.0
ROOM = 8 * 2**20


def handed_down(block, parity):
    strips = lax.axis_size("probe")
    return lax.ppermute(block, "probe", [(i + 1, i) for i in range(parity, strips - 1, 2)])


def sent_on(block, parities, pairs):
    strips = lax.axis_size("probe")
    route = [(a * strips + p, b * strips + p) for a, b in pairs for p in range(strips) if p % 2 in parities]
    return lax.ppermute(block, ("depth", "probe"), route)


def operator_tables(size):
    k = np.arange(size)
    freq = np.where(k < size // 2, k, k - size) / size
    taps = np.fft.ifft(np.exp(-1j * CHIRP * freq * freq))
    half = size // 2
    lag = (np.arange(half)[:, None] - np.arange(half)[None, :]) % size
    right, left = [], []
    for sign in (1.0, -1.0):
        part = 0.5 * (taps[lag] + sign * taps[(lag + half) % size])
        full = np.block([[part.real, part.imag], [-part.imag, part.real]]).astype(np.float32)
        high = full.astype(BF16)
        low = (full - high.astype(np.float32)).astype(BF16)
        right.append(np.concatenate([high, low], axis=0))
        left.append(np.concatenate([high.T, low.T], axis=1))
    return [jnp.asarray(np.stack(right)), jnp.asarray(np.stack(left))]


def fit(function, powers, reach):
    x = np.cos(np.pi * (np.arange(400) + 0.5) / 400) * reach
    basis = np.stack([(x / reach) ** p for p in powers], axis=1)
    found = np.linalg.lstsq(basis, function(x), rcond=None)[0]
    return [float(c / reach**p) for c, p in zip(found, powers)]


REACH = 0.5 * OCTAVES * math.log(2.0)


def half_angle(position):
    return position * (0.5 * math.pi / REACH)


SIN_FIT = fit(lambda y: math.sqrt(2.0) * np.sin(half_angle(y)), (1, 3, 5, 7), REACH)
COS_FIT = fit(lambda y: math.sqrt(2.0) * np.cos(half_angle(y)), (0, 2, 4, 6), REACH)


def horner(square, coefficients):
    value = coefficients[-1]
    for c in coefficients[-2::-1]:
        value = value * square + c
    return value


def phase_factor(code):
    position = jnp.log(code)
    square = position * position
    sine = position * horner(square, SIN_FIT)
    cosine = horner(square, COS_FIT)
    return 1.0 - sine * sine, sine * cosine


def coded(phase):
    turns = phase * (0.5 / math.pi)
    return jnp.exp2(OCTAVES * (turns - jnp.round(turns))).astype(BF16)


SMEM = pl.BlockSpec(memory_space=pltpu.SMEM)
VMEM = pl.BlockSpec(memory_space=pltpu.VMEM)


def product(a, b):
    return jnp.dot(a, b, preferred_element_type=F32)


def propagated(real, imag, right_ref, left_ref):
    size = real.shape[-1]
    half = size // 2

    def right(k, combine):
        data = jnp.concatenate([combine(real[:, :half], real[:, half:]), combine(imag[:, :half], imag[:, half:])], axis=1).astype(BF16)
        return product(data, right_ref[k, :size]) + product(data, right_ref[k, size:])

    plus, minus = right(0, jnp.add), right(1, jnp.subtract)
    re = jnp.concatenate([plus[:, :half], minus[:, :half]], axis=1)
    im = jnp.concatenate([plus[:, half:], minus[:, half:]], axis=1)

    def left(k, combine):
        data = jnp.concatenate([combine(re[:half], re[half:]), combine(im[:half], im[half:])], axis=0).astype(BF16)
        return product(left_ref[k, :, :size], data) + product(left_ref[k, :, size:], data)

    top, low = left(0, jnp.add), left(1, jnp.subtract)
    re = jnp.concatenate([top[:half] + low[:half], top[:half] - low[:half]], axis=0)
    im = jnp.concatenate([top[half:] + low[half:], top[half:] - low[half:]], axis=0)
    real = jnp.concatenate([re[:, :half] + re[:, half:], re[:, :half] - re[:, half:]], axis=1)
    imag = jnp.concatenate([im[:, :half] + im[:, half:], im[:, :half] - im[:, half:]], axis=1)
    return real, imag


def sliced(real, imag, code, right_ref, left_ref):
    cosine, sine = phase_factor(code.astype(F32))
    real, imag = cosine * real - sine * imag, cosine * imag + sine * real
    return propagated(real, imag, right_ref, left_ref)


def first_kernel(count, parity, starts_ref, own_ref, next_ref, probe_ref, right_ref, left_ref, *refs):
    outs, scratch = refs[-1 - count : -1], refs[-1]
    layers, strip, width = own_ref.shape
    size = outs[0].shape[-1]
    span = size + 128
    place = lax.axis_index("probe")

    @pl.when(place % 2 == parity)
    def _():
        edge = (place == lax.axis_size("probe") - 1).astype(F32)
        line = lax.broadcasted_iota(jnp.int32, (strip, span), 0)
        for j, out in enumerate(outs):
            r = starts_ref[j, 0]
            c = starts_ref[j, 1]
            base = jnp.minimum(c // 128, (width - span) // 128)
            shift = c - base * 128
            lanes = pl.ds(pl.multiple_of(base * 128, 128), span)
            for s in range(layers):
                own = own_ref[s, :, lanes].astype(F32)
                following = next_ref[s, :, lanes].astype(F32) + edge
                merged = jnp.where(line >= r, own, following)
                turned = pltpu.roll(merged, span - shift, 1)[:, :size]
                for part in range(size // 128):
                    columns = turned[:, part * 128 : (part + 1) * 128]
                    scratch[part, pl.ds(0, strip), :] = columns
                    scratch[part, pl.ds(strip, strip), :] = columns
                    out[s, :, part * 128 : (part + 1) * 128] = scratch[part, pl.ds(r, size), :].astype(BF16)

        @pl.when(lax.axis_index("depth") == 0)
        def _():
            waves = [(probe_ref[0], probe_ref[1])] * count
            for s in range(layers):
                waves = [sliced(*wave, out[s], right_ref, left_ref) for wave, out in zip(waves, outs)]
            for (real, imag), out in zip(waves, outs):
                out[0] = real.astype(BF16)
                out[1] = imag.astype(BF16)


def first_group(parity, starts, own, following, probe, tables, after):
    layers, strip, _ = own.shape
    size = probe.shape[-1]
    count = starts.shape[0]
    return pl.pallas_call(
        functools.partial(first_kernel, count, parity),
        out_shape=[jax.ShapeDtypeStruct((layers, size, size), BF16)] * count,
        in_specs=[SMEM] + [VMEM] * (5 + len(after)),
        out_specs=[VMEM] * count,
        scratch_shapes=[pltpu.VMEM((size // 128, 2 * strip, 128), F32)],
        compiler_params=pltpu.CompilerParams(vmem_limit_bytes=ROOM),
    )(starts, own, following, probe, *tables, *after)


def through_groups(wave_ref, first, groups, block, layers, right_ref, left_ref):
    group = lax.axis_index("depth")
    for g in range(first, groups):

        @pl.when(g <= group)
        def _():
            real, imag = wave_ref[0].astype(F32), wave_ref[1].astype(F32)
            for s in range(layers):
                real, imag = sliced(real, imag, block(g, s), right_ref, left_ref)
            wave_ref[0] = real.astype(BF16)
            wave_ref[1] = imag.astype(BF16)


def chain_kernel(groups, distances, before, starting, right_ref, left_ref, *refs):
    some = len(distances)
    arrived = tuple(dict(zip(distances, refs[k * some : (k + 1) * some])) for k in range(2))
    more = refs[2 * some :]
    out_ref, wave_ref = refs[-2], refs[-1]
    group = lax.axis_index("depth")
    even = lax.axis_index("probe") % 2 == 0

    def block(g, s):
        value = None
        for m in sorted({g ^ own for own in range(g, groups)}):
            this = jnp.where(even, arrived[0][m][s], arrived[1][m][s])
            value = this if value is None else jnp.where(group ^ g == m, this, value)
        return value

    for s in range(2):
        if starting:
            value = jnp.where(even, arrived[0][0][s], arrived[1][0][s])
            for k in range(starting):
                value = jnp.where(group == k + 1, more[k][s], value)
            wave_ref[s] = value
        else:
            wave_ref[s] = block(0, s)
    through_groups(wave_ref, 2 if starting else 1, groups, block, arrived[0][0].shape[0], right_ref, left_ref)
    out_ref[before] = wave_ref[...]
    for j in range(before):
        out_ref[j] = more[starting + j][0]


def chain(groups, tables, even, odd, starting, finished):
    distances = sorted(even)
    shape = (2, *even[0].shape[1:])
    arguments = [*tables, *(even[m] for m in distances), *(odd[m] for m in distances), *starting, *finished]
    return pl.pallas_call(
        functools.partial(chain_kernel, groups, distances, len(finished), len(starting)),
        out_shape=jax.ShapeDtypeStruct((len(finished) + 1, *shape), BF16),
        in_specs=[VMEM] * len(arguments),
        out_specs=VMEM,
        scratch_shapes=[pltpu.VMEM(shape, BF16)],
        compiler_params=pltpu.CompilerParams(vmem_limit_bytes=ROOM),
    )(*arguments)


def second_kernel(right_ref, left_ref, even_own_ref, even_near_ref, odd_own_ref, odd_near_ref, out_ref):
    even = lax.axis_index("probe") % 2 == 0

    @pl.when(lax.axis_index("depth") == 1)
    def _():
        real, imag = [jnp.where(even, even_near_ref[s], odd_near_ref[s]).astype(F32) for s in range(2)]
        for s in range(even_own_ref.shape[0]):
            real, imag = sliced(real, imag, jnp.where(even, even_own_ref[s], odd_own_ref[s]), right_ref, left_ref)
        out_ref[0] = real.astype(BF16)
        out_ref[1] = imag.astype(BF16)


def second_group(tables, even, odd):
    arguments = [*tables, even[0], even[1], odd[0], odd[1]]
    return pl.pallas_call(
        second_kernel,
        out_shape=jax.ShapeDtypeStruct((2, *even[0].shape[1:]), BF16),
        in_specs=[VMEM] * len(arguments),
        out_specs=VMEM,
        compiler_params=pltpu.CompilerParams(vmem_limit_bytes=ROOM),
    )(*arguments)


def mark_kernel(block_ref, out_ref):
    out_ref[...] = block_ref[0, :16, :128]


def mark(block):
    return pl.pallas_call(
        mark_kernel,
        out_shape=jax.ShapeDtypeStruct((16, 128), BF16),
        in_specs=[VMEM],
        out_specs=VMEM,
        compiler_params=pltpu.CompilerParams(vmem_limit_bytes=ROOM),
    )(block)


def hops(groups, count):
    return [(j, m) for j in range(count) for m in range(1, 2 if groups == 4 else groups)]


def body(probe, phase, row_offsets, col_offsets):
    size = probe.shape[-1]
    strip = phase.shape[1]
    count = row_offsets.shape[0]
    groups = lax.axis_size("depth")
    starts = jnp.stack([row_offsets - lax.axis_index("probe") * strip, col_offsets], axis=1)
    tables = operator_tables(size)
    own = coded(phase)
    following = {}
    for parity in (1, 0):
        following[parity] = handed_down(own, parity)
    arrived = {}
    after = []
    for parity in (0, 1):
        firsts = first_group(parity, starts, own, following[parity], probe, tables, after)
        blocks = [{0: first} for first in firsts]
        for j, m in hops(groups, count):
            blocks[j][m] = sent_on(firsts[j], (parity,), [(i, i ^ m) for i in range(groups) if i < i ^ m < groups])
        if parity == 0:
            after = [mark(firsts[-1])]
        arrived[parity] = blocks
    starting = [[] for _ in range(count)]
    if groups == 4:
        for j in range(count):
            starting[j].append(second_group(tables, arrived[0][j], arrived[1][j]))
        for target in (2, 3):
            for j in range(count):
                starting[j].append(sent_on(starting[j][0], (0, 1), [(1, target)]))
    finished = []
    for j in range(count):
        wave = chain(groups, tables, arrived[0][j], arrived[1][j], starting[j], finished if j == count - 1 else [])
        finished.append(wave)
    return wave[None]


def solution(mesh):
    return jax.shard_map(
        body,
        mesh=mesh,
        in_specs=(P(), P("depth", "probe", None), P("probe"), P("probe")),
        out_specs=P("depth", "probe", None, None, None),
        check_vma=False,
    )
```

time: 58.6 us -> 49.8 us (0.85)
  the two profiles are of different devices: /device:TPU:21 before, /device:TPU:23 now
where the time goes in v3:
time: 49.8 us; the launch traced here: 49.5 us
  waiting for transfers between devices  25.2 us (51%)
  starting transfers between devices  12.6 us (25%)
  Pallas kernels  9.35 us (19%)
  other arithmetic  1.95 us (4%)
    ppermute x8, waiting for transfers between devices, sent_on(): return lax.ppermute(block, ('depth', 'probe'), route)  14.6 us
    ppermute x2, waiting for transfers between devices, handed_down(): lax.ppermute(block, 'probe', [(i + 1, i) for i in range(parity, strips -...  10.5 us
    ppermute x8, starting transfers between devices, sent_on(): return lax.ppermute(block, ('depth', 'probe'), route)  7.86 us
    pallas_call x2, Pallas kernels, chain(): pl.pallas_call(functools.partial(chain_kernel, groups, distances, len(fin...  6.97 us
    ppermute x2, starting transfers between devices, handed_down(): lax.ppermute(block, 'probe', [(i + 1, i) for i in range(parity, strips -...  4.77 us
    pallas_call x2, Pallas kernels, first_group(): pl.pallas_call(functools.partial(first_kernel, count, parity), out_shape=...  2.39 us
    convert_element_type x1, other arithmetic, coded(): return jnp.exp2(OCTAVES * (turns - jnp.round(turns))).astype(BF16)  1.87 us
  transfers between devices with their start and end apart: 10, of which 5 were waited for; matrix products, arithmetic and copies ran while one was open for 1% of the time, Pallas kernels for 9%

profile of v3, /device:TPU:23, one launch (start us, length us, event | category | flops | bytes accessed | tf_op | source)
XLA Modules:
  0.0 49.5 jit_solution(5170969004741098465)
XLA Ops:
  0.0 0.0 copy-start.4
  0.0 0.0 copy-start.2
  0.0 1.9 %fusion.2.own_ref = bf16[2,256,768]{2,1,0:T(8,128)(2,1)S(1)} fusion(f32[2,256,768]{2,1,0:T(8,128)} %param.7), kind=kLoop, calls=%fused_computation.3 | loop fusion | flops 1966080 | bytes 2359296 | tf_op jit(solution)/shard_map/convert_element_type | solution.py:83
  1.9 3.5 %collective-permute-start = (bf16[2,256,768]{2,1,0:T(8,128)(2,1)S(1)}, bf16[2,256,768]{2,1,0:T(8,128)(2,1)}, u32[]{:S(2)}, u32[]{:S(2)}) collective-permute-start(bf16[2,256,768]{2,1,0:T(8,128)(2,1)S(1)} %fusion.2.own_ref), channel_id=1, source_target_pairs={{1,0},{3,2},{5,4},{7,6},{9,8},{11,10},{13,12},{15,14},{17,16},{19,... | collective-permute-start | bytes 2359304 | tf_op jit(solution)/shard_map/ppermute | solution.py:22
  5.4 1.3 %collective-permute-start.2 = (bf16[2,256,768]{2,1,0:T(8,128)(2,1)S(1)}, bf16[2,256,768]{2,1,0:T(8,128)(2,1)S(1)}, u32[]{:S(2)}, u32[]{:S(2)}) collective-permute-start(bf16[2,256,768]{2,1,0:T(8,128)(2,1)S(1)} %fusion.2.own_ref), channel_id=1, source_target_pairs={{2,1},{4,3},{6,5},{10,9},{12,11},{14,13},{18,17},{20,19},{22,21},{... | collective-permute-start | bytes 2359304 | tf_op jit(solution)/shard_map/ppermute | solution.py:22
  6.7 0.0 copy-done.3
  6.7 0.1 copy.7
  6.8 0.1 copy.8
  6.9 0.1 pad_add_fusion.starts_ref
  7.0 0.0 collective-permute-done.next_ref
  7.0 0.0 copy-done
  7.0 1.2 %shard_map.64 = (bf16[2,256,256]{2,1,0:T(8,128)(2,1)S(1)}, bf16[2,256,256]{2,1,0:T(8,128)(2,1)S(1)}) custom-call(s32[2,2]{1,0:T(2,128)S(1)} %pad_add_fusion.starts_ref, bf16[2,256,768]{2,1,0:T(8,128)(2,1)S(1)} %fusion.2.own_ref, bf16[2,256,768]{2,1,0:T(8,128)(2,1)} %collective-permute-done.next_ref, f32[2,256,256]{2,1,0:T(8,128)S(1)} %copy-done.2, ...), custom_call_target="tpu_custom_call" | custom-call | tf_op jit(solution)/shard_map/pallas_call | solution.py:166
  8.2 10.5 %collective-permute-done.2.next_ref = bf16[2,256,768]{2,1,0:T(8,128)(2,1)S(1)} collective-permute-done((bf16[2,256,768]{2,1,0:T(8,128)(2,1)S(1)}, bf16[2,256,768]{2,1,0:T(8,128)(2,1)S(1)}, u32[]{:S(2)}, u32[]{:S(2)}) %collective-permute-start.2) | collective-permute-done | bytes 786464 | tf_op jit(solution)/shard_map/ppermute | solution.py:22
  18.7 1.2 %shard_map.66 = (bf16[2,256,256]{2,1,0:T(8,128)(2,1)S(1)}, bf16[2,256,256]{2,1,0:T(8,128)(2,1)S(1)}) custom-call(s32[2,2]{1,0:T(2,128)S(1)} %pad_add_fusion.starts_ref, bf16[2,256,768]{2,1,0:T(8,128)(2,1)S(1)} %fusion.2.own_ref, bf16[2,256,768]{2,1,0:T(8,128)(2,1)S(1)} %collective-permute-done.2.next_ref, f32[2,256,256]{2,1,0:T(8,128)S(1)} %copy-done.2, ...), custom_call_target="tpu_custom_call" | custom-call | tf_op jit(solution)/shard_map/pallas_call | solution.py:166
  19.9 1.3 %collective-permute-start.7 = (bf16[2,256,256]{2,1,0:T(8,128)(2,1)S(1)}, bf16[2,256,256]{2,1,0:T(8,128)(2,1)S(1)}, u32[]{:S(2)}, u32[]{:S(2)}) collective-permute-start(bf16[2,256,256]{2,1,0:T(8,128)(2,1)S(1)} %get-tuple-element.12.odd_own_ref.refs_2_), channel_id=1, source_target_pairs={{1,9},{3,11},{5,13},{7,15},{17,25},{19,27},{21,29},{23,31}} | collective-permute-start | bytes 786440 | tf_op jit(solution)/shard_map/ppermute | solution.py:28
  21.2 0.7 %collective-permute-start.6 = (bf16[2,256,256]{2,1,0:T(8,128)(2,1)S(1)}, bf16[2,256,256]{2,1,0:T(8,128)(2,1)S(1)}, u32[]{:S(2)}, u32[]{:S(2)}) collective-permute-start(bf16[2,256,256]{2,1,0:T(8,128)(2,1)S(1)} %get-tuple-element.11.even_own_ref.refs_0_), channel_id=1, source_target_pairs={{0,8},{2,10},{4,12},{6,14},{16,24},{18,26},{20,28},{22,30}} | collective-permute-start | bytes 786440 | tf_op jit(solution)/shard_map/ppermute | solution.py:28
  21.9 1.3 %collective-permute-start.3 = (bf16[2,256,256]{2,1,0:T(8,128)(2,1)S(1)}, bf16[2,256,256]{2,1,0:T(8,128)(2,1)S(1)}, u32[]{:S(2)}, u32[]{:S(2)}) collective-permute-start(bf16[2,256,256]{2,1,0:T(8,128)(2,1)S(1)} %get-tuple-element.10.odd_own_ref.refs_2_), channel_id=1, source_target_pairs={{1,9},{3,11},{5,13},{7,15},{17,25},{19,27},{21,29},{23,31}} | collective-permute-start | bytes 786440 | tf_op jit(solution)/shard_map/ppermute | solution.py:28
  23.2 0.7 %collective-permute-start.1 = (bf16[2,256,256]{2,1,0:T(8,128)(2,1)S(1)}, bf16[2,256,256]{2,1,0:T(8,128)(2,1)S(1)}, u32[]{:S(2)}, u32[]{:S(2)}) collective-permute-start(bf16[2,256,256]{2,1,0:T(8,128)(2,1)S(1)} %get-tuple-element.9.block_ref.even_own_ref.refs_0_), channel_id=1, source_target_pairs={{0,8},{2,10},{4,12},{6,14},{16,24},{18,26},{20,28},{22,30}} | collective-permute-start | bytes 786440 | tf_op jit(solution)/shard_map/ppermute | solution.py:28
  23.9 6.2 %collective-permute-done.7.odd_near_ref.refs_3_ = bf16[2,256,256]{2,1,0:T(8,128)(2,1)S(1)} collective-permute-done((bf16[2,256,256]{2,1,0:T(8,128)(2,1)S(1)}, bf16[2,256,256]{2,1,0:T(8,128)(2,1)S(1)}, u32[]{:S(2)}, u32[]{:S(2)}) %collective-permute-start.7) | collective-permute-done | bytes 262176 | tf_op jit(solution)/shard_map/ppermute | solution.py:28
  30.1 0.0 collective-permute-done.6.even_near_ref.refs_1_
  30.1 0.7 %collective-permute-start.8 = (bf16[2,256,256]{2,1,0:T(8,128)(2,1)S(1)}, bf16[2,256,256]{2,1,0:T(8,128)(2,1)S(1)}, u32[]{:S(2)}, u32[]{:S(2)}) collective-permute-start(bf16[2,256,256]{2,1,0:T(8,128)(2,1)S(1)} %shard_map.68.refs_4_), channel_id=1, source_target_pairs={{8,16},{9,17},{10,18},{11,19},{12,20},{13,21},{14,22},{15,23}} | collective-permute-start | bytes 786440 | tf_op jit(solution)/shard_map/ppermute | solution.py:28
  30.8 1.3 %collective-permute-start.9 = (bf16[2,256,256]{2,1,0:T(8,128)(2,1)S(1)}, bf16[2,256,256]{2,1,0:T(8,128)(2,1)S(1)}, u32[]{:S(2)}, u32[]{:S(2)}) collective-permute-start(bf16[2,256,256]{2,1,0:T(8,128)(2,1)S(1)} %shard_map.68.refs_4_), channel_id=1, source_target_pairs={{8,24},{9,25},{10,26},{11,27},{12,28},{13,29},{14,30},{15,31}} | collective-permute-start | bytes 786440 | tf_op jit(solution)/shard_map/ppermute | solution.py:28
  32.1 2.8 %collective-permute-done.3.odd_near_ref.refs_3_ = bf16[2,256,256]{2,1,0:T(8,128)(2,1)S(1)} collective-permute-done((bf16[2,256,256]{2,1,0:T(8,128)(2,1)S(1)}, bf16[2,256,256]{2,1,0:T(8,128)(2,1)S(1)}, u32[]{:S(2)}, u32[]{:S(2)}) %collective-permute-start.3) | collective-permute-done | bytes 262176 | tf_op jit(solution)/shard_map/ppermute | solution.py:28
  34.9 0.0 collective-permute-done.1.even_near_ref.refs_1_
  34.9 0.7 %collective-permute-start.4 = (bf16[2,256,256]{2,1,0:T(8,128)(2,1)S(1)}, bf16[2,256,256]{2,1,0:T(8,128)(2,1)S(1)}, u32[]{:S(2)}, u32[]{:S(2)}) collective-permute-start(bf16[2,256,256]{2,1,0:T(8,128)(2,1)S(1)} %shard_map.67.refs_4_), channel_id=1, source_target_pairs={{8,16},{9,17},{10,18},{11,19},{12,20},{13,21},{14,22},{15,23}} | collective-permute-start | bytes 786440 | tf_op jit(solution)/shard_map/ppermute | solution.py:28
  35.6 1.3 %collective-permute-start.5 = (bf16[2,256,256]{2,1,0:T(8,128)(2,1)S(1)}, bf16[2,256,256]{2,1,0:T(8,128)(2,1)S(1)}, u32[]{:S(2)}, u32[]{:S(2)}) collective-permute-start(bf16[2,256,256]{2,1,0:T(8,128)(2,1)S(1)} %shard_map.67.refs_4_), channel_id=1, source_target_pairs={{8,24},{9,25},{10,26},{11,27},{12,28},{13,29},{14,30},{15,31}} | collective-permute-start | bytes 786440 | tf_op jit(solution)/shard_map/ppermute | solution.py:28
  36.9 0.0 collective-permute-done.8.refs_5_
  36.9 3.0 %collective-permute-done.9.refs_6_ = bf16[2,256,256]{2,1,0:T(8,128)(2,1)S(1)} collective-permute-done((bf16[2,256,256]{2,1,0:T(8,128)(2,1)S(1)}, bf16[2,256,256]{2,1,0:T(8,128)(2,1)S(1)}, u32[]{:S(2)}, u32[]{:S(2)}) %collective-permute-start.9) | collective-permute-done | bytes 262176 | tf_op jit(solution)/shard_map/ppermute | solution.py:28
  39.9 3.1 %shard_map.69.refs_7_ = bf16[1,2,256,256]{3,2,1,0:T(8,128)(2,1)S(1)} custom-call(bf16[2,512,256]{2,1,0:T(8,128)(2,1)S(1)} %copy-done, bf16[2,256,512]{2,1,0:T(8,128)(2,1)S(1)} %copy-done.1, bf16[2,256,256]{2,1,0:T(8,128)(2,1)S(1)} %get-tuple-element.11.even_own_ref.refs_0_, bf16[2,256,256]{2,1,0:T(8,128)(2,1)S(1)} %collective-permute-done.6.even_near_ref.refs_1_, ...), custom_call_target="tpu_custom_call" | custom-call | tf_op jit(solution)/shard_map/pallas_call | solution.py:222
  43.0 0.0 collective-permute-done.4.refs_5_
  43.0 2.6 %collective-permute-done.5.refs_6_ = bf16[2,256,256]{2,1,0:T(8,128)(2,1)S(1)} collective-permute-done((bf16[2,256,256]{2,1,0:T(8,128)(2,1)S(1)}, bf16[2,256,256]{2,1,0:T(8,128)(2,1)S(1)}, u32[]{:S(2)}, u32[]{:S(2)}) %collective-permute-start.5) | collective-permute-done | bytes 262176 | tf_op jit(solution)/shard_map/ppermute | solution.py:28
  45.6 3.9 %shard_map.70 = bf16[2,2,256,256]{3,2,1,0:T(8,128)(2,1)} custom-call(bf16[2,512,256]{2,1,0:T(8,128)(2,1)S(1)} %copy-done, bf16[2,256,512]{2,1,0:T(8,128)(2,1)S(1)} %copy-done.1, bf16[2,256,256]{2,1,0:T(8,128)(2,1)S(1)} %get-tuple-element.9.block_ref.even_own_ref.refs_0_, bf16[2,256,256]{2,1,0:T(8,128)(2,1)S(1)} %collective-permute-done.1.even_near_ref.refs_1_, ...), custom_call_target="tpu_custom_call" | custom-call | tf_op jit(solution)/shard_map/pallas_call | solution.py:222
  (10 shorter events, 0.0 us)
Async XLA Ops:
  0.0 7.0 %copy-start = (bf16[2,512,256]{2,1,0:T(8,128)(2,1)S(1)}, bf16[2,512,256]{2,1,0:T(8,128)(2,1)}, u32[]{:S(2)}) copy-start(bf16[2,512,256]{2,1,0:T(8,128)(2,1)} %constant.16.clone.right_ref) | copy-start | bytes 1572868
  0.0 7.0 %copy-start.1 = (bf16[2,256,512]{2,1,0:T(8,128)(2,1)S(1)}, bf16[2,256,512]{2,1,0:T(8,128)(2,1)}, u32[]{:S(2)}) copy-start(bf16[2,256,512]{2,1,0:T(8,128)(2,1)} %constant.17.clone.left_ref) | copy-start | bytes 1572868
  0.0 6.7 %copy-start.3 = (s32[2]{0:T(128)S(1)}, s32[2]{0:T(128)}, u32[]{:S(2)}) copy-start(s32[2]{0:T(128)} %param.8) | copy-start | bytes 28
  0.0 6.8 %copy-start.4 = (s32[2]{0:T(128)S(1)}, s32[2]{0:T(128)}, u32[]{:S(2)}) copy-start(s32[2]{0:T(128)} %param.9) | copy-start | bytes 28
  0.0 7.0 %copy-start.2 = (f32[2,256,256]{2,1,0:T(8,128)S(1)}, f32[2,256,256]{2,1,0:T(8,128)}, u32[]{:S(2)}) copy-start(f32[2,256,256]{2,1,0:T(8,128)} %probe_ref.3) | copy-start | bytes 1572868
  1.9 5.1 %collective-permute-start = (bf16[2,256,768]{2,1,0:T(8,128)(2,1)S(1)}, bf16[2,256,768]{2,1,0:T(8,128)(2,1)}, u32[]{:S(2)}, u32[]{:S(2)}) collective-permute-start(bf16[2,256,768]{2,1,0:T(8,128)(2,1)S(1)} %fusion.2.own_ref), channel_id=1, source_target_pairs={{1,0},{3,2},{5,4},{7,6},{9,8},{11,10},{13,12},{15,14},{17,16},{19,... | collective-permute-start | bytes 2359304 | tf_op jit(solution)/shard_map/ppermute | solution.py:22
  5.4 13.3 %collective-permute-start.2 = (bf16[2,256,768]{2,1,0:T(8,128)(2,1)S(1)}, bf16[2,256,768]{2,1,0:T(8,128)(2,1)S(1)}, u32[]{:S(2)}, u32[]{:S(2)}) collective-permute-start(bf16[2,256,768]{2,1,0:T(8,128)(2,1)S(1)} %fusion.2.own_ref), channel_id=1, source_target_pairs={{2,1},{4,3},{6,5},{10,9},{12,11},{14,13},{18,17},{20,19},{22,21},{... | collective-permute-start | bytes 2359304 | tf_op jit(solution)/shard_map/ppermute | solution.py:22
  19.9 10.2 %collective-permute-start.7 = (bf16[2,256,256]{2,1,0:T(8,128)(2,1)S(1)}, bf16[2,256,256]{2,1,0:T(8,128)(2,1)S(1)}, u32[]{:S(2)}, u32[]{:S(2)}) collective-permute-start(bf16[2,256,256]{2,1,0:T(8,128)(2,1)S(1)} %get-tuple-element.12.odd_own_ref.refs_2_), channel_id=1, source_target_pairs={{1,9},{3,11},{5,13},{7,15},{17,25},{19,27},{21,29},{23,31}} | collective-permute-start | bytes 786440 | tf_op jit(solution)/shard_map/ppermute | solution.py:28
  21.2 8.9 %collective-permute-start.6 = (bf16[2,256,256]{2,1,0:T(8,128)(2,1)S(1)}, bf16[2,256,256]{2,1,0:T(8,128)(2,1)S(1)}, u32[]{:S(2)}, u32[]{:S(2)}) collective-permute-start(bf16[2,256,256]{2,1,0:T(8,128)(2,1)S(1)} %get-tuple-element.11.even_own_ref.refs_0_), channel_id=1, source_target_pairs={{0,8},{2,10},{4,12},{6,14},{16,24},{18,26},{20,28},{22,30}} | collective-permute-start | bytes 786440 | tf_op jit(solution)/shard_map/ppermute | solution.py:28
  21.9 13.0 %collective-permute-start.3 = (bf16[2,256,256]{2,1,0:T(8,128)(2,1)S(1)}, bf16[2,256,256]{2,1,0:T(8,128)(2,1)S(1)}, u32[]{:S(2)}, u32[]{:S(2)}) collective-permute-start(bf16[2,256,256]{2,1,0:T(8,128)(2,1)S(1)} %get-tuple-element.10.odd_own_ref.refs_2_), channel_id=1, source_target_pairs={{1,9},{3,11},{5,13},{7,15},{17,25},{19,27},{21,29},{23,31}} | collective-permute-start | bytes 786440 | tf_op jit(solution)/shard_map/ppermute | solution.py:28
  23.2 11.7 %collective-permute-start.1 = (bf16[2,256,256]{2,1,0:T(8,128)(2,1)S(1)}, bf16[2,256,256]{2,1,0:T(8,128)(2,1)S(1)}, u32[]{:S(2)}, u32[]{:S(2)}) collective-permute-start(bf16[2,256,256]{2,1,0:T(8,128)(2,1)S(1)} %get-tuple-element.9.block_ref.even_own_ref.refs_0_), channel_id=1, source_target_pairs={{0,8},{2,10},{4,12},{6,14},{16,24},{18,26},{20,28},{22,30}} | collective-permute-start | bytes 786440 | tf_op jit(solution)/shard_map/ppermute | solution.py:28
  30.1 6.7 %collective-permute-start.8 = (bf16[2,256,256]{2,1,0:T(8,128)(2,1)S(1)}, bf16[2,256,256]{2,1,0:T(8,128)(2,1)S(1)}, u32[]{:S(2)}, u32[]{:S(2)}) collective-permute-start(bf16[2,256,256]{2,1,0:T(8,128)(2,1)S(1)} %shard_map.68.refs_4_), channel_id=1, source_target_pairs={{8,16},{9,17},{10,18},{11,19},{12,20},{13,21},{14,22},{15,23}} | collective-permute-start | bytes 786440 | tf_op jit(solution)/shard_map/ppermute | solution.py:28
  30.8 9.1 %collective-permute-start.9 = (bf16[2,256,256]{2,1,0:T(8,128)(2,1)S(1)}, bf16[2,256,256]{2,1,0:T(8,128)(2,1)S(1)}, u32[]{:S(2)}, u32[]{:S(2)}) collective-permute-start(bf16[2,256,256]{2,1,0:T(8,128)(2,1)S(1)} %shard_map.68.refs_4_), channel_id=1, source_target_pairs={{8,24},{9,25},{10,26},{11,27},{12,28},{13,29},{14,30},{15,31}} | collective-permute-start | bytes 786440 | tf_op jit(solution)/shard_map/ppermute | solution.py:28
  34.9 8.1 %collective-permute-start.4 = (bf16[2,256,256]{2,1,0:T(8,128)(2,1)S(1)}, bf16[2,256,256]{2,1,0:T(8,128)(2,1)S(1)}, u32[]{:S(2)}, u32[]{:S(2)}) collective-permute-start(bf16[2,256,256]{2,1,0:T(8,128)(2,1)S(1)} %shard_map.67.refs_4_), channel_id=1, source_target_pairs={{8,16},{9,17},{10,18},{11,19},{12,20},{13,21},{14,22},{15,23}} | collective-permute-start | bytes 786440 | tf_op jit(solution)/shard_map/ppermute | solution.py:28
  35.6 10.0 %collective-permute-start.5 = (bf16[2,256,256]{2,1,0:T(8,128)(2,1)S(1)}, bf16[2,256,256]{2,1,0:T(8,128)(2,1)S(1)}, u32[]{:S(2)}, u32[]{:S(2)}) collective-permute-start(bf16[2,256,256]{2,1,0:T(8,128)(2,1)S(1)} %shard_map.67.refs_4_), channel_id=1, source_target_pairs={{8,24},{9,25},{10,26},{11,27},{12,28},{13,29},{14,30},{15,31}} | collective-permute-start | bytes 786440 | tf_op jit(solution)/shard_map/ppermute | solution.py:28

commit v4 on v3

--- a/solution.py
+++ b/solution.py
@@ -115,13 +115,16 @@
     return real, imag
 
 
-def sliced(real, imag, code, right_ref, left_ref):
-    cosine, sine = phase_factor(code.astype(F32))
+def transmitted(real, imag, cosine, sine, right_ref, left_ref):
     real, imag = cosine * real - sine * imag, cosine * imag + sine * real
     return propagated(real, imag, right_ref, left_ref)
 
 
-def first_kernel(count, parity, starts_ref, own_ref, next_ref, probe_ref, right_ref, left_ref, *refs):
+def sliced(real, imag, code, right_ref, left_ref):
+    return transmitted(real, imag, *phase_factor(code.astype(F32)), right_ref, left_ref)
+
+
+def window_kernel(count, parity, starts_ref, own_ref, next_ref, *refs):
     outs, scratch = refs[-1 - count : -1], refs[-1]
     layers, strip, width = own_ref.shape
     size = outs[0].shape[-1]
@@ -149,48 +152,28 @@
                     scratch[part, pl.ds(strip, strip), :] = columns
                     out[s, :, part * 128 : (part + 1) * 128] = scratch[part, pl.ds(r, size), :].astype(BF16)
 
-        @pl.when(lax.axis_index("depth") == 0)
-        def _():
-            waves = [(probe_ref[0], probe_ref[1])] * count
-            for s in range(layers):
-                waves = [sliced(*wave, out[s], right_ref, left_ref) for wave, out in zip(waves, outs)]
-            for (real, imag), out in zip(waves, outs):
-                out[0] = real.astype(BF16)
-                out[1] = imag.astype(BF16)
-
-
-def first_group(parity, starts, own, following, probe, tables, after):
+
+def windows(parity, size, starts, own, following, after):
     layers, strip, _ = own.shape
-    size = probe.shape[-1]
     count = starts.shape[0]
     return pl.pallas_call(
-        functools.partial(first_kernel, count, parity),
+        functools.partial(window_kernel, count, parity),
         out_shape=[jax.ShapeDtypeStruct((layers, size, size), BF16)] * count,
-        in_specs=[SMEM] + [VMEM] * (5 + len(after)),
+        in_specs=[SMEM] + [VMEM] * (2 + len(after)),
         out_specs=[VMEM] * count,
         scratch_shapes=[pltpu.VMEM((size // 128, 2 * strip, 128), F32)],
         compiler_params=pltpu.CompilerParams(vmem_limit_bytes=ROOM),
-    )(starts, own, following, probe, *tables, *after)
-
-
-def through_groups(wave_ref, first, groups, block, layers, right_ref, left_ref):
-    group = lax.axis_index("depth")
-    for g in range(first, groups):
-
-        @pl.when(g <= group)
-        def _():
-            real, imag = wave_ref[0].astype(F32), wave_ref[1].astype(F32)
-            for s in range(layers):
-                real, imag = sliced(real, imag, block(g, s), right_ref, left_ref)
-            wave_ref[0] = real.astype(BF16)
-            wave_ref[1] = imag.astype(BF16)
-
-
-def chain_kernel(groups, distances, before, starting, right_ref, left_ref, *refs):
-    some = len(distances)
-    arrived = tuple(dict(zip(distances, refs[k * some : (k + 1) * some])) for k in range(2))
-    more = refs[2 * some :]
-    out_ref, wave_ref = refs[-2], refs[-1]
+    )(starts, own, following, *after)
+
+
+def rounded(state_ref, real, imag):
+    state_ref[0] = real.astype(BF16).astype(F32)
+    state_ref[1] = imag.astype(BF16).astype(F32)
+
+
+def chain_kernel(groups, before, probe_ref, right_ref, left_ref, *refs):
+    arrived = (refs[:groups], refs[groups : 2 * groups])
+    out_ref, state_ref = refs[-2], refs[-1]
     group = lax.axis_index("depth")
     even = lax.axis_index("probe") % 2 == 0
 
@@ -201,53 +184,121 @@
             value = this if value is None else jnp.where(group ^ g == m, this, value)
         return value
 
-    for s in range(2):
-        if starting:
-            value = jnp.where(even, arrived[0][0][s], arrived[1][0][s])
-            for k in range(starting):
-                value = jnp.where(group == k + 1, more[k][s], value)
-            wave_ref[s] = value
-        else:
-            wave_ref[s] = block(0, s)
-    through_groups(wave_ref, 2 if starting else 1, groups, block, arrived[0][0].shape[0], right_ref, left_ref)
-    out_ref[before] = wave_ref[...]
+    state_ref[...] = probe_ref[...]
+    for g in range(groups):
+
+        @pl.when(g <= group)
+        def _():
+            real, imag = state_ref[0], state_ref[1]
+            for s in range(arrived[0][0].shape[0]):
+                real, imag = sliced(real, imag, block(g, s), right_ref, left_ref)
+            rounded(state_ref, real, imag)
+
+    out_ref[before] = state_ref[...].astype(BF16)
     for j in range(before):
-        out_ref[j] = more[starting + j][0]
-
-
-def chain(groups, tables, even, odd, starting, finished):
-    distances = sorted(even)
-    shape = (2, *even[0].shape[1:])
-    arguments = [*tables, *(even[m] for m in distances), *(odd[m] for m in distances), *starting, *finished]
-    return pl.pallas_call(
-        functools.partial(chain_kernel, groups, distances, len(finished), len(starting)),
+        out_ref[j] = refs[2 * groups + j][0]
+
+
+def chain(groups, probe, tables, even, odd, finished):
+    blocks = [each[m] for each in (even, odd) for m in range(groups)]
+    arguments = [probe, *tables, *blocks, *finished]
+    return pl.pallas_call(
+        functools.partial(chain_kernel, groups, len(finished)),
+        out_shape=jax.ShapeDtypeStruct((len(finished) + 1, *probe.shape), BF16),
+        in_specs=[VMEM] * len(arguments),
+        out_specs=VMEM,
+        scratch_shapes=[pltpu.VMEM(probe.shape, F32)],
+        compiler_params=pltpu.CompilerParams(vmem_limit_bytes=ROOM),
+    )(*arguments)
+
+
+def factor_kernel(count, unused, *refs):
+    even_refs, odd_refs, outs = refs[:count], refs[count : 2 * count], refs[2 * count :]
+    even = lax.axis_index("probe") % 2 == 0
+    group = lax.axis_index("depth")
+
+    @pl.when(group != unused)
+    def _():
+        for j in range(count):
+            for s in range(even_refs[j].shape[0]):
+                code = jnp.where(even, even_refs[j][s], odd_refs[j][s])
+                outs[j][s, 0], outs[j][s, 1] = phase_factor(code.astype(F32))
+
+
+def phase_factors(unused, even, odd):
+    count = len(even)
+    layers, size, _ = even[0].shape
+    return pl.pallas_call(
+        functools.partial(factor_kernel, count, unused),
+        out_shape=[jax.ShapeDtypeStruct((layers, 2, size, size), F32)] * count,
+        in_specs=[VMEM] * (2 * count),
+        out_specs=[VMEM] * count,
+        compiler_params=pltpu.CompilerParams(vmem_limit_bytes=ROOM),
+    )(*even, *odd)
+
+
+def group_of(state_ref, factor, layers, right_ref, left_ref):
+    real, imag = state_ref[0], state_ref[1]
+    for s in range(layers):
+        real, imag = transmitted(real, imag, factor(s, 0), factor(s, 1), right_ref, left_ref)
+    rounded(state_ref, real, imag)
+
+
+def second_kernel(probe_ref, right_ref, left_ref, own_ref, near_ref, first_ref, second_ref, state_ref):
+    group = lax.axis_index("depth")
+
+    @pl.when(group < 2)
+    def _():
+        state_ref[...] = probe_ref[...]
+        for g, out_ref in enumerate((first_ref, second_ref)):
+            factor = lambda s, k: jnp.where(group == g, own_ref[s, k], near_ref[s, k])
+            group_of(state_ref, factor, own_ref.shape[0], right_ref, left_ref)
+            out_ref[...] = state_ref[...].astype(BF16)
+
+
+def second_group(probe, tables, own, near):
+    return pl.pallas_call(
+        second_kernel,
+        out_shape=[jax.ShapeDtypeStruct(probe.shape, BF16)] * 2,
+        in_specs=[VMEM] * 5,
+        out_specs=[VMEM] * 2,
+        scratch_shapes=[pltpu.VMEM(probe.shape, F32)],
+        compiler_params=pltpu.CompilerParams(vmem_limit_bytes=ROOM),
+    )(probe, *tables, own, near)
+
+
+def last_kernel(right_ref, left_ref, own_ref, near_ref, first_ref, second_ref, far_ref, *refs):
+    out_ref, state_ref = refs[-2:]
+    finished = refs[:-2]
+    layers = own_ref.shape[0]
+    group = lax.axis_index("depth")
+    for part in range(2):
+        value = jnp.where(group == 0, first_ref[part], second_ref[part])
+        value = jnp.where(group >= 2, far_ref[part], value)
+        state_ref[part] = value.astype(F32)
+
+    @pl.when(group == 3)
+    def _():
+        group_of(state_ref, lambda s, k: near_ref[s, k], layers, right_ref, left_ref)
+
+    @pl.when(group >= 2)
+    def _():
+        group_of(state_ref, lambda s, k: own_ref[s, k], layers, right_ref, left_ref)
+
+    out_ref[len(finished)] = state_ref[...].astype(BF16)
+    for j, ref in enumerate(finished):
+        out_ref[j] = ref[0]
+
+
+def last_groups(tables, own, near, waves, finished):
+    shape = waves[0].shape
+    arguments = [*tables, own, near, *waves, *finished]
+    return pl.pallas_call(
+        last_kernel,
         out_shape=jax.ShapeDtypeStruct((len(finished) + 1, *shape), BF16),
         in_specs=[VMEM] * len(arguments),
         out_specs=VMEM,
-        scratch_shapes=[pltpu.VMEM(shape, BF16)],
-        compiler_params=pltpu.CompilerParams(vmem_limit_bytes=ROOM),
-    )(*arguments)
-
-
-def second_kernel(right_ref, left_ref, even_own_ref, even_near_ref, odd_own_ref, odd_near_ref, out_ref):
-    even = lax.axis_index("probe") % 2 == 0
-
-    @pl.when(lax.axis_index("depth") == 1)
-    def _():
-        real, imag = [jnp.where(even, even_near_ref[s], odd_near_ref[s]).astype(F32) for s in range(2)]
-        for s in range(even_own_ref.shape[0]):
-            real, imag = sliced(real, imag, jnp.where(even, even_own_ref[s], odd_own_ref[s]), right_ref, left_ref)
-        out_ref[0] = real.astype(BF16)
-        out_ref[1] = imag.astype(BF16)
-
-
-def second_group(tables, even, odd):
-    arguments = [*tables, even[0], even[1], odd[0], odd[1]]
-    return pl.pallas_call(
-        second_kernel,
-        out_shape=jax.ShapeDtypeStruct((2, *even[0].shape[1:]), BF16),
-        in_specs=[VMEM] * len(arguments),
-        out_specs=VMEM,
+        scratch_shapes=[pltpu.VMEM(shape, F32)],
         compiler_params=pltpu.CompilerParams(vmem_limit_bytes=ROOM),
     )(*arguments)
 
@@ -264,6 +315,12 @@
         out_specs=VMEM,
         compiler_params=pltpu.CompilerParams(vmem_limit_bytes=ROOM),
     )(block)
+
+
+def pairs_at(groups, m):
+    if groups == 4:
+        return [(0, 1), (1, 0), (2, 3)]
+    return [(i, i ^ m) for i in range(groups) if i < i ^ m < groups]
 
 
 def hops(groups, count):
@@ -284,25 +341,36 @@
     arrived = {}
     after = []
     for parity in (0, 1):
-        firsts = first_group(parity, starts, own, following[parity], probe, tables, after)
+        firsts = windows(parity, size, starts, own, following[parity], after)
         blocks = [{0: first} for first in firsts]
         for j, m in hops(groups, count):
-            blocks[j][m] = sent_on(firsts[j], (parity,), [(i, i ^ m) for i in range(groups) if i < i ^ m < groups])
+            blocks[j][m] = sent_on(firsts[j], (parity,), pairs_at(groups, m))
         if parity == 0:
             after = [mark(firsts[-1])]
         arrived[parity] = blocks
-    starting = [[] for _ in range(count)]
     if groups == 4:
-        for j in range(count):
-            starting[j].append(second_group(tables, arrived[0][j], arrived[1][j]))
-        for target in (2, 3):
-            for j in range(count):
-                starting[j].append(sent_on(starting[j][0], (0, 1), [(1, target)]))
+        return four_groups(probe, tables, arrived)[None]
     finished = []
     for j in range(count):
-        wave = chain(groups, tables, arrived[0][j], arrived[1][j], starting[j], finished if j == count - 1 else [])
+        wave = chain(groups, probe, tables, arrived[0][j], arrived[1][j], finished if j == count - 1 else [])
         finished.append(wave)
     return wave[None]
+
+
+def four_groups(probe, tables, arrived):
+    even, odd = arrived[0], arrived[1]
+    count = len(even)
+    own = phase_factors(-1, [b[0] for b in even], [b[0] for b in odd])
+    near, waves = [], []
+    for j in range(count):
+        near += phase_factors(2, [even[j][1]], [odd[j][1]])
+        waves.append([*second_group(probe, tables, own[j], near[j])])
+        waves[j].append(sent_on(waves[j][1], (0, 1), [(0, 2), (1, 3)]))
+    finished = []
+    for j in range(count):
+        wave = last_groups(tables, own[j], near[j], waves[j], finished if j == count - 1 else [])
+        finished.append(wave)
+    return wave
 
 
 def solution(mesh):

time: 49.8 us -> 48.5 us (0.974)
  starting transfers between devices: 12.6 us -> 10.6 us
  waiting for transfers between devices: 25.2 us -> 26.3 us
    ppermute x8 -> x6, starting transfers between devices: 7.86 us -> 6.65 us  [sent_on(): return lax.ppermute(block, ('depth', 'probe'), route)]
    ppermute x2, starting transfers between devices: 4.77 us -> 3.92 us  [handed_down(): lax.ppermute(block, 'probe', [(i + 1, i) for i in range(parity, strips -...]
    ppermute x2, waiting for transfers between devices: 10.5 us -> 11.1 us  [handed_down(): lax.ppermute(block, 'probe', [(i + 1, i) for i in range(parity, strips -...]
    ppermute x8 -> x6, waiting for transfers between devices: 14.6 us -> 15.1 us  [sent_on(): return lax.ppermute(block, ('depth', 'probe'), route)]
    pallas_call x6 -> x9, Pallas kernels: 9.35 us -> 9.05 us  [the longest x2 5.66 us: last_groups(): pl.pallas_call(last_kernel, out_shape=jax.ShapeDtypeStruct((len(finished)...]
  transfers between devices with their start and end apart: 10 -> 8, of which waited for: 5 -> 6; matrix products, arithmetic and copies ran while one was open for 1% -> 1% of each run, Pallas kernels for 9% -> 10%
where the time goes in v4:
time: 48.5 us; the launch traced here: 48.2 us
  waiting for transfers between devices  26.3 us (54%)
  starting transfers between devices  10.6 us (22%)
  Pallas kernels  9.05 us (19%)
  other arithmetic  1.86 us (4%)
    ppermute x6, waiting for transfers between devices, sent_on(): return lax.ppermute(block, ('depth', 'probe'), route)  15.1 us
    ppermute x2, waiting for transfers between devices, handed_down(): lax.ppermute(block, 'probe', [(i + 1, i) for i in range(parity, strips -...  11.1 us
    ppermute x6, starting transfers between devices, sent_on(): return lax.ppermute(block, ('depth', 'probe'), route)  6.65 us
    pallas_call x2, Pallas kernels, last_groups(): pl.pallas_call(last_kernel, out_shape=jax.ShapeDtypeStruct((len(finished)...  5.66 us
    ppermute x2, starting transfers between devices, handed_down(): lax.ppermute(block, 'probe', [(i + 1, i) for i in range(parity, strips -...  3.92 us
    pallas_call x2, Pallas kernels, windows(): pl.pallas_call(functools.partial(window_kernel, count, parity), out_shape...  1.79 us
    convert_element_type x1, other arithmetic, coded(): return jnp.exp2(OCTAVES * (turns - jnp.round(turns))).astype(BF16)  1.78 us
    pallas_call x3, Pallas kernels, phase_factors(): pl.pallas_call(functools.partial(factor_kernel, count, unused), out_shape...  1.56 us
  transfers between devices with their start and end apart: 8, of which 6 were waited for; matrix products, arithmetic and copies ran while one was open for 1% of the time, Pallas kernels for 10%

profile of v4, /device:TPU:23, one launch (start us, length us, event | category | flops | bytes accessed | tf_op | source)
XLA Modules:
  0.0 48.2 jit_solution(2243857209699461364)
XLA Ops:
  0.0 1.8 %fusion.2.own_ref = bf16[2,256,768]{2,1,0:T(8,128)(2,1)S(1)} fusion(f32[2,256,768]{2,1,0:T(8,128)} %param.7), kind=kLoop, calls=%fused_computation.3 | loop fusion | flops 1966080 | bytes 2359296 | tf_op jit(solution)/shard_map/convert_element_type | solution.py:83
  1.8 2.6 %collective-permute-start = (bf16[2,256,768]{2,1,0:T(8,128)(2,1)S(1)}, bf16[2,256,768]{2,1,0:T(8,128)(2,1)S(1)}, u32[]{:S(2)}, u32[]{:S(2)}) collective-permute-start(bf16[2,256,768]{2,1,0:T(8,128)(2,1)S(1)} %fusion.2.own_ref), channel_id=1, source_target_pairs={{1,0},{3,2},{5,4},{7,6},{9,8},{11,10},{13,12},{15,14},{17,16},{19,... | collective-permute-start | bytes 2359304 | tf_op jit(solution)/shard_map/ppermute | solution.py:22
  4.4 1.3 %collective-permute-start.1 = (bf16[2,256,768]{2,1,0:T(8,128)(2,1)S(1)}, bf16[2,256,768]{2,1,0:T(8,128)(2,1)S(1)}, u32[]{:S(2)}, u32[]{:S(2)}) collective-permute-start(bf16[2,256,768]{2,1,0:T(8,128)(2,1)S(1)} %fusion.2.own_ref), channel_id=1, source_target_pairs={{2,1},{4,3},{6,5},{10,9},{12,11},{14,13},{18,17},{20,19},{22,21},{... | collective-permute-start | bytes 2359304 | tf_op jit(solution)/shard_map/ppermute | solution.py:22
  5.7 0.0 copy-done.3
  5.8 0.1 copy.7
  5.8 0.0 copy-done.4
  5.8 0.1 copy.8
  5.9 0.1 pad_add_fusion.starts_ref
  6.0 0.3 collective-permute-done.next_ref
  6.3 0.6 %shard_map.64 = (bf16[2,256,256]{2,1,0:T(8,128)(2,1)S(1)}, bf16[2,256,256]{2,1,0:T(8,128)(2,1)S(1)}) custom-call(s32[2,2]{1,0:T(2,128)S(1)} %pad_add_fusion.starts_ref, bf16[2,256,768]{2,1,0:T(8,128)(2,1)S(1)} %fusion.2.own_ref, bf16[2,256,768]{2,1,0:T(8,128)(2,1)S(1)} %collective-permute-done.next_ref), custom_call_target="tpu_custom_call" | custom-call | tf_op jit(solution)/shard_map/pallas_call | solution.py:159
  6.9 10.9 %collective-permute-done.1.next_ref = bf16[2,256,768]{2,1,0:T(8,128)(2,1)S(1)} collective-permute-done((bf16[2,256,768]{2,1,0:T(8,128)(2,1)S(1)}, bf16[2,256,768]{2,1,0:T(8,128)(2,1)S(1)}, u32[]{:S(2)}, u32[]{:S(2)}) %collective-permute-start.1) | collective-permute-done | bytes 786464 | tf_op jit(solution)/shard_map/ppermute | solution.py:22
  17.7 1.2 %shard_map.66 = (bf16[2,256,256]{2,1,0:T(8,128)(2,1)S(1)}, bf16[2,256,256]{2,1,0:T(8,128)(2,1)S(1)}) custom-call(s32[2,2]{1,0:T(2,128)S(1)} %pad_add_fusion.starts_ref, bf16[2,256,768]{2,1,0:T(8,128)(2,1)S(1)} %fusion.2.own_ref, bf16[2,256,768]{2,1,0:T(8,128)(2,1)S(1)} %collective-permute-done.1.next_ref, bf16[16,128]{1,0:T(8,128)(2,1)S(1)} %shard_map.65.refs_0_), custom_call_target="tpu_custom_call" | custom-call | tf_op jit(solution)/shard_map/pallas_call | solution.py:159
  19.0 0.0 copy-start
  19.0 0.0 copy-start.1
  19.0 0.0 copy-start.2
  19.0 1.4 %collective-permute-start.6 = (bf16[2,256,256]{2,1,0:T(8,128)(2,1)S(1)}, bf16[2,256,256]{2,1,0:T(8,128)(2,1)S(1)}, u32[]{:S(2)}, u32[]{:S(2)}) collective-permute-start(bf16[2,256,256]{2,1,0:T(8,128)(2,1)S(1)} %get-tuple-element.17.refs_2_), channel_id=1, source_target_pairs={{1,9},{3,11},{5,13},{7,15},{9,1},{11,3},{13,5},{15,7},{17,25},{19,... | collective-permute-start | bytes 786440 | tf_op jit(solution)/shard_map/ppermute | solution.py:28
  20.4 0.7 %collective-permute-start.5 = (bf16[2,256,256]{2,1,0:T(8,128)(2,1)S(1)}, bf16[2,256,256]{2,1,0:T(8,128)(2,1)S(1)}, u32[]{:S(2)}, u32[]{:S(2)}) collective-permute-start(bf16[2,256,256]{2,1,0:T(8,128)(2,1)S(1)} %get-tuple-element.15.refs_0_), channel_id=1, source_target_pairs={{0,8},{2,10},{4,12},{6,14},{8,0},{10,2},{12,4},{14,6},{16,24},{18,... | collective-permute-start | bytes 786440 | tf_op jit(solution)/shard_map/ppermute | solution.py:28
  21.1 1.3 %collective-permute-start.3 = (bf16[2,256,256]{2,1,0:T(8,128)(2,1)S(1)}, bf16[2,256,256]{2,1,0:T(8,128)(2,1)S(1)}, u32[]{:S(2)}, u32[]{:S(2)}) collective-permute-start(bf16[2,256,256]{2,1,0:T(8,128)(2,1)S(1)} %get-tuple-element.18.refs_3_), channel_id=1, source_target_pairs={{1,9},{3,11},{5,13},{7,15},{9,1},{11,3},{13,5},{15,7},{17,25},{19,... | collective-permute-start | bytes 786440 | tf_op jit(solution)/shard_map/ppermute | solution.py:28
  22.4 0.7 %collective-permute-start.2 = (bf16[2,256,256]{2,1,0:T(8,128)(2,1)S(1)}, bf16[2,256,256]{2,1,0:T(8,128)(2,1)S(1)}, u32[]{:S(2)}, u32[]{:S(2)}) collective-permute-start(bf16[2,256,256]{2,1,0:T(8,128)(2,1)S(1)} %get-tuple-element.16.block_ref.refs_1_), channel_id=1, source_target_pairs={{0,8},{2,10},{4,12},{6,14},{8,0},{10,2},{12,4},{14,6},{16,24},{18,... | collective-permute-start | bytes 786440 | tf_op jit(solution)/shard_map/ppermute | solution.py:28
  23.1 0.8 %shard_map.67 = (f32[2,2,256,256]{3,2,1,0:T(8,128)S(1)}, f32[2,2,256,256]{3,2,1,0:T(8,128)S(1)}) custom-call(bf16[2,256,256]{2,1,0:T(8,128)(2,1)S(1)} %get-tuple-element.15.refs_0_, bf16[2,256,256]{2,1,0:T(8,128)(2,1)S(1)} %get-tuple-element.16.block_ref.refs_1_, bf16[2,256,256]{2,1,0:T(8,128)(2,1)S(1)} %get-tuple-element.17.refs_2_, ...), custom_call_target="tpu_custom_call" | custom-call | tf_op jit(solution)/shard_map/pallas_call | solution.py:231
  23.9 5.5 %collective-permute-done.6.refs_1_ = bf16[2,256,256]{2,1,0:T(8,128)(2,1)S(1)} collective-permute-done((bf16[2,256,256]{2,1,0:T(8,128)(2,1)S(1)}, bf16[2,256,256]{2,1,0:T(8,128)(2,1)S(1)}, u32[]{:S(2)}, u32[]{:S(2)}) %collective-permute-start.6) | collective-permute-done | bytes 262176 | tf_op jit(solution)/shard_map/ppermute | solution.py:28
  29.4 0.0 collective-permute-done.5.refs_0_
  29.4 0.4 shard_map.70.near_ref
  29.8 1.3 %collective-permute-start.7 = (bf16[2,256,256]{2,1,0:T(8,128)(2,1)S(1)}, bf16[2,256,256]{2,1,0:T(8,128)(2,1)S(1)}, u32[]{:S(2)}, u32[]{:S(2)}) collective-permute-start(bf16[2,256,256]{2,1,0:T(8,128)(2,1)S(1)} %get-tuple-element.24.second_ref), channel_id=1, source_target_pairs={{0,16},{1,17},{2,18},{3,19},{4,20},{5,21},{6,22},{7,23},{8,24},{9,... | collective-permute-start | bytes 786440 | tf_op jit(solution)/shard_map/ppermute | solution.py:28
  31.1 3.0 %collective-permute-done.3.refs_1_ = bf16[2,256,256]{2,1,0:T(8,128)(2,1)S(1)} collective-permute-done((bf16[2,256,256]{2,1,0:T(8,128)(2,1)S(1)}, bf16[2,256,256]{2,1,0:T(8,128)(2,1)S(1)}, u32[]{:S(2)}, u32[]{:S(2)}) %collective-permute-start.3) | collective-permute-done | bytes 262176 | tf_op jit(solution)/shard_map/ppermute | solution.py:28
  34.1 0.0 collective-permute-done.2.refs_0_
  34.1 0.4 shard_map.68.near_ref
  34.5 1.3 %collective-permute-start.4 = (bf16[2,256,256]{2,1,0:T(8,128)(2,1)S(1)}, bf16[2,256,256]{2,1,0:T(8,128)(2,1)S(1)}, u32[]{:S(2)}, u32[]{:S(2)}) collective-permute-start(bf16[2,256,256]{2,1,0:T(8,128)(2,1)S(1)} %get-tuple-element.21.second_ref), channel_id=1, source_target_pairs={{0,16},{1,17},{2,18},{3,19},{4,20},{5,21},{6,22},{7,23},{8,24},{9,... | collective-permute-start | bytes 786440 | tf_op jit(solution)/shard_map/ppermute | solution.py:28
  35.8 3.6 %collective-permute-done.7.far_ref = bf16[2,256,256]{2,1,0:T(8,128)(2,1)S(1)} collective-permute-done((bf16[2,256,256]{2,1,0:T(8,128)(2,1)S(1)}, bf16[2,256,256]{2,1,0:T(8,128)(2,1)S(1)}, u32[]{:S(2)}, u32[]{:S(2)}) %collective-permute-start.7) | collective-permute-done | bytes 262176 | tf_op jit(solution)/shard_map/ppermute | solution.py:28
  39.4 2.4 %shard_map.72.refs_0_ = bf16[1,2,256,256]{3,2,1,0:T(8,128)(2,1)S(1)} custom-call(bf16[2,512,256]{2,1,0:T(8,128)(2,1)S(1)} %copy-done, bf16[2,256,512]{2,1,0:T(8,128)(2,1)S(1)} %copy-done.1, f32[2,2,256,256]{3,2,1,0:T(8,128)S(1)} %get-tuple-element.22.own_ref, f32[2,2,256,256]{3,2,1,0:T(8,128)S(1)} %shard_map.70.near_ref, ...), custom_call_target="tpu_custom_call" | custom-call | tf_op jit(solution)/shard_map/pallas_call | solution.py:296
  41.8 3.1 %collective-permute-done.4.far_ref = bf16[2,256,256]{2,1,0:T(8,128)(2,1)S(1)} collective-permute-done((bf16[2,256,256]{2,1,0:T(8,128)(2,1)S(1)}, bf16[2,256,256]{2,1,0:T(8,128)(2,1)S(1)}, u32[]{:S(2)}, u32[]{:S(2)}) %collective-permute-start.4) | collective-permute-done | bytes 262176 | tf_op jit(solution)/shard_map/ppermute | solution.py:28
  44.9 3.2 %shard_map.73 = bf16[2,2,256,256]{3,2,1,0:T(8,128)(2,1)} custom-call(bf16[2,512,256]{2,1,0:T(8,128)(2,1)S(1)} %copy-done, bf16[2,256,512]{2,1,0:T(8,128)(2,1)S(1)} %copy-done.1, f32[2,2,256,256]{3,2,1,0:T(8,128)S(1)} %get-tuple-element.19.own_ref, f32[2,2,256,256]{3,2,1,0:T(8,128)S(1)} %shard_map.68.near_ref, ...), custom_call_target="tpu_custom_call" | custom-call | tf_op jit(solution)/shard_map/pallas_call | solution.py:296
  (9 shorter events, 0.1 us)
Async XLA Ops:
  0.0 5.7 %copy-start.3 = (s32[2]{0:T(128)S(1)}, s32[2]{0:T(128)}, u32[]{:S(2)}) copy-start(s32[2]{0:T(128)} %param.8) | copy-start | bytes 28
  0.0 5.8 %copy-start.4 = (s32[2]{0:T(128)S(1)}, s32[2]{0:T(128)}, u32[]{:S(2)}) copy-start(s32[2]{0:T(128)} %param.9) | copy-start | bytes 28
  1.8 4.5 %collective-permute-start = (bf16[2,256,768]{2,1,0:T(8,128)(2,1)S(1)}, bf16[2,256,768]{2,1,0:T(8,128)(2,1)S(1)}, u32[]{:S(2)}, u32[]{:S(2)}) collective-permute-start(bf16[2,256,768]{2,1,0:T(8,128)(2,1)S(1)} %fusion.2.own_ref), channel_id=1, source_target_pairs={{1,0},{3,2},{5,4},{7,6},{9,8},{11,10},{13,12},{15,14},{17,16},{19,... | collective-permute-start | bytes 2359304 | tf_op jit(solution)/shard_map/ppermute | solution.py:22
  4.4 13.3 %collective-permute-start.1 = (bf16[2,256,768]{2,1,0:T(8,128)(2,1)S(1)}, bf16[2,256,768]{2,1,0:T(8,128)(2,1)S(1)}, u32[]{:S(2)}, u32[]{:S(2)}) collective-permute-start(bf16[2,256,768]{2,1,0:T(8,128)(2,1)S(1)} %fusion.2.own_ref), channel_id=1, source_target_pairs={{2,1},{4,3},{6,5},{10,9},{12,11},{14,13},{18,17},{20,19},{22,21},{... | collective-permute-start | bytes 2359304 | tf_op jit(solution)/shard_map/ppermute | solution.py:22
  19.0 10.8 %copy-start = (bf16[2,512,256]{2,1,0:T(8,128)(2,1)S(1)}, bf16[2,512,256]{2,1,0:T(8,128)(2,1)}, u32[]{:S(2)}) copy-start(bf16[2,512,256]{2,1,0:T(8,128)(2,1)} %constant.16.clone.right_ref) | copy-start | bytes 1572868
  19.0 10.8 %copy-start.1 = (bf16[2,256,512]{2,1,0:T(8,128)(2,1)S(1)}, bf16[2,256,512]{2,1,0:T(8,128)(2,1)}, u32[]{:S(2)}) copy-start(bf16[2,256,512]{2,1,0:T(8,128)(2,1)} %constant.17.clone.left_ref) | copy-start | bytes 1572868
  19.0 10.8 %copy-start.2 = (f32[2,256,256]{2,1,0:T(8,128)S(1)}, f32[2,256,256]{2,1,0:T(8,128)}, u32[]{:S(2)}) copy-start(f32[2,256,256]{2,1,0:T(8,128)} %probe_ref.3) | copy-start | bytes 1572868
  19.0 10.3 %collective-permute-start.6 = (bf16[2,256,256]{2,1,0:T(8,128)(2,1)S(1)}, bf16[2,256,256]{2,1,0:T(8,128)(2,1)S(1)}, u32[]{:S(2)}, u32[]{:S(2)}) collective-permute-start(bf16[2,256,256]{2,1,0:T(8,128)(2,1)S(1)} %get-tuple-element.17.refs_2_), channel_id=1, source_target_pairs={{1,9},{3,11},{5,13},{7,15},{9,1},{11,3},{13,5},{15,7},{17,25},{19,... | collective-permute-start | bytes 786440 | tf_op jit(solution)/shard_map/ppermute | solution.py:28
  20.4 8.9 %collective-permute-start.5 = (bf16[2,256,256]{2,1,0:T(8,128)(2,1)S(1)}, bf16[2,256,256]{2,1,0:T(8,128)(2,1)S(1)}, u32[]{:S(2)}, u32[]{:S(2)}) collective-permute-start(bf16[2,256,256]{2,1,0:T(8,128)(2,1)S(1)} %get-tuple-element.15.refs_0_), channel_id=1, source_target_pairs={{0,8},{2,10},{4,12},{6,14},{8,0},{10,2},{12,4},{14,6},{16,24},{18,... | collective-permute-start | bytes 786440 | tf_op jit(solution)/shard_map/ppermute | solution.py:28
  21.1 13.0 %collective-permute-start.3 = (bf16[2,256,256]{2,1,0:T(8,128)(2,1)S(1)}, bf16[2,256,256]{2,1,0:T(8,128)(2,1)S(1)}, u32[]{:S(2)}, u32[]{:S(2)}) collective-permute-start(bf16[2,256,256]{2,1,0:T(8,128)(2,1)S(1)} %get-tuple-element.18.refs_3_), channel_id=1, source_target_pairs={{1,9},{3,11},{5,13},{7,15},{9,1},{11,3},{13,5},{15,7},{17,25},{19,... | collective-permute-start | bytes 786440 | tf_op jit(solution)/shard_map/ppermute | solution.py:28
  22.4 11.7 %collective-permute-start.2 = (bf16[2,256,256]{2,1,0:T(8,128)(2,1)S(1)}, bf16[2,256,256]{2,1,0:T(8,128)(2,1)S(1)}, u32[]{:S(2)}, u32[]{:S(2)}) collective-permute-start(bf16[2,256,256]{2,1,0:T(8,128)(2,1)S(1)} %get-tuple-element.16.block_ref.refs_1_), channel_id=1, source_target_pairs={{0,8},{2,10},{4,12},{6,14},{8,0},{10,2},{12,4},{14,6},{16,24},{18,... | collective-permute-start | bytes 786440 | tf_op jit(solution)/shard_map/ppermute | solution.py:28
  29.8 9.6 %collective-permute-start.7 = (bf16[2,256,256]{2,1,0:T(8,128)(2,1)S(1)}, bf16[2,256,256]{2,1,0:T(8,128)(2,1)S(1)}, u32[]{:S(2)}, u32[]{:S(2)}) collective-permute-start(bf16[2,256,256]{2,1,0:T(8,128)(2,1)S(1)} %get-tuple-element.24.second_ref), channel_id=1, source_target_pairs={{0,16},{1,17},{2,18},{3,19},{4,20},{5,21},{6,22},{7,23},{8,24},{9,... | collective-permute-start | bytes 786440 | tf_op jit(solution)/shard_map/ppermute | solution.py:28
  34.5 10.4 %collective-permute-start.4 = (bf16[2,256,256]{2,1,0:T(8,128)(2,1)S(1)}, bf16[2,256,256]{2,1,0:T(8,128)(2,1)S(1)}, u32[]{:S(2)}, u32[]{:S(2)}) collective-permute-start(bf16[2,256,256]{2,1,0:T(8,128)(2,1)S(1)} %get-tuple-element.21.second_ref), channel_id=1, source_target_pairs={{0,16},{1,17},{2,18},{3,19},{4,20},{5,21},{6,22},{7,23},{8,24},{9,... | collective-permute-start | bytes 786440 | tf_op jit(solution)/shard_map/ppermute | solution.py:28

commit v5 on v4

--- a/solution.py
+++ b/solution.py
@@ -136,8 +136,8 @@
         edge = (place == lax.axis_size("probe") - 1).astype(F32)
         line = lax.broadcasted_iota(jnp.int32, (strip, span), 0)
         for j, out in enumerate(outs):
-            r = starts_ref[j, 0]
-            c = starts_ref[j, 1]
+            r = jnp.max(starts_ref[j, 0]).astype(jnp.int32)
+            c = jnp.max(starts_ref[j, 1]).astype(jnp.int32)
             base = jnp.minimum(c // 128, (width - span) // 128)
             shift = c - base * 128
             lanes = pl.ds(pl.multiple_of(base * 128, 128), span)
@@ -159,7 +159,7 @@
     return pl.pallas_call(
         functools.partial(window_kernel, count, parity),
         out_shape=[jax.ShapeDtypeStruct((layers, size, size), BF16)] * count,
-        in_specs=[SMEM] + [VMEM] * (2 + len(after)),
+        in_specs=[VMEM] * (3 + len(after)),
         out_specs=[VMEM] * count,
         scratch_shapes=[pltpu.VMEM((size // 128, 2 * strip, 128), F32)],
         compiler_params=pltpu.CompilerParams(vmem_limit_bytes=ROOM),
@@ -333,6 +333,7 @@
     count = row_offsets.shape[0]
     groups = lax.axis_size("depth")
     starts = jnp.stack([row_offsets - lax.axis_index("probe") * strip, col_offsets], axis=1)
+    starts = jnp.broadcast_to(starts.astype(F32)[:, :, None, None], (count, 2, 8, 128))
     tables = operator_tables(size)
     own = coded(phase)
     following = {}

time: 48.5 us -> 47.3 us (0.975)
  Pallas kernels: 9.05 us -> 8.17 us
    pallas_call x2, Pallas kernels: 1.79 us -> 0.92 us  [windows(): pl.pallas_call(functools.partial(window_kernel, count, parity), out_shape...]
    ppermute x6, waiting for transfers between devices: 15.1 us -> 14.3 us  [sent_on(): return lax.ppermute(block, ('depth', 'probe'), route)]
    ppermute x2, waiting for transfers between devices: 11.1 us -> 11.8 us  [handed_down(): lax.ppermute(block, 'probe', [(i + 1, i) for i in range(parity, strips -...]
  transfers between devices with their start and end apart: 8 -> 8, of which waited for: 6 -> 6; matrix products, arithmetic and copies ran while one was open for 1% -> 0% of each run, Pallas kernels for 10% -> 9%
where the time goes in v5:
time: 47.3 us; the launch traced here: 47 us
  waiting for transfers between devices  26.1 us (55%)
  starting transfers between devices  10.6 us (22%)
  Pallas kernels  8.17 us (17%)
  other arithmetic  1.8 us (4%)
    ppermute x6, waiting for transfers between devices, sent_on(): return lax.ppermute(block, ('depth', 'probe'), route)  14.3 us
    ppermute x2, waiting for transfers between devices, handed_down(): lax.ppermute(block, 'probe', [(i + 1, i) for i in range(parity, strips -...  11.8 us
    ppermute x6, starting transfers between devices, sent_on(): return lax.ppermute(block, ('depth', 'probe'), route)  6.65 us
    pallas_call x2, Pallas kernels, last_groups(): pl.pallas_call(last_kernel, out_shape=jax.ShapeDtypeStruct((len(finished)...  5.66 us
    ppermute x2, starting transfers between devices, handed_down(): lax.ppermute(block, 'probe', [(i + 1, i) for i in range(parity, strips -...  3.92 us
    convert_element_type x1, other arithmetic, coded(): return jnp.exp2(OCTAVES * (turns - jnp.round(turns))).astype(BF16)  1.78 us
    pallas_call x3, Pallas kernels, phase_factors(): pl.pallas_call(functools.partial(factor_kernel, count, unused), out_shape...  1.56 us
  transfers between devices with their start and end apart: 8, of which 6 were waited for; matrix products, arithmetic and copies ran while one was open for 0% of the time, Pallas kernels for 9%

profile of v5, /device:TPU:23, one launch (start us, length us, event | category | flops | bytes accessed | tf_op | source)
XLA Modules:
  0.0 47.0 jit_solution(8591129707773453877)
XLA Ops:
  0.0 1.8 %fusion.2.own_ref = bf16[2,256,768]{2,1,0:T(8,128)(2,1)S(1)} fusion(f32[2,256,768]{2,1,0:T(8,128)} %param.7), kind=kLoop, calls=%fused_computation.3 | loop fusion | flops 1966080 | bytes 2359296 | tf_op jit(solution)/shard_map/convert_element_type | solution.py:83
  1.8 2.6 %collective-permute-start = (bf16[2,256,768]{2,1,0:T(8,128)(2,1)S(1)}, bf16[2,256,768]{2,1,0:T(8,128)(2,1)S(1)}, u32[]{:S(2)}, u32[]{:S(2)}) collective-permute-start(bf16[2,256,768]{2,1,0:T(8,128)(2,1)S(1)} %fusion.2.own_ref), channel_id=1, source_target_pairs={{1,0},{3,2},{5,4},{7,6},{9,8},{11,10},{13,12},{15,14},{17,16},{19,... | collective-permute-start | bytes 2359304 | tf_op jit(solution)/shard_map/ppermute | solution.py:22
  4.4 1.3 %collective-permute-start.1 = (bf16[2,256,768]{2,1,0:T(8,128)(2,1)S(1)}, bf16[2,256,768]{2,1,0:T(8,128)(2,1)S(1)}, u32[]{:S(2)}, u32[]{:S(2)}) collective-permute-start(bf16[2,256,768]{2,1,0:T(8,128)(2,1)S(1)} %fusion.2.own_ref), channel_id=1, source_target_pairs={{2,1},{4,3},{6,5},{10,9},{12,11},{14,13},{18,17},{20,19},{22,21},{... | collective-permute-start | bytes 2359304 | tf_op jit(solution)/shard_map/ppermute | solution.py:22
  5.7 0.0 copy-done.4
  5.8 0.0 copy-done.3
  5.8 0.1 copy.7
  5.9 0.4 collective-permute-done.next_ref
  6.3 0.1 broadcast_in_dim.4.starts_ref
  6.3 11.4 %collective-permute-done.1.next_ref = bf16[2,256,768]{2,1,0:T(8,128)(2,1)S(1)} collective-permute-done((bf16[2,256,768]{2,1,0:T(8,128)(2,1)S(1)}, bf16[2,256,768]{2,1,0:T(8,128)(2,1)S(1)}, u32[]{:S(2)}, u32[]{:S(2)}) %collective-permute-start.1) | collective-permute-done | bytes 786464 | tf_op jit(solution)/shard_map/ppermute | solution.py:22
  17.7 0.9 %shard_map.66 = (bf16[2,256,256]{2,1,0:T(8,128)(2,1)S(1)}, bf16[2,256,256]{2,1,0:T(8,128)(2,1)S(1)}) custom-call(f32[2,2,8,128]{3,2,1,0:T(8,128)S(1)} %broadcast_in_dim.4.starts_ref, bf16[2,256,768]{2,1,0:T(8,128)(2,1)S(1)} %fusion.2.own_ref, bf16[2,256,768]{2,1,0:T(8,128)(2,1)S(1)} %collective-permute-done.1.next_ref, bf16[16,128]{1,0:T(8,128)(2,1)S(1)} %shard_map.65.refs_0_), custom_call_target="tpu_custom_call" | custom-call | tf_op jit(solution)/shard_map/pallas_call | solution.py:159
  18.7 0.0 copy-start
  18.7 0.0 copy-start.1
  18.7 0.0 copy-start.2
  18.7 1.4 %collective-permute-start.6 = (bf16[2,256,256]{2,1,0:T(8,128)(2,1)S(1)}, bf16[2,256,256]{2,1,0:T(8,128)(2,1)S(1)}, u32[]{:S(2)}, u32[]{:S(2)}) collective-permute-start(bf16[2,256,256]{2,1,0:T(8,128)(2,1)S(1)} %get-tuple-element.17.refs_2_), channel_id=1, source_target_pairs={{1,9},{3,11},{5,13},{7,15},{9,1},{11,3},{13,5},{15,7},{17,25},{19,... | collective-permute-start | bytes 786440 | tf_op jit(solution)/shard_map/ppermute | solution.py:28
  20.1 0.7 %collective-permute-start.5 = (bf16[2,256,256]{2,1,0:T(8,128)(2,1)S(1)}, bf16[2,256,256]{2,1,0:T(8,128)(2,1)S(1)}, u32[]{:S(2)}, u32[]{:S(2)}) collective-permute-start(bf16[2,256,256]{2,1,0:T(8,128)(2,1)S(1)} %get-tuple-element.15.refs_0_), channel_id=1, source_target_pairs={{0,8},{2,10},{4,12},{6,14},{8,0},{10,2},{12,4},{14,6},{16,24},{18,... | collective-permute-start | bytes 786440 | tf_op jit(solution)/shard_map/ppermute | solution.py:28
  20.8 1.3 %collective-permute-start.3 = (bf16[2,256,256]{2,1,0:T(8,128)(2,1)S(1)}, bf16[2,256,256]{2,1,0:T(8,128)(2,1)S(1)}, u32[]{:S(2)}, u32[]{:S(2)}) collective-permute-start(bf16[2,256,256]{2,1,0:T(8,128)(2,1)S(1)} %get-tuple-element.18.refs_3_), channel_id=1, source_target_pairs={{1,9},{3,11},{5,13},{7,15},{9,1},{11,3},{13,5},{15,7},{17,25},{19,... | collective-permute-start | bytes 786440 | tf_op jit(solution)/shard_map/ppermute | solution.py:28
  22.1 0.7 %collective-permute-start.2 = (bf16[2,256,256]{2,1,0:T(8,128)(2,1)S(1)}, bf16[2,256,256]{2,1,0:T(8,128)(2,1)S(1)}, u32[]{:S(2)}, u32[]{:S(2)}) collective-permute-start(bf16[2,256,256]{2,1,0:T(8,128)(2,1)S(1)} %get-tuple-element.16.block_ref.refs_1_), channel_id=1, source_target_pairs={{0,8},{2,10},{4,12},{6,14},{8,0},{10,2},{12,4},{14,6},{16,24},{18,... | collective-permute-start | bytes 786440 | tf_op jit(solution)/shard_map/ppermute | solution.py:28
  22.8 0.8 %shard_map.67 = (f32[2,2,256,256]{3,2,1,0:T(8,128)S(1)}, f32[2,2,256,256]{3,2,1,0:T(8,128)S(1)}) custom-call(bf16[2,256,256]{2,1,0:T(8,128)(2,1)S(1)} %get-tuple-element.15.refs_0_, bf16[2,256,256]{2,1,0:T(8,128)(2,1)S(1)} %get-tuple-element.16.block_ref.refs_1_, bf16[2,256,256]{2,1,0:T(8,128)(2,1)S(1)} %get-tuple-element.17.refs_2_, ...), custom_call_target="tpu_custom_call" | custom-call | tf_op jit(solution)/shard_map/pallas_call | solution.py:231
  23.6 5.5 %collective-permute-done.6.refs_1_ = bf16[2,256,256]{2,1,0:T(8,128)(2,1)S(1)} collective-permute-done((bf16[2,256,256]{2,1,0:T(8,128)(2,1)S(1)}, bf16[2,256,256]{2,1,0:T(8,128)(2,1)S(1)}, u32[]{:S(2)}, u32[]{:S(2)}) %collective-permute-start.6) | collective-permute-done | bytes 262176 | tf_op jit(solution)/shard_map/ppermute | solution.py:28
  29.0 0.0 collective-permute-done.5.refs_0_
  29.0 0.4 shard_map.70.near_ref
  29.4 0.0 copy-done
  29.4 0.0 copy-done.1
  29.5 1.3 %collective-permute-start.7 = (bf16[2,256,256]{2,1,0:T(8,128)(2,1)S(1)}, bf16[2,256,256]{2,1,0:T(8,128)(2,1)S(1)}, u32[]{:S(2)}, u32[]{:S(2)}) collective-permute-start(bf16[2,256,256]{2,1,0:T(8,128)(2,1)S(1)} %get-tuple-element.24.second_ref), channel_id=1, source_target_pairs={{0,16},{1,17},{2,18},{3,19},{4,20},{5,21},{6,22},{7,23},{8,24},{9,... | collective-permute-start | bytes 786440 | tf_op jit(solution)/shard_map/ppermute | solution.py:28
  30.8 2.7 %collective-permute-done.3.refs_1_ = bf16[2,256,256]{2,1,0:T(8,128)(2,1)S(1)} collective-permute-done((bf16[2,256,256]{2,1,0:T(8,128)(2,1)S(1)}, bf16[2,256,256]{2,1,0:T(8,128)(2,1)S(1)}, u32[]{:S(2)}, u32[]{:S(2)}) %collective-permute-start.3) | collective-permute-done | bytes 262176 | tf_op jit(solution)/shard_map/ppermute | solution.py:28
  33.5 0.0 collective-permute-done.2.refs_0_
  33.5 0.4 shard_map.68.near_ref
  33.9 1.3 %collective-permute-start.4 = (bf16[2,256,256]{2,1,0:T(8,128)(2,1)S(1)}, bf16[2,256,256]{2,1,0:T(8,128)(2,1)S(1)}, u32[]{:S(2)}, u32[]{:S(2)}) collective-permute-start(bf16[2,256,256]{2,1,0:T(8,128)(2,1)S(1)} %get-tuple-element.21.second_ref), channel_id=1, source_target_pairs={{0,16},{1,17},{2,18},{3,19},{4,20},{5,21},{6,22},{7,23},{8,24},{9,... | collective-permute-start | bytes 786440 | tf_op jit(solution)/shard_map/ppermute | solution.py:28
  35.2 3.2 %collective-permute-done.7.far_ref = bf16[2,256,256]{2,1,0:T(8,128)(2,1)S(1)} collective-permute-done((bf16[2,256,256]{2,1,0:T(8,128)(2,1)S(1)}, bf16[2,256,256]{2,1,0:T(8,128)(2,1)S(1)}, u32[]{:S(2)}, u32[]{:S(2)}) %collective-permute-start.7) | collective-permute-done | bytes 262176 | tf_op jit(solution)/shard_map/ppermute | solution.py:28
  38.5 2.4 %shard_map.72.refs_0_ = bf16[1,2,256,256]{3,2,1,0:T(8,128)(2,1)S(1)} custom-call(bf16[2,512,256]{2,1,0:T(8,128)(2,1)S(1)} %copy-done, bf16[2,256,512]{2,1,0:T(8,128)(2,1)S(1)} %copy-done.1, f32[2,2,256,256]{3,2,1,0:T(8,128)S(1)} %get-tuple-element.22.own_ref, f32[2,2,256,256]{3,2,1,0:T(8,128)S(1)} %shard_map.70.near_ref, ...), custom_call_target="tpu_custom_call" | custom-call | tf_op jit(solution)/shard_map/pallas_call | solution.py:296
  40.9 2.9 %collective-permute-done.4.far_ref = bf16[2,256,256]{2,1,0:T(8,128)(2,1)S(1)} collective-permute-done((bf16[2,256,256]{2,1,0:T(8,128)(2,1)S(1)}, bf16[2,256,256]{2,1,0:T(8,128)(2,1)S(1)}, u32[]{:S(2)}, u32[]{:S(2)}) %collective-permute-start.4) | collective-permute-done | bytes 262176 | tf_op jit(solution)/shard_map/ppermute | solution.py:28
  43.8 3.2 %shard_map.73 = bf16[2,2,256,256]{3,2,1,0:T(8,128)(2,1)} custom-call(bf16[2,512,256]{2,1,0:T(8,128)(2,1)S(1)} %copy-done, bf16[2,256,512]{2,1,0:T(8,128)(2,1)S(1)} %copy-done.1, f32[2,2,256,256]{3,2,1,0:T(8,128)S(1)} %get-tuple-element.19.own_ref, f32[2,2,256,256]{3,2,1,0:T(8,128)S(1)} %shard_map.68.near_ref, ...), custom_call_target="tpu_custom_call" | custom-call | tf_op jit(solution)/shard_map/pallas_call | solution.py:296
  (9 shorter events, 0.1 us)
Async XLA Ops:
  0.0 5.7 %copy-start.4 = (s32[2]{0:T(128)S(1)}, s32[2]{0:T(128)}, u32[]{:S(2)}) copy-start(s32[2]{0:T(128)} %param.8) | copy-start | bytes 28
  0.0 5.8 %copy-start.3 = (s32[2]{0:T(128)S(1)}, s32[2]{0:T(128)}, u32[]{:S(2)}) copy-start(s32[2]{0:T(128)} %param.9) | copy-start | bytes 28
  1.8 4.5 %collective-permute-start = (bf16[2,256,768]{2,1,0:T(8,128)(2,1)S(1)}, bf16[2,256,768]{2,1,0:T(8,128)(2,1)S(1)}, u32[]{:S(2)}, u32[]{:S(2)}) collective-permute-start(bf16[2,256,768]{2,1,0:T(8,128)(2,1)S(1)} %fusion.2.own_ref), channel_id=1, source_target_pairs={{1,0},{3,2},{5,4},{7,6},{9,8},{11,10},{13,12},{15,14},{17,16},{19,... | collective-permute-start | bytes 2359304 | tf_op jit(solution)/shard_map/ppermute | solution.py:22
  4.4 13.3 %collective-permute-start.1 = (bf16[2,256,768]{2,1,0:T(8,128)(2,1)S(1)}, bf16[2,256,768]{2,1,0:T(8,128)(2,1)S(1)}, u32[]{:S(2)}, u32[]{:S(2)}) collective-permute-start(bf16[2,256,768]{2,1,0:T(8,128)(2,1)S(1)} %fusion.2.own_ref), channel_id=1, source_target_pairs={{2,1},{4,3},{6,5},{10,9},{12,11},{14,13},{18,17},{20,19},{22,21},{... | collective-permute-start | bytes 2359304 | tf_op jit(solution)/shard_map/ppermute | solution.py:22
  18.7 10.8 %copy-start = (bf16[2,512,256]{2,1,0:T(8,128)(2,1)S(1)}, bf16[2,512,256]{2,1,0:T(8,128)(2,1)}, u32[]{:S(2)}) copy-start(bf16[2,512,256]{2,1,0:T(8,128)(2,1)} %constant.16.clone.right_ref) | copy-start | bytes 1572868
  18.7 10.8 %copy-start.1 = (bf16[2,256,512]{2,1,0:T(8,128)(2,1)S(1)}, bf16[2,256,512]{2,1,0:T(8,128)(2,1)}, u32[]{:S(2)}) copy-start(bf16[2,256,512]{2,1,0:T(8,128)(2,1)} %constant.17.clone.left_ref) | copy-start | bytes 1572868
  18.7 10.8 %copy-start.2 = (f32[2,256,256]{2,1,0:T(8,128)S(1)}, f32[2,256,256]{2,1,0:T(8,128)}, u32[]{:S(2)}) copy-start(f32[2,256,256]{2,1,0:T(8,128)} %probe_ref.3) | copy-start | bytes 1572868
  18.7 10.3 %collective-permute-start.6 = (bf16[2,256,256]{2,1,0:T(8,128)(2,1)S(1)}, bf16[2,256,256]{2,1,0:T(8,128)(2,1)S(1)}, u32[]{:S(2)}, u32[]{:S(2)}) collective-permute-start(bf16[2,256,256]{2,1,0:T(8,128)(2,1)S(1)} %get-tuple-element.17.refs_2_), channel_id=1, source_target_pairs={{1,9},{3,11},{5,13},{7,15},{9,1},{11,3},{13,5},{15,7},{17,25},{19,... | collective-permute-start | bytes 786440 | tf_op jit(solution)/shard_map/ppermute | solution.py:28
  20.1 8.9 %collective-permute-start.5 = (bf16[2,256,256]{2,1,0:T(8,128)(2,1)S(1)}, bf16[2,256,256]{2,1,0:T(8,128)(2,1)S(1)}, u32[]{:S(2)}, u32[]{:S(2)}) collective-permute-start(bf16[2,256,256]{2,1,0:T(8,128)(2,1)S(1)} %get-tuple-element.15.refs_0_), channel_id=1, source_target_pairs={{0,8},{2,10},{4,12},{6,14},{8,0},{10,2},{12,4},{14,6},{16,24},{18,... | collective-permute-start | bytes 786440 | tf_op jit(solution)/shard_map/ppermute | solution.py:28
  20.8 12.7 %collective-permute-start.3 = (bf16[2,256,256]{2,1,0:T(8,128)(2,1)S(1)}, bf16[2,256,256]{2,1,0:T(8,128)(2,1)S(1)}, u32[]{:S(2)}, u32[]{:S(2)}) collective-permute-start(bf16[2,256,256]{2,1,0:T(8,128)(2,1)S(1)} %get-tuple-element.18.refs_3_), channel_id=1, source_target_pairs={{1,9},{3,11},{5,13},{7,15},{9,1},{11,3},{13,5},{15,7},{17,25},{19,... | collective-permute-start | bytes 786440 | tf_op jit(solution)/shard_map/ppermute | solution.py:28
  22.1 11.4 %collective-permute-start.2 = (bf16[2,256,256]{2,1,0:T(8,128)(2,1)S(1)}, bf16[2,256,256]{2,1,0:T(8,128)(2,1)S(1)}, u32[]{:S(2)}, u32[]{:S(2)}) collective-permute-start(bf16[2,256,256]{2,1,0:T(8,128)(2,1)S(1)} %get-tuple-element.16.block_ref.refs_1_), channel_id=1, source_target_pairs={{0,8},{2,10},{4,12},{6,14},{8,0},{10,2},{12,4},{14,6},{16,24},{18,... | collective-permute-start | bytes 786440 | tf_op jit(solution)/shard_map/ppermute | solution.py:28
  29.5 9.0 %collective-permute-start.7 = (bf16[2,256,256]{2,1,0:T(8,128)(2,1)S(1)}, bf16[2,256,256]{2,1,0:T(8,128)(2,1)S(1)}, u32[]{:S(2)}, u32[]{:S(2)}) collective-permute-start(bf16[2,256,256]{2,1,0:T(8,128)(2,1)S(1)} %get-tuple-element.24.second_ref), channel_id=1, source_target_pairs={{0,16},{1,17},{2,18},{3,19},{4,20},{5,21},{6,22},{7,23},{8,24},{9,... | collective-permute-start | bytes 786440 | tf_op jit(solution)/shard_map/ppermute | solution.py:28
  33.9 9.9 %collective-permute-start.4 = (bf16[2,256,256]{2,1,0:T(8,128)(2,1)S(1)}, bf16[2,256,256]{2,1,0:T(8,128)(2,1)S(1)}, u32[]{:S(2)}, u32[]{:S(2)}) collective-permute-start(bf16[2,256,256]{2,1,0:T(8,128)(2,1)S(1)} %get-tuple-element.21.second_ref), channel_id=1, source_target_pairs={{0,16},{1,17},{2,18},{3,19},{4,20},{5,21},{6,22},{7,23},{8,24},{9,... | collective-permute-start | bytes 786440 | tf_op jit(solution)/shard_map/ppermute | solution.py:28

commit v6 on v4

--- a/solution.py
+++ b/solution.py
@@ -267,9 +267,15 @@
     )(probe, *tables, own, near)
 
 
-def last_kernel(right_ref, left_ref, own_ref, near_ref, first_ref, second_ref, far_ref, *refs):
-    out_ref, state_ref = refs[-2:]
-    finished = refs[:-2]
+def last_kernel(before, right_ref, left_ref, own_ref, near_ref, first_ref, second_ref, far_ref, *refs):
+    finished = refs[:before]
+    out_ref, state_ref = refs[before : before + 2]
+    copies = []
+    if before:
+        wave_ref, done = refs[before + 2 :]
+        copies = [pltpu.make_async_copy(ref.at[0], out_ref.at[j], done.at[j]) for j, ref in enumerate(finished)]
+    for copy in copies:
+        copy.start()
     layers = own_ref.shape[0]
     group = lax.axis_index("depth")
     for part in range(2):
@@ -285,20 +291,29 @@
     def _():
         group_of(state_ref, lambda s, k: own_ref[s, k], layers, right_ref, left_ref)
 
-    out_ref[len(finished)] = state_ref[...].astype(BF16)
-    for j, ref in enumerate(finished):
-        out_ref[j] = ref[0]
+    if before:
+        wave_ref[...] = state_ref[...].astype(BF16)
+        copies.append(pltpu.make_async_copy(wave_ref, out_ref.at[before], done.at[before]))
+        copies[-1].start()
+    else:
+        out_ref[0] = state_ref[...].astype(BF16)
+    for copy in copies:
+        copy.wait()
 
 
 def last_groups(tables, own, near, waves, finished):
     shape = waves[0].shape
+    before = len(finished)
+    scratch = [pltpu.VMEM(shape, F32)]
+    if before:
+        scratch += [pltpu.VMEM(shape, BF16), pltpu.SemaphoreType.DMA((before + 1,))]
     arguments = [*tables, own, near, *waves, *finished]
     return pl.pallas_call(
-        last_kernel,
+        functools.partial(last_kernel, before),
         out_shape=jax.ShapeDtypeStruct((len(finished) + 1, *shape), BF16),
         in_specs=[VMEM] * len(arguments),
-        out_specs=VMEM,
-        scratch_shapes=[pltpu.VMEM(shape, F32)],
+        out_specs=pl.BlockSpec(memory_space=pl.ANY) if before else VMEM,
+        scratch_shapes=scratch,
         compiler_params=pltpu.CompilerParams(vmem_limit_bytes=ROOM),
     )(*arguments)
 

time: 48.5 us -> 48.4 us (level)
  no operation moved by 1% of the time
where the time goes in v6:
time: 48.4 us; the launch traced here: 48.1 us
  waiting for transfers between devices  26.3 us (54%)
  starting transfers between devices  10.6 us (22%)
  Pallas kernels  8.96 us (19%)
  other arithmetic  1.86 us (4%)
    ppermute x6, waiting for transfers between devices, sent_on(): return lax.ppermute(block, ('depth', 'probe'), route)  15.1 us
    ppermute x2, waiting for transfers between devices, handed_down(): lax.ppermute(block, 'probe', [(i + 1, i) for i in range(parity, strips -...  11.1 us
    ppermute x6, starting transfers between devices, sent_on(): return lax.ppermute(block, ('depth', 'probe'), route)  6.65 us
    pallas_call x2, Pallas kernels, last_groups(): pl.pallas_call(functools.partial(last_kernel, before), out_shape=jax.Shap...  5.57 us
    ppermute x2, starting transfers between devices, handed_down(): lax.ppermute(block, 'probe', [(i + 1, i) for i in range(parity, strips -...  3.92 us
    pallas_call x2, Pallas kernels, windows(): pl.pallas_call(functools.partial(window_kernel, count, parity), out_shape...  1.79 us
    convert_element_type x1, other arithmetic, coded(): return jnp.exp2(OCTAVES * (turns - jnp.round(turns))).astype(BF16)  1.78 us
    pallas_call x3, Pallas kernels, phase_factors(): pl.pallas_call(functools.partial(factor_kernel, count, unused), out_shape...  1.56 us
  transfers between devices with their start and end apart: 8, of which 6 were waited for; matrix products, arithmetic and copies ran while one was open for 1% of the time, Pallas kernels for 10%

profile of v6, /device:TPU:23, one launch (start us, length us, event | category | flops | bytes accessed | tf_op | source)
XLA Modules:
  0.0 48.1 jit_solution(360025152221358545)
XLA Ops:
  0.0 1.8 %fusion.2.own_ref = bf16[2,256,768]{2,1,0:T(8,128)(2,1)S(1)} fusion(f32[2,256,768]{2,1,0:T(8,128)} %param.7), kind=kLoop, calls=%fused_computation.3 | loop fusion | flops 1966080 | bytes 2359296 | tf_op jit(solution)/shard_map/convert_element_type | solution.py:83
  1.8 2.6 %collective-permute-start = (bf16[2,256,768]{2,1,0:T(8,128)(2,1)S(1)}, bf16[2,256,768]{2,1,0:T(8,128)(2,1)S(1)}, u32[]{:S(2)}, u32[]{:S(2)}) collective-permute-start(bf16[2,256,768]{2,1,0:T(8,128)(2,1)S(1)} %fusion.2.own_ref), channel_id=1, source_target_pairs={{1,0},{3,2},{5,4},{7,6},{9,8},{11,10},{13,12},{15,14},{17,16},{19,... | collective-permute-start | bytes 2359304 | tf_op jit(solution)/shard_map/ppermute | solution.py:22
  4.4 1.3 %collective-permute-start.1 = (bf16[2,256,768]{2,1,0:T(8,128)(2,1)S(1)}, bf16[2,256,768]{2,1,0:T(8,128)(2,1)S(1)}, u32[]{:S(2)}, u32[]{:S(2)}) collective-permute-start(bf16[2,256,768]{2,1,0:T(8,128)(2,1)S(1)} %fusion.2.own_ref), channel_id=1, source_target_pairs={{2,1},{4,3},{6,5},{10,9},{12,11},{14,13},{18,17},{20,19},{22,21},{... | collective-permute-start | bytes 2359304 | tf_op jit(solution)/shard_map/ppermute | solution.py:22
  5.7 0.0 copy-done.3
  5.8 0.1 copy.7
  5.8 0.0 copy-done.4
  5.8 0.1 copy.8
  5.9 0.1 pad_add_fusion.starts_ref
  6.0 0.3 collective-permute-done.next_ref
  6.3 0.6 %shard_map.64 = (bf16[2,256,256]{2,1,0:T(8,128)(2,1)S(1)}, bf16[2,256,256]{2,1,0:T(8,128)(2,1)S(1)}) custom-call(s32[2,2]{1,0:T(2,128)S(1)} %pad_add_fusion.starts_ref, bf16[2,256,768]{2,1,0:T(8,128)(2,1)S(1)} %fusion.2.own_ref, bf16[2,256,768]{2,1,0:T(8,128)(2,1)S(1)} %collective-permute-done.next_ref), custom_call_target="tpu_custom_call" | custom-call | tf_op jit(solution)/shard_map/pallas_call | solution.py:159
  6.9 10.9 %collective-permute-done.1.next_ref = bf16[2,256,768]{2,1,0:T(8,128)(2,1)S(1)} collective-permute-done((bf16[2,256,768]{2,1,0:T(8,128)(2,1)S(1)}, bf16[2,256,768]{2,1,0:T(8,128)(2,1)S(1)}, u32[]{:S(2)}, u32[]{:S(2)}) %collective-permute-start.1) | collective-permute-done | bytes 786464 | tf_op jit(solution)/shard_map/ppermute | solution.py:22
  17.7 1.2 %shard_map.66 = (bf16[2,256,256]{2,1,0:T(8,128)(2,1)S(1)}, bf16[2,256,256]{2,1,0:T(8,128)(2,1)S(1)}) custom-call(s32[2,2]{1,0:T(2,128)S(1)} %pad_add_fusion.starts_ref, bf16[2,256,768]{2,1,0:T(8,128)(2,1)S(1)} %fusion.2.own_ref, bf16[2,256,768]{2,1,0:T(8,128)(2,1)S(1)} %collective-permute-done.1.next_ref, bf16[16,128]{1,0:T(8,128)(2,1)S(1)} %shard_map.65.refs_0_), custom_call_target="tpu_custom_call" | custom-call | tf_op jit(solution)/shard_map/pallas_call | solution.py:159
  19.0 0.0 copy-start
  19.0 0.0 copy-start.1
  19.0 0.0 copy-start.2
  19.0 1.4 %collective-permute-start.6 = (bf16[2,256,256]{2,1,0:T(8,128)(2,1)S(1)}, bf16[2,256,256]{2,1,0:T(8,128)(2,1)S(1)}, u32[]{:S(2)}, u32[]{:S(2)}) collective-permute-start(bf16[2,256,256]{2,1,0:T(8,128)(2,1)S(1)} %get-tuple-element.17.refs_2_), channel_id=1, source_target_pairs={{1,9},{3,11},{5,13},{7,15},{9,1},{11,3},{13,5},{15,7},{17,25},{19,... | collective-permute-start | bytes 786440 | tf_op jit(solution)/shard_map/ppermute | solution.py:28
  20.4 0.7 %collective-permute-start.5 = (bf16[2,256,256]{2,1,0:T(8,128)(2,1)S(1)}, bf16[2,256,256]{2,1,0:T(8,128)(2,1)S(1)}, u32[]{:S(2)}, u32[]{:S(2)}) collective-permute-start(bf16[2,256,256]{2,1,0:T(8,128)(2,1)S(1)} %get-tuple-element.15.refs_0_), channel_id=1, source_target_pairs={{0,8},{2,10},{4,12},{6,14},{8,0},{10,2},{12,4},{14,6},{16,24},{18,... | collective-permute-start | bytes 786440 | tf_op jit(solution)/shard_map/ppermute | solution.py:28
  21.1 1.3 %collective-permute-start.3 = (bf16[2,256,256]{2,1,0:T(8,128)(2,1)S(1)}, bf16[2,256,256]{2,1,0:T(8,128)(2,1)S(1)}, u32[]{:S(2)}, u32[]{:S(2)}) collective-permute-start(bf16[2,256,256]{2,1,0:T(8,128)(2,1)S(1)} %get-tuple-element.18.refs_3_), channel_id=1, source_target_pairs={{1,9},{3,11},{5,13},{7,15},{9,1},{11,3},{13,5},{15,7},{17,25},{19,... | collective-permute-start | bytes 786440 | tf_op jit(solution)/shard_map/ppermute | solution.py:28
  22.4 0.7 %collective-permute-start.2 = (bf16[2,256,256]{2,1,0:T(8,128)(2,1)S(1)}, bf16[2,256,256]{2,1,0:T(8,128)(2,1)S(1)}, u32[]{:S(2)}, u32[]{:S(2)}) collective-permute-start(bf16[2,256,256]{2,1,0:T(8,128)(2,1)S(1)} %get-tuple-element.16.block_ref.refs_1_), channel_id=1, source_target_pairs={{0,8},{2,10},{4,12},{6,14},{8,0},{10,2},{12,4},{14,6},{16,24},{18,... | collective-permute-start | bytes 786440 | tf_op jit(solution)/shard_map/ppermute | solution.py:28
  23.1 0.8 %shard_map.67 = (f32[2,2,256,256]{3,2,1,0:T(8,128)S(1)}, f32[2,2,256,256]{3,2,1,0:T(8,128)S(1)}) custom-call(bf16[2,256,256]{2,1,0:T(8,128)(2,1)S(1)} %get-tuple-element.15.refs_0_, bf16[2,256,256]{2,1,0:T(8,128)(2,1)S(1)} %get-tuple-element.16.block_ref.refs_1_, bf16[2,256,256]{2,1,0:T(8,128)(2,1)S(1)} %get-tuple-element.17.refs_2_, ...), custom_call_target="tpu_custom_call" | custom-call | tf_op jit(solution)/shard_map/pallas_call | solution.py:231
  23.9 5.5 %collective-permute-done.6.refs_1_ = bf16[2,256,256]{2,1,0:T(8,128)(2,1)S(1)} collective-permute-done((bf16[2,256,256]{2,1,0:T(8,128)(2,1)S(1)}, bf16[2,256,256]{2,1,0:T(8,128)(2,1)S(1)}, u32[]{:S(2)}, u32[]{:S(2)}) %collective-permute-start.6) | collective-permute-done | bytes 262176 | tf_op jit(solution)/shard_map/ppermute | solution.py:28
  29.4 0.0 collective-permute-done.5.refs_0_
  29.4 0.4 shard_map.70.near_ref
  29.8 1.3 %collective-permute-start.7 = (bf16[2,256,256]{2,1,0:T(8,128)(2,1)S(1)}, bf16[2,256,256]{2,1,0:T(8,128)(2,1)S(1)}, u32[]{:S(2)}, u32[]{:S(2)}) collective-permute-start(bf16[2,256,256]{2,1,0:T(8,128)(2,1)S(1)} %get-tuple-element.24.second_ref), channel_id=1, source_target_pairs={{0,16},{1,17},{2,18},{3,19},{4,20},{5,21},{6,22},{7,23},{8,24},{9,... | collective-permute-start | bytes 786440 | tf_op jit(solution)/shard_map/ppermute | solution.py:28
  31.1 3.0 %collective-permute-done.3.refs_1_ = bf16[2,256,256]{2,1,0:T(8,128)(2,1)S(1)} collective-permute-done((bf16[2,256,256]{2,1,0:T(8,128)(2,1)S(1)}, bf16[2,256,256]{2,1,0:T(8,128)(2,1)S(1)}, u32[]{:S(2)}, u32[]{:S(2)}) %collective-permute-start.3) | collective-permute-done | bytes 262176 | tf_op jit(solution)/shard_map/ppermute | solution.py:28
  34.1 0.0 collective-permute-done.2.refs_0_
  34.1 0.4 shard_map.68.near_ref
  34.5 1.3 %collective-permute-start.4 = (bf16[2,256,256]{2,1,0:T(8,128)(2,1)S(1)}, bf16[2,256,256]{2,1,0:T(8,128)(2,1)S(1)}, u32[]{:S(2)}, u32[]{:S(2)}) collective-permute-start(bf16[2,256,256]{2,1,0:T(8,128)(2,1)S(1)} %get-tuple-element.21.second_ref), channel_id=1, source_target_pairs={{0,16},{1,17},{2,18},{3,19},{4,20},{5,21},{6,22},{7,23},{8,24},{9,... | collective-permute-start | bytes 786440 | tf_op jit(solution)/shard_map/ppermute | solution.py:28
  35.8 3.6 %collective-permute-done.7.far_ref = bf16[2,256,256]{2,1,0:T(8,128)(2,1)S(1)} collective-permute-done((bf16[2,256,256]{2,1,0:T(8,128)(2,1)S(1)}, bf16[2,256,256]{2,1,0:T(8,128)(2,1)S(1)}, u32[]{:S(2)}, u32[]{:S(2)}) %collective-permute-start.7) | collective-permute-done | bytes 262176 | tf_op jit(solution)/shard_map/ppermute | solution.py:28
  39.4 2.4 %shard_map.72.refs_0_ = bf16[1,2,256,256]{3,2,1,0:T(8,128)(2,1)S(1)} custom-call(bf16[2,512,256]{2,1,0:T(8,128)(2,1)S(1)} %copy-done, bf16[2,256,512]{2,1,0:T(8,128)(2,1)S(1)} %copy-done.1, f32[2,2,256,256]{3,2,1,0:T(8,128)S(1)} %get-tuple-element.22.own_ref, f32[2,2,256,256]{3,2,1,0:T(8,128)S(1)} %shard_map.70.near_ref, ...), custom_call_target="tpu_custom_call" | custom-call | tf_op jit(solution)/shard_map/pallas_call | solution.py:311
  41.8 3.1 %collective-permute-done.4.far_ref = bf16[2,256,256]{2,1,0:T(8,128)(2,1)S(1)} collective-permute-done((bf16[2,256,256]{2,1,0:T(8,128)(2,1)S(1)}, bf16[2,256,256]{2,1,0:T(8,128)(2,1)S(1)}, u32[]{:S(2)}, u32[]{:S(2)}) %collective-permute-start.4) | collective-permute-done | bytes 262176 | tf_op jit(solution)/shard_map/ppermute | solution.py:28
  44.9 3.1 %shard_map.73 = bf16[2,2,256,256]{3,2,1,0:T(8,128)(2,1)} custom-call(bf16[2,512,256]{2,1,0:T(8,128)(2,1)S(1)} %copy-done, bf16[2,256,512]{2,1,0:T(8,128)(2,1)S(1)} %copy-done.1, f32[2,2,256,256]{3,2,1,0:T(8,128)S(1)} %get-tuple-element.19.own_ref, f32[2,2,256,256]{3,2,1,0:T(8,128)S(1)} %shard_map.68.near_ref, ...), custom_call_target="tpu_custom_call" | custom-call | tf_op jit(solution)/shard_map/pallas_call | solution.py:311
  (9 shorter events, 0.1 us)
Async XLA Ops:
  0.0 5.7 %copy-start.3 = (s32[2]{0:T(128)S(1)}, s32[2]{0:T(128)}, u32[]{:S(2)}) copy-start(s32[2]{0:T(128)} %param.8) | copy-start | bytes 28
  0.0 5.8 %copy-start.4 = (s32[2]{0:T(128)S(1)}, s32[2]{0:T(128)}, u32[]{:S(2)}) copy-start(s32[2]{0:T(128)} %param.9) | copy-start | bytes 28
  1.8 4.5 %collective-permute-start = (bf16[2,256,768]{2,1,0:T(8,128)(2,1)S(1)}, bf16[2,256,768]{2,1,0:T(8,128)(2,1)S(1)}, u32[]{:S(2)}, u32[]{:S(2)}) collective-permute-start(bf16[2,256,768]{2,1,0:T(8,128)(2,1)S(1)} %fusion.2.own_ref), channel_id=1, source_target_pairs={{1,0},{3,2},{5,4},{7,6},{9,8},{11,10},{13,12},{15,14},{17,16},{19,... | collective-permute-start | bytes 2359304 | tf_op jit(solution)/shard_map/ppermute | solution.py:22
  4.4 13.3 %collective-permute-start.1 = (bf16[2,256,768]{2,1,0:T(8,128)(2,1)S(1)}, bf16[2,256,768]{2,1,0:T(8,128)(2,1)S(1)}, u32[]{:S(2)}, u32[]{:S(2)}) collective-permute-start(bf16[2,256,768]{2,1,0:T(8,128)(2,1)S(1)} %fusion.2.own_ref), channel_id=1, source_target_pairs={{2,1},{4,3},{6,5},{10,9},{12,11},{14,13},{18,17},{20,19},{22,21},{... | collective-permute-start | bytes 2359304 | tf_op jit(solution)/shard_map/ppermute | solution.py:22
  19.0 10.8 %copy-start = (bf16[2,512,256]{2,1,0:T(8,128)(2,1)S(1)}, bf16[2,512,256]{2,1,0:T(8,128)(2,1)}, u32[]{:S(2)}) copy-start(bf16[2,512,256]{2,1,0:T(8,128)(2,1)} %constant.16.clone.right_ref) | copy-start | bytes 1572868
  19.0 10.8 %copy-start.1 = (bf16[2,256,512]{2,1,0:T(8,128)(2,1)S(1)}, bf16[2,256,512]{2,1,0:T(8,128)(2,1)}, u32[]{:S(2)}) copy-start(bf16[2,256,512]{2,1,0:T(8,128)(2,1)} %constant.17.clone.left_ref) | copy-start | bytes 1572868
  19.0 10.8 %copy-start.2 = (f32[2,256,256]{2,1,0:T(8,128)S(1)}, f32[2,256,256]{2,1,0:T(8,128)}, u32[]{:S(2)}) copy-start(f32[2,256,256]{2,1,0:T(8,128)} %probe_ref.3) | copy-start | bytes 1572868
  19.0 10.3 %collective-permute-start.6 = (bf16[2,256,256]{2,1,0:T(8,128)(2,1)S(1)}, bf16[2,256,256]{2,1,0:T(8,128)(2,1)S(1)}, u32[]{:S(2)}, u32[]{:S(2)}) collective-permute-start(bf16[2,256,256]{2,1,0:T(8,128)(2,1)S(1)} %get-tuple-element.17.refs_2_), channel_id=1, source_target_pairs={{1,9},{3,11},{5,13},{7,15},{9,1},{11,3},{13,5},{15,7},{17,25},{19,... | collective-permute-start | bytes 786440 | tf_op jit(solution)/shard_map/ppermute | solution.py:28
  20.4 8.9 %collective-permute-start.5 = (bf16[2,256,256]{2,1,0:T(8,128)(2,1)S(1)}, bf16[2,256,256]{2,1,0:T(8,128)(2,1)S(1)}, u32[]{:S(2)}, u32[]{:S(2)}) collective-permute-start(bf16[2,256,256]{2,1,0:T(8,128)(2,1)S(1)} %get-tuple-element.15.refs_0_), channel_id=1, source_target_pairs={{0,8},{2,10},{4,12},{6,14},{8,0},{10,2},{12,4},{14,6},{16,24},{18,... | collective-permute-start | bytes 786440 | tf_op jit(solution)/shard_map/ppermute | solution.py:28
  21.1 13.0 %collective-permute-start.3 = (bf16[2,256,256]{2,1,0:T(8,128)(2,1)S(1)}, bf16[2,256,256]{2,1,0:T(8,128)(2,1)S(1)}, u32[]{:S(2)}, u32[]{:S(2)}) collective-permute-start(bf16[2,256,256]{2,1,0:T(8,128)(2,1)S(1)} %get-tuple-element.18.refs_3_), channel_id=1, source_target_pairs={{1,9},{3,11},{5,13},{7,15},{9,1},{11,3},{13,5},{15,7},{17,25},{19,... | collective-permute-start | bytes 786440 | tf_op jit(solution)/shard_map/ppermute | solution.py:28
  22.4 11.7 %collective-permute-start.2 = (bf16[2,256,256]{2,1,0:T(8,128)(2,1)S(1)}, bf16[2,256,256]{2,1,0:T(8,128)(2,1)S(1)}, u32[]{:S(2)}, u32[]{:S(2)}) collective-permute-start(bf16[2,256,256]{2,1,0:T(8,128)(2,1)S(1)} %get-tuple-element.16.block_ref.refs_1_), channel_id=1, source_target_pairs={{0,8},{2,10},{4,12},{6,14},{8,0},{10,2},{12,4},{14,6},{16,24},{18,... | collective-permute-start | bytes 786440 | tf_op jit(solution)/shard_map/ppermute | solution.py:28
  29.8 9.6 %collective-permute-start.7 = (bf16[2,256,256]{2,1,0:T(8,128)(2,1)S(1)}, bf16[2,256,256]{2,1,0:T(8,128)(2,1)S(1)}, u32[]{:S(2)}, u32[]{:S(2)}) collective-permute-start(bf16[2,256,256]{2,1,0:T(8,128)(2,1)S(1)} %get-tuple-element.24.second_ref), channel_id=1, source_target_pairs={{0,16},{1,17},{2,18},{3,19},{4,20},{5,21},{6,22},{7,23},{8,24},{9,... | collective-permute-start | bytes 786440 | tf_op jit(solution)/shard_map/ppermute | solution.py:28
  34.5 10.4 %collective-permute-start.4 = (bf16[2,256,256]{2,1,0:T(8,128)(2,1)S(1)}, bf16[2,256,256]{2,1,0:T(8,128)(2,1)S(1)}, u32[]{:S(2)}, u32[]{:S(2)}) collective-permute-start(bf16[2,256,256]{2,1,0:T(8,128)(2,1)S(1)} %get-tuple-element.21.second_ref), channel_id=1, source_target_pairs={{0,16},{1,17},{2,18},{3,19},{4,20},{5,21},{6,22},{7,23},{8,24},{9,... | collective-permute-start | bytes 786440 | tf_op jit(solution)/shard_map/ppermute | solution.py:28

commit v7 on v6

--- a/solution.py
+++ b/solution.py
@@ -136,8 +136,8 @@
         edge = (place == lax.axis_size("probe") - 1).astype(F32)
         line = lax.broadcasted_iota(jnp.int32, (strip, span), 0)
         for j, out in enumerate(outs):
-            r = starts_ref[j, 0]
-            c = starts_ref[j, 1]
+            r = jnp.max(starts_ref[j, 0]).astype(jnp.int32)
+            c = jnp.max(starts_ref[j, 1]).astype(jnp.int32)
             base = jnp.minimum(c // 128, (width - span) // 128)
             shift = c - base * 128
             lanes = pl.ds(pl.multiple_of(base * 128, 128), span)
@@ -159,7 +159,7 @@
     return pl.pallas_call(
         functools.partial(window_kernel, count, parity),
         out_shape=[jax.ShapeDtypeStruct((layers, size, size), BF16)] * count,
-        in_specs=[SMEM] + [VMEM] * (2 + len(after)),
+        in_specs=[VMEM] * (3 + len(after)),
         out_specs=[VMEM] * count,
         scratch_shapes=[pltpu.VMEM((size // 128, 2 * strip, 128), F32)],
         compiler_params=pltpu.CompilerParams(vmem_limit_bytes=ROOM),
@@ -348,6 +348,7 @@
     count = row_offsets.shape[0]
     groups = lax.axis_size("depth")
     starts = jnp.stack([row_offsets - lax.axis_index("probe") * strip, col_offsets], axis=1)
+    starts = jnp.broadcast_to(starts.astype(F32)[:, :, None, None], (count, 2, 8, 128))
     tables = operator_tables(size)
     own = coded(phase)
     following = {}

time: 48.4 us -> 47.2 us (0.975)
  Pallas kernels: 8.96 us -> 8.08 us
    pallas_call x2, Pallas kernels: 1.79 us -> 0.92 us  [windows(): pl.pallas_call(functools.partial(window_kernel, count, parity), out_shape...]
    ppermute x6, waiting for transfers between devices: 15.1 us -> 14.3 us  [sent_on(): return lax.ppermute(block, ('depth', 'probe'), route)]
    ppermute x2, waiting for transfers between devices: 11.1 us -> 11.8 us  [handed_down(): lax.ppermute(block, 'probe', [(i + 1, i) for i in range(parity, strips -...]
  transfers between devices with their start and end apart: 8 -> 8, of which waited for: 6 -> 6; matrix products, arithmetic and copies ran while one was open for 1% -> 0% of each run, Pallas kernels for 10% -> 9%
where the time goes in v7:
time: 47.2 us; the launch traced here: 46.9 us
  waiting for transfers between devices  26.1 us (55%)
  starting transfers between devices  10.6 us (22%)
  Pallas kernels  8.08 us (17%)
  other arithmetic  1.8 us (4%)
    ppermute x6, waiting for transfers between devices, sent_on(): return lax.ppermute(block, ('depth', 'probe'), route)  14.3 us
    ppermute x2, waiting for transfers between devices, handed_down(): lax.ppermute(block, 'probe', [(i + 1, i) for i in range(parity, strips -...  11.8 us
    ppermute x6, starting transfers between devices, sent_on(): return lax.ppermute(block, ('depth', 'probe'), route)  6.65 us
    pallas_call x2, Pallas kernels, last_groups(): pl.pallas_call(functools.partial(last_kernel, before), out_shape=jax.Shap...  5.57 us
    ppermute x2, starting transfers between devices, handed_down(): lax.ppermute(block, 'probe', [(i + 1, i) for i in range(parity, strips -...  3.92 us
    convert_element_type x1, other arithmetic, coded(): return jnp.exp2(OCTAVES * (turns - jnp.round(turns))).astype(BF16)  1.78 us
    pallas_call x3, Pallas kernels, phase_factors(): pl.pallas_call(functools.partial(factor_kernel, count, unused), out_shape...  1.56 us
  transfers between devices with their start and end apart: 8, of which 6 were waited for; matrix products, arithmetic and copies ran while one was open for 0% of the time, Pallas kernels for 9%

profile of v7, /device:TPU:23, one launch (start us, length us, event | category | flops | bytes accessed | tf_op | source)
XLA Modules:
  0.0 46.9 jit_solution(2934977451636151383)
XLA Ops:
  0.0 1.8 %fusion.2.own_ref = bf16[2,256,768]{2,1,0:T(8,128)(2,1)S(1)} fusion(f32[2,256,768]{2,1,0:T(8,128)} %param.7), kind=kLoop, calls=%fused_computation.3 | loop fusion | flops 1966080 | bytes 2359296 | tf_op jit(solution)/shard_map/convert_element_type | solution.py:83
  1.8 2.6 %collective-permute-start = (bf16[2,256,768]{2,1,0:T(8,128)(2,1)S(1)}, bf16[2,256,768]{2,1,0:T(8,128)(2,1)S(1)}, u32[]{:S(2)}, u32[]{:S(2)}) collective-permute-start(bf16[2,256,768]{2,1,0:T(8,128)(2,1)S(1)} %fusion.2.own_ref), channel_id=1, source_target_pairs={{1,0},{3,2},{5,4},{7,6},{9,8},{11,10},{13,12},{15,14},{17,16},{19,... | collective-permute-start | bytes 2359304 | tf_op jit(solution)/shard_map/ppermute | solution.py:22
  4.4 1.3 %collective-permute-start.1 = (bf16[2,256,768]{2,1,0:T(8,128)(2,1)S(1)}, bf16[2,256,768]{2,1,0:T(8,128)(2,1)S(1)}, u32[]{:S(2)}, u32[]{:S(2)}) collective-permute-start(bf16[2,256,768]{2,1,0:T(8,128)(2,1)S(1)} %fusion.2.own_ref), channel_id=1, source_target_pairs={{2,1},{4,3},{6,5},{10,9},{12,11},{14,13},{18,17},{20,19},{22,21},{... | collective-permute-start | bytes 2359304 | tf_op jit(solution)/shard_map/ppermute | solution.py:22
  5.7 0.0 copy-done.4
  5.8 0.0 copy-done.3
  5.8 0.1 copy.7
  5.9 0.4 collective-permute-done.next_ref
  6.3 0.1 broadcast_in_dim.4.starts_ref
  6.3 11.4 %collective-permute-done.1.next_ref = bf16[2,256,768]{2,1,0:T(8,128)(2,1)S(1)} collective-permute-done((bf16[2,256,768]{2,1,0:T(8,128)(2,1)S(1)}, bf16[2,256,768]{2,1,0:T(8,128)(2,1)S(1)}, u32[]{:S(2)}, u32[]{:S(2)}) %collective-permute-start.1) | collective-permute-done | bytes 786464 | tf_op jit(solution)/shard_map/ppermute | solution.py:22
  17.7 0.9 %shard_map.66 = (bf16[2,256,256]{2,1,0:T(8,128)(2,1)S(1)}, bf16[2,256,256]{2,1,0:T(8,128)(2,1)S(1)}) custom-call(f32[2,2,8,128]{3,2,1,0:T(8,128)S(1)} %broadcast_in_dim.4.starts_ref, bf16[2,256,768]{2,1,0:T(8,128)(2,1)S(1)} %fusion.2.own_ref, bf16[2,256,768]{2,1,0:T(8,128)(2,1)S(1)} %collective-permute-done.1.next_ref, bf16[16,128]{1,0:T(8,128)(2,1)S(1)} %shard_map.65.refs_0_), custom_call_target="tpu_custom_call" | custom-call | tf_op jit(solution)/shard_map/pallas_call | solution.py:159
  18.7 0.0 copy-start
  18.7 0.0 copy-start.1
  18.7 0.0 copy-start.2
  18.7 1.4 %collective-permute-start.6 = (bf16[2,256,256]{2,1,0:T(8,128)(2,1)S(1)}, bf16[2,256,256]{2,1,0:T(8,128)(2,1)S(1)}, u32[]{:S(2)}, u32[]{:S(2)}) collective-permute-start(bf16[2,256,256]{2,1,0:T(8,128)(2,1)S(1)} %get-tuple-element.17.refs_2_), channel_id=1, source_target_pairs={{1,9},{3,11},{5,13},{7,15},{9,1},{11,3},{13,5},{15,7},{17,25},{19,... | collective-permute-start | bytes 786440 | tf_op jit(solution)/shard_map/ppermute | solution.py:28
  20.1 0.7 %collective-permute-start.5 = (bf16[2,256,256]{2,1,0:T(8,128)(2,1)S(1)}, bf16[2,256,256]{2,1,0:T(8,128)(2,1)S(1)}, u32[]{:S(2)}, u32[]{:S(2)}) collective-permute-start(bf16[2,256,256]{2,1,0:T(8,128)(2,1)S(1)} %get-tuple-element.15.refs_0_), channel_id=1, source_target_pairs={{0,8},{2,10},{4,12},{6,14},{8,0},{10,2},{12,4},{14,6},{16,24},{18,... | collective-permute-start | bytes 786440 | tf_op jit(solution)/shard_map/ppermute | solution.py:28
  20.8 1.3 %collective-permute-start.3 = (bf16[2,256,256]{2,1,0:T(8,128)(2,1)S(1)}, bf16[2,256,256]{2,1,0:T(8,128)(2,1)S(1)}, u32[]{:S(2)}, u32[]{:S(2)}) collective-permute-start(bf16[2,256,256]{2,1,0:T(8,128)(2,1)S(1)} %get-tuple-element.18.refs_3_), channel_id=1, source_target_pairs={{1,9},{3,11},{5,13},{7,15},{9,1},{11,3},{13,5},{15,7},{17,25},{19,... | collective-permute-start | bytes 786440 | tf_op jit(solution)/shard_map/ppermute | solution.py:28
  22.1 0.7 %collective-permute-start.2 = (bf16[2,256,256]{2,1,0:T(8,128)(2,1)S(1)}, bf16[2,256,256]{2,1,0:T(8,128)(2,1)S(1)}, u32[]{:S(2)}, u32[]{:S(2)}) collective-permute-start(bf16[2,256,256]{2,1,0:T(8,128)(2,1)S(1)} %get-tuple-element.16.block_ref.refs_1_), channel_id=1, source_target_pairs={{0,8},{2,10},{4,12},{6,14},{8,0},{10,2},{12,4},{14,6},{16,24},{18,... | collective-permute-start | bytes 786440 | tf_op jit(solution)/shard_map/ppermute | solution.py:28
  22.8 0.8 %shard_map.67 = (f32[2,2,256,256]{3,2,1,0:T(8,128)S(1)}, f32[2,2,256,256]{3,2,1,0:T(8,128)S(1)}) custom-call(bf16[2,256,256]{2,1,0:T(8,128)(2,1)S(1)} %get-tuple-element.15.refs_0_, bf16[2,256,256]{2,1,0:T(8,128)(2,1)S(1)} %get-tuple-element.16.block_ref.refs_1_, bf16[2,256,256]{2,1,0:T(8,128)(2,1)S(1)} %get-tuple-element.17.refs_2_, ...), custom_call_target="tpu_custom_call" | custom-call | tf_op jit(solution)/shard_map/pallas_call | solution.py:231
  23.6 5.5 %collective-permute-done.6.refs_1_ = bf16[2,256,256]{2,1,0:T(8,128)(2,1)S(1)} collective-permute-done((bf16[2,256,256]{2,1,0:T(8,128)(2,1)S(1)}, bf16[2,256,256]{2,1,0:T(8,128)(2,1)S(1)}, u32[]{:S(2)}, u32[]{:S(2)}) %collective-permute-start.6) | collective-permute-done | bytes 262176 | tf_op jit(solution)/shard_map/ppermute | solution.py:28
  29.0 0.0 collective-permute-done.5.refs_0_
  29.0 0.4 shard_map.70.near_ref
  29.4 0.0 copy-done
  29.4 0.0 copy-done.1
  29.5 1.3 %collective-permute-start.7 = (bf16[2,256,256]{2,1,0:T(8,128)(2,1)S(1)}, bf16[2,256,256]{2,1,0:T(8,128)(2,1)S(1)}, u32[]{:S(2)}, u32[]{:S(2)}) collective-permute-start(bf16[2,256,256]{2,1,0:T(8,128)(2,1)S(1)} %get-tuple-element.24.second_ref), channel_id=1, source_target_pairs={{0,16},{1,17},{2,18},{3,19},{4,20},{5,21},{6,22},{7,23},{8,24},{9,... | collective-permute-start | bytes 786440 | tf_op jit(solution)/shard_map/ppermute | solution.py:28
  30.8 2.7 %collective-permute-done.3.refs_1_ = bf16[2,256,256]{2,1,0:T(8,128)(2,1)S(1)} collective-permute-done((bf16[2,256,256]{2,1,0:T(8,128)(2,1)S(1)}, bf16[2,256,256]{2,1,0:T(8,128)(2,1)S(1)}, u32[]{:S(2)}, u32[]{:S(2)}) %collective-permute-start.3) | collective-permute-done | bytes 262176 | tf_op jit(solution)/shard_map/ppermute | solution.py:28
  33.5 0.0 collective-permute-done.2.refs_0_
  33.5 0.4 shard_map.68.near_ref
  33.9 1.3 %collective-permute-start.4 = (bf16[2,256,256]{2,1,0:T(8,128)(2,1)S(1)}, bf16[2,256,256]{2,1,0:T(8,128)(2,1)S(1)}, u32[]{:S(2)}, u32[]{:S(2)}) collective-permute-start(bf16[2,256,256]{2,1,0:T(8,128)(2,1)S(1)} %get-tuple-element.21.second_ref), channel_id=1, source_target_pairs={{0,16},{1,17},{2,18},{3,19},{4,20},{5,21},{6,22},{7,23},{8,24},{9,... | collective-permute-start | bytes 786440 | tf_op jit(solution)/shard_map/ppermute | solution.py:28
  35.2 3.2 %collective-permute-done.7.far_ref = bf16[2,256,256]{2,1,0:T(8,128)(2,1)S(1)} collective-permute-done((bf16[2,256,256]{2,1,0:T(8,128)(2,1)S(1)}, bf16[2,256,256]{2,1,0:T(8,128)(2,1)S(1)}, u32[]{:S(2)}, u32[]{:S(2)}) %collective-permute-start.7) | collective-permute-done | bytes 262176 | tf_op jit(solution)/shard_map/ppermute | solution.py:28
  38.5 2.4 %shard_map.72.refs_0_ = bf16[1,2,256,256]{3,2,1,0:T(8,128)(2,1)S(1)} custom-call(bf16[2,512,256]{2,1,0:T(8,128)(2,1)S(1)} %copy-done, bf16[2,256,512]{2,1,0:T(8,128)(2,1)S(1)} %copy-done.1, f32[2,2,256,256]{3,2,1,0:T(8,128)S(1)} %get-tuple-element.22.own_ref, f32[2,2,256,256]{3,2,1,0:T(8,128)S(1)} %shard_map.70.near_ref, ...), custom_call_target="tpu_custom_call" | custom-call | tf_op jit(solution)/shard_map/pallas_call | solution.py:311
  40.9 2.9 %collective-permute-done.4.far_ref = bf16[2,256,256]{2,1,0:T(8,128)(2,1)S(1)} collective-permute-done((bf16[2,256,256]{2,1,0:T(8,128)(2,1)S(1)}, bf16[2,256,256]{2,1,0:T(8,128)(2,1)S(1)}, u32[]{:S(2)}, u32[]{:S(2)}) %collective-permute-start.4) | collective-permute-done | bytes 262176 | tf_op jit(solution)/shard_map/ppermute | solution.py:28
  43.8 3.1 %shard_map.73 = bf16[2,2,256,256]{3,2,1,0:T(8,128)(2,1)} custom-call(bf16[2,512,256]{2,1,0:T(8,128)(2,1)S(1)} %copy-done, bf16[2,256,512]{2,1,0:T(8,128)(2,1)S(1)} %copy-done.1, f32[2,2,256,256]{3,2,1,0:T(8,128)S(1)} %get-tuple-element.19.own_ref, f32[2,2,256,256]{3,2,1,0:T(8,128)S(1)} %shard_map.68.near_ref, ...), custom_call_target="tpu_custom_call" | custom-call | tf_op jit(solution)/shard_map/pallas_call | solution.py:311
  (9 shorter events, 0.1 us)
Async XLA Ops:
  0.0 5.7 %copy-start.4 = (s32[2]{0:T(128)S(1)}, s32[2]{0:T(128)}, u32[]{:S(2)}) copy-start(s32[2]{0:T(128)} %param.8) | copy-start | bytes 28
  0.0 5.8 %copy-start.3 = (s32[2]{0:T(128)S(1)}, s32[2]{0:T(128)}, u32[]{:S(2)}) copy-start(s32[2]{0:T(128)} %param.9) | copy-start | bytes 28
  1.8 4.5 %collective-permute-start = (bf16[2,256,768]{2,1,0:T(8,128)(2,1)S(1)}, bf16[2,256,768]{2,1,0:T(8,128)(2,1)S(1)}, u32[]{:S(2)}, u32[]{:S(2)}) collective-permute-start(bf16[2,256,768]{2,1,0:T(8,128)(2,1)S(1)} %fusion.2.own_ref), channel_id=1, source_target_pairs={{1,0},{3,2},{5,4},{7,6},{9,8},{11,10},{13,12},{15,14},{17,16},{19,... | collective-permute-start | bytes 2359304 | tf_op jit(solution)/shard_map/ppermute | solution.py:22
  4.4 13.3 %collective-permute-start.1 = (bf16[2,256,768]{2,1,0:T(8,128)(2,1)S(1)}, bf16[2,256,768]{2,1,0:T(8,128)(2,1)S(1)}, u32[]{:S(2)}, u32[]{:S(2)}) collective-permute-start(bf16[2,256,768]{2,1,0:T(8,128)(2,1)S(1)} %fusion.2.own_ref), channel_id=1, source_target_pairs={{2,1},{4,3},{6,5},{10,9},{12,11},{14,13},{18,17},{20,19},{22,21},{... | collective-permute-start | bytes 2359304 | tf_op jit(solution)/shard_map/ppermute | solution.py:22
  18.7 10.8 %copy-start = (bf16[2,512,256]{2,1,0:T(8,128)(2,1)S(1)}, bf16[2,512,256]{2,1,0:T(8,128)(2,1)}, u32[]{:S(2)}) copy-start(bf16[2,512,256]{2,1,0:T(8,128)(2,1)} %constant.16.clone.right_ref) | copy-start | bytes 1572868
  18.7 10.8 %copy-start.1 = (bf16[2,256,512]{2,1,0:T(8,128)(2,1)S(1)}, bf16[2,256,512]{2,1,0:T(8,128)(2,1)}, u32[]{:S(2)}) copy-start(bf16[2,256,512]{2,1,0:T(8,128)(2,1)} %constant.17.clone.left_ref) | copy-start | bytes 1572868
  18.7 10.8 %copy-start.2 = (f32[2,256,256]{2,1,0:T(8,128)S(1)}, f32[2,256,256]{2,1,0:T(8,128)}, u32[]{:S(2)}) copy-start(f32[2,256,256]{2,1,0:T(8,128)} %probe_ref.3) | copy-start | bytes 1572868
  18.7 10.3 %collective-permute-start.6 = (bf16[2,256,256]{2,1,0:T(8,128)(2,1)S(1)}, bf16[2,256,256]{2,1,0:T(8,128)(2,1)S(1)}, u32[]{:S(2)}, u32[]{:S(2)}) collective-permute-start(bf16[2,256,256]{2,1,0:T(8,128)(2,1)S(1)} %get-tuple-element.17.refs_2_), channel_id=1, source_target_pairs={{1,9},{3,11},{5,13},{7,15},{9,1},{11,3},{13,5},{15,7},{17,25},{19,... | collective-permute-start | bytes 786440 | tf_op jit(solution)/shard_map/ppermute | solution.py:28
  20.1 8.9 %collective-permute-start.5 = (bf16[2,256,256]{2,1,0:T(8,128)(2,1)S(1)}, bf16[2,256,256]{2,1,0:T(8,128)(2,1)S(1)}, u32[]{:S(2)}, u32[]{:S(2)}) collective-permute-start(bf16[2,256,256]{2,1,0:T(8,128)(2,1)S(1)} %get-tuple-element.15.refs_0_), channel_id=1, source_target_pairs={{0,8},{2,10},{4,12},{6,14},{8,0},{10,2},{12,4},{14,6},{16,24},{18,... | collective-permute-start | bytes 786440 | tf_op jit(solution)/shard_map/ppermute | solution.py:28
  20.8 12.7 %collective-permute-start.3 = (bf16[2,256,256]{2,1,0:T(8,128)(2,1)S(1)}, bf16[2,256,256]{2,1,0:T(8,128)(2,1)S(1)}, u32[]{:S(2)}, u32[]{:S(2)}) collective-permute-start(bf16[2,256,256]{2,1,0:T(8,128)(2,1)S(1)} %get-tuple-element.18.refs_3_), channel_id=1, source_target_pairs={{1,9},{3,11},{5,13},{7,15},{9,1},{11,3},{13,5},{15,7},{17,25},{19,... | collective-permute-start | bytes 786440 | tf_op jit(solution)/shard_map/ppermute | solution.py:28
  22.1 11.4 %collective-permute-start.2 = (bf16[2,256,256]{2,1,0:T(8,128)(2,1)S(1)}, bf16[2,256,256]{2,1,0:T(8,128)(2,1)S(1)}, u32[]{:S(2)}, u32[]{:S(2)}) collective-permute-start(bf16[2,256,256]{2,1,0:T(8,128)(2,1)S(1)} %get-tuple-element.16.block_ref.refs_1_), channel_id=1, source_target_pairs={{0,8},{2,10},{4,12},{6,14},{8,0},{10,2},{12,4},{14,6},{16,24},{18,... | collective-permute-start | bytes 786440 | tf_op jit(solution)/shard_map/ppermute | solution.py:28
  29.5 9.0 %collective-permute-start.7 = (bf16[2,256,256]{2,1,0:T(8,128)(2,1)S(1)}, bf16[2,256,256]{2,1,0:T(8,128)(2,1)S(1)}, u32[]{:S(2)}, u32[]{:S(2)}) collective-permute-start(bf16[2,256,256]{2,1,0:T(8,128)(2,1)S(1)} %get-tuple-element.24.second_ref), channel_id=1, source_target_pairs={{0,16},{1,17},{2,18},{3,19},{4,20},{5,21},{6,22},{7,23},{8,24},{9,... | collective-permute-start | bytes 786440 | tf_op jit(solution)/shard_map/ppermute | solution.py:28
  33.9 9.9 %collective-permute-start.4 = (bf16[2,256,256]{2,1,0:T(8,128)(2,1)S(1)}, bf16[2,256,256]{2,1,0:T(8,128)(2,1)S(1)}, u32[]{:S(2)}, u32[]{:S(2)}) collective-permute-start(bf16[2,256,256]{2,1,0:T(8,128)(2,1)S(1)} %get-tuple-element.21.second_ref), channel_id=1, source_target_pairs={{0,16},{1,17},{2,18},{3,19},{4,20},{5,21},{6,22},{7,23},{8,24},{9,... | collective-permute-start | bytes 786440 | tf_op jit(solution)/shard_map/ppermute | solution.py:28
